TPU v7x, 32 devices: a whole 2x2x4 slice. The times are simulated.
32 devices in a mesh: ctx: 8 (over z, x), head: 4 (over y, core).
Axes of the slice: x: 2, y: 2, z: 4, core: 2. Of those that a mesh axis runs over, the one named last changes fastest.
Arguments:
- video_rows: bfloat16 [4096, 5120], P('ctx'), may hold values from -6 to 6
- w_query: bfloat16 [5120, 5120], P('ctx', 'head'), may hold values from -0.078125 to 0.078125
- w_output: bfloat16 [5120, 5120], P('ctx', 'head'), may hold values from -0.078125 to 0.078125
- audio_tokens: bfloat16 [2, 32, 768], P(None, 'ctx'), may hold values from -544 to 544
- w_key: bfloat16 [768, 5120], P(None, 'head'), may hold values from -0.21875 to 0.21875
- w_value: bfloat16 [768, 5120], P(None, 'head'), may hold values from -0.21875 to 0.21875
- row_lists: int32 [2, 4096], P(None, 'ctx'), may hold values from 0 to 511, as said below
- row_counts: int32 [2, 8], P(None, 'ctx'), may hold values from 0 to 512, as said below
Outputs:
- layer_out: bfloat16 [4096, 5120], P('ctx', 'head')
Inputs may be any that keep to these rules, and one draw needn't show every extreme that they name: `row_lists`: the first row_counts[s, c] entries of speaker s's block on shard c are distinct, live entries of the two speakers on one shard are distinct rows, and the other entries are arbitrary row numbers of the shard. `row_counts`: on each shard the two counts add up to at most 512.
All inputs are finite; a program needn't handle non-finite values.
Results may differ from a plain program's by a relative error of at most 0.0045.
The roundings to bfloat16 on the way count: a program that leaves them out, or rounds other values in their place, can miss the bound.
Values may be sent and summed in bfloat16 or wider, within the bound.
No kernel may reach another device: no remote copies, remote signals or barrier semaphores. Data moves between devices by JAX's collectives and lax.ppermute only.
A program may use at most 128 MiB of HBM per device.

v0:
```python
import jax
import jax.numpy as jnp
from jax import lax
from jax.sharding import PartitionSpec as P

HD = 128
SPK = 2


def add_rows(left_rows, shard_piece):
    return jnp.dot(left_rows, shard_piece, preferred_element_type=jnp.float32)


def shards(video_rows, w_query, w_output, audio_tokens, w_key, w_value, row_lists, row_counts):
    rows_dev = video_rows.shape[0]
    columns = w_query.shape[1]
    heads_dev = columns // HD
    queries = add_rows(video_rows, lax.all_gather(w_query, "ctx", axis=0, tiled=True)).astype(
        jnp.bfloat16
    )
    whole_audio = lax.all_gather(audio_tokens, "ctx", axis=1, tiled=True)
    key_rows = jnp.einsum(
        "sta,ad->std", whole_audio, w_key, preferred_element_type=jnp.float32
    ).astype(jnp.bfloat16)
    value_rows = jnp.einsum(
        "sta,ad->std", whole_audio, w_value, preferred_element_type=jnp.float32
    ).astype(jnp.bfloat16)
    audio_length = key_rows.shape[1]
    position = jnp.arange(rows_dev, dtype=jnp.int32)
    score_scale = 1.0 / HD**0.5
    summed = jnp.zeros((rows_dev, columns), jnp.float32)
    for speaker in range(SPK):
        target = row_lists[speaker]
        row_live = position < row_counts[speaker, 0]
        picked = queries[target].reshape(rows_dev, heads_dev, HD)
        key_block = key_rows[speaker].reshape(audio_length, heads_dev, HD)
        value_block = value_rows[speaker].reshape(audio_length, heads_dev, HD)
        scores = (
            jnp.einsum("rhd,khd->hrk", picked, key_block, preferred_element_type=jnp.float32)
            * score_scale
        )
        scores = scores - jnp.max(scores, axis=-1, keepdims=True)
        weights = jnp.exp(scores)
        weights = (weights / jnp.sum(weights, axis=-1, keepdims=True)).astype(jnp.bfloat16)
        blended = jnp.einsum(
            "hrk,khd->rhd", weights, value_block, preferred_element_type=jnp.float32
        ).astype(jnp.bfloat16)
        blended = blended.reshape(rows_dev, columns).astype(jnp.float32)
        blended = jnp.where(row_live[:, None], blended, jnp.zeros_like(blended))
        summed = summed.at[target].add(blended)
    attended = summed.astype(jnp.bfloat16)
    all_heads = lax.all_gather(attended, "head", axis=1, tiled=True)
    result = add_rows(all_heads, lax.all_gather(w_output, "ctx", axis=0, tiled=True))
    return result.astype(jnp.bfloat16)


def solution(mesh):
    in_specs = (
        P("ctx", None),
        P("ctx", "head"),
        P("ctx", "head"),
        P(None, "ctx", None),
        P(None, "head"),
        P(None, "head"),
        P(None, "ctx"),
        P(None, "ctx"),
    )
    out_specs = P("ctx", "head")
    return jax.shard_map(shards, mesh=mesh, in_specs=in_specs, out_specs=out_specs, check_vma=False)
```

profile of v0, /device:TPU:0, one launch (start us, length us, event | category | flops | bytes accessed | tf_op | source)
XLA Modules:
  0.0 439.1 jit_solution(14626335249302658859)
XLA Ops:
  6.5 0.7 all-gather.4.cloned.1.call-update
  7.3 0.7 all-gather.8.cloned.1.call-update
  8.1 32.9 %all_gather.12 = bf16[2,32,768]{2,0,1:T(2,128)(2,1)S(1)} all-gather(bf16[2,4,768]{2,0,1:T(2,128)(2,1)S(1)} %copy.25), channel_id=1, replica_groups=mesh['ctx'=8,'head'=4] {'ctx'}, dimensions={1}, use_global_device_ids=true | all-gather | bytes 110592 | tf_op jit(solution)/shard_map/all_gather | solution.py:21
  41.0 0.5 convolution_convert_fusion.2
  41.5 0.1 reshape_squeeze.13
  41.6 2.0 convolution_convert_fusion.3
  43.6 0.1 reshape_squeeze.12
  43.7 0.1 reshape_squeeze.15
  43.8 0.1 reshape_squeeze.14
  43.8 0.6 fusion.29
  44.4 0.7 iota_compare_fusion.1
  45.1 0.7 iota_compare_fusion
  45.8 149.7 %all-gather.4.cloned.1.call-done = bf16[5120,1280]{1,0:T(8,128)(2,1)} async-done(((bf16[640,1280]{1,0:T(8,128)(2,1)}), bf16[5120,1280]{1,0:T(8,128)(2,1)}) %all-gather.4.cloned.1.call-update) | async-done | bytes 13107216 | tf_op jit(solution)/shard_map/all_gather | solution.py:18
  195.5 12.6 %convolution_convert_fusion.1 = bf16[512,1280]{1,0:T(8,128)(2,1)S(1)} fusion(bf16[512,5120]{1,0:T(8,128)(2,1)} %param.8, bf16[5120,1280]{1,0:T(8,128)(2,1)} %all-gather.4.cloned.1.call-done), kind=kOutput, calls=%fused_computation.7 | convolution fusion | flops 6711541760 | bytes 19660800 | tf_op jit(solution)/shard_map/dot_general | solution.py:11
  208.2 2.1 gather_fusion
  210.3 1.5 copy.27
  211.8 1.6 convolution_multiply_fusion.1
  213.4 0.2 fusion.30
  213.6 2.0 fusion.7
  215.6 3.2 copy.32
  218.8 2.1 gather_fusion.1
  221.0 0.7 copy.33
  221.6 0.3 convolution_multiply_fusion
  221.9 0.2 fusion.31
  222.1 2.0 fusion.6
  224.1 3.4 copy.37
  227.5 7.2 %scatter_custom_fusion = f32[512,1280]{1,0:T(8,128)} fusion(s32[512]{0:T(512)S(1)} %bitcast.39, f32[]{:T(128)} %constant.5.clone.1, f32[512,1280]{1,0:T(8,128)S(1)} %copy-done.2, pred[512]{0:T(512)(128)(4,1)S(1)} %iota_compare_fusion.1), kind=kCustom, calls=%fused_computation.21 | custom fusion | flops 1310720 | bytes 5244416 | tf_op jit(solution)/shard_map/scatter-add | solution.py:50
  234.7 9.8 %scatter_custom_fusion.1 = f32[512,1280]{1,0:T(8,128)} fusion(f32[512,1280]{1,0:T(8,128)} %scatter_custom_fusion, s32[512]{0:T(512)S(1)} %bitcast.37, f32[512,1280]{1,0:T(8,128)} %copy.37, f32[]{:T(128)} %constant.5.clone.1, pred[512]{0:T(512)(128)(4,1)S(1)} %iota_compare_fusion), kind=kCustom, calls=%fused_computation.8 | custom fusion | flops 1310720 | bytes 5243904 | tf_op jit(solution)/shard_map/scatter-add | solution.py:50
  244.5 2.9 convert_element_type.60
  247.4 131.3 %all-gather.8.cloned.1.call-done = bf16[5120,1280]{1,0:T(8,128)(2,1)} async-done(((bf16[640,1280]{1,0:T(8,128)(2,1)}), bf16[5120,1280]{1,0:T(8,128)(2,1)}) %all-gather.8.cloned.1.call-update) | async-done | bytes 13107216 | tf_op jit(solution)/shard_map/all_gather | solution.py:53
  378.8 40.2 %all-gather.6.cloned.1.call-done = bf16[512,5120]{1,0:T(8,128)(2,1)} async-done(((bf16[512,1280]{1,0:T(8,128)(2,1)}), bf16[512,5120]{1,0:T(8,128)(2,1)}) %all-gather.6.cloned.1.call-update) | async-done | bytes 5242896 | tf_op jit(solution)/shard_map/all_gather | solution.py:52
  419.0 13.6 %convolution_convert_fusion = bf16[512,1280]{1,0:T(8,128)(2,1)} fusion(bf16[512,5120]{1,0:T(8,128)(2,1)} %all-gather.6.cloned.1.call-done, bf16[5120,1280]{1,0:T(8,128)(2,1)} %all-gather.8.cloned.1.call-done), kind=kOutput, calls=%fused_computation.6 | convolution fusion | flops 6711541760 | bytes 19660800 | tf_op jit(solution)/shard_map/dot_general | solution.py:11
  (22 shorter events, 0.2 us)
Async XLA Ops:
  6.5 34.5 %copy-start = (bf16[768,1280]{1,0:T(8,128)(2,1)S(1)}, bf16[768,1280]{1,0:T(8,128)(2,1)}, u32[]{:S(2)}) copy-start(bf16[768,1280]{1,0:T(8,128)(2,1)} %param.12) | copy-start | bytes 5898244
  6.5 1.5 copy-start.3
  6.5 189.0 %all-gather.4.cloned.1.call-start = ((), (), s32[]{:S(2)}) async-start(), calls=%async_computation | async-start | bytes 14745600 | tf_op jit(solution)/shard_map/all_gather | solution.py:18
  7.3 371.5 %all-gather.8.cloned.1.call-start = ((), (), s32[]{:S(2)}) async-start(), calls=%async_computation.2 | async-start | bytes 14745600 | tf_op jit(solution)/shard_map/all_gather | solution.py:53
  8.0 411.0 %all-gather.6.cloned.1.call-start = ((), (), s32[]{:S(2)}) async-start(), calls=%async_computation.1 | async-start | bytes 6553600 | tf_op jit(solution)/shard_map/all_gather | solution.py:52
  41.0 2.8 copy-start.5
  41.0 4.8 %copy-start.4 = (s32[2,512]{1,0:T(2,128)S(1)}, s32[2,512]{1,0:T(2,128)}, u32[]{:S(2)}) copy-start(s32[2,512]{1,0:T(2,128)} %param.14) | copy-start | bytes 12292
  224.1 3.4 copy-start.2
  419.0 13.6 %copy-start.1 = (bf16[768,1280]{1,0:T(8,128)(2,1)S(1)}, bf16[768,1280]{1,0:T(8,128)(2,1)}, u32[]{:S(2)}) copy-start(bf16[768,1280]{1,0:T(8,128)(2,1)} %param.12) | copy-start | bytes 5898244
Sparse Core Ops, SparseCore 0:
  9.6 185.9 all-gather.3
  197.7 180.9 all-gather.7
  380.3 38.6 all-gather.5
where the time goes:
time: 439 us
  waiting for transfers between devices  323 us (74%)
  matrix products  34.7 us (8%)
  blocking collectives  32.9 us (7%)
  other arithmetic  21.6 us (5%)
  local copies, waits for them, and re-layouts  13.9 us (3%)
  between operations  13.3 us (3%)
    all_gather x1, waiting for transfers between devices, shards(): lax.all_gather(w_query, 'ctx', axis=0, tiled=True)  150 us
    all_gather x1, waiting for transfers between devices, shards(): lax.all_gather(w_output, 'ctx', axis=0, tiled=True)  131 us
    all_gather x1, waiting for transfers between devices, shards(): all_heads = lax.all_gather(attended, 'head', axis=1, tiled=True)  40.2 us
    all_gather x1, blocking collectives, shards(): whole_audio = lax.all_gather(audio_tokens, 'ctx', axis=1, tiled=True)  32.9 us
    dot_general x2, matrix products, add_rows(): return jnp.dot(left_rows, shard_piece, preferred_element_type=jnp.float32)  26.2 us
    scatter-add x2, other arithmetic, shards(): summed = summed.at[target].add(blended)  17 us
  transfers between devices with their start and end apart: 3, of which 3 were waited for; matrix products, arithmetic and copies ran while one was open for 13% of the time, Pallas kernels for 0%

commit v1 on v0

--- a/solution.py
+++ b/solution.py
@@ -1,17 +1,24 @@
+import functools
+
 import jax
 import jax.numpy as jnp
 from jax import lax
+from jax.experimental import pallas as pl
+from jax.experimental.pallas import tpu as pltpu
 from jax.sharding import PartitionSpec as P
 
 HD = 128
 SPK = 2
+AXES = ("ctx", "head")
+QUERY_CHUNKS = (3, 2)
+OUT_CHUNKS = (3, 3, 2, 2)
 
 
 def add_rows(left_rows, shard_piece):
     return jnp.dot(left_rows, shard_piece, preferred_element_type=jnp.float32)
 
 
-def shards(video_rows, w_query, w_output, audio_tokens, w_key, w_value, row_lists, row_counts):
+def plain_shards(video_rows, w_query, w_output, audio_tokens, w_key, w_value, row_lists, row_counts):
     rows_dev = video_rows.shape[0]
     columns = w_query.shape[1]
     heads_dev = columns // HD
@@ -54,6 +61,285 @@
     return result.astype(jnp.bfloat16)
 
 
+def pairs(move):
+    found = []
+    for z in range(4):
+        for x in range(2):
+            for h in range(4):
+                to = move(z, x, h)
+                if to is not None:
+                    found.append(((2 * z + x) * 4 + h, (2 * to[0] + to[1]) * 4 + to[2]))
+    return found
+
+
+ACROSS_X = pairs(lambda z, x, h: (z, 1 - x, h))
+ACROSS_Y = pairs(lambda z, x, h: (z, x, h ^ 2))
+ACROSS_CORE = pairs(lambda z, x, h: (z, x, h ^ 1))
+SWAP_END = pairs(lambda z, x, h: (z ^ 1, x, h))
+END_TO_MID = pairs(lambda z, x, h: (z ^ 1, x, h) if z in (0, 3) else None)
+MID_TO_END = pairs(lambda z, x, h: (z ^ 1, x, h) if z in (1, 2) else None)
+MID_TO_MID = pairs(lambda z, x, h: (3 - z, x, h) if z in (1, 2) else None)
+
+
+def send(value, move):
+    return lax.ppermute(value, AXES, move)
+
+
+def product_body(place, *refs, k_sizes):
+    *lefts, weights, kept, sent = refs
+    total = None
+    for j in range(4):
+        first = 0
+        for i, size in enumerate(k_sizes):
+            left = lefts[i * 4 + j][...]
+            right = weights[place[j], first : first + size, :]
+            term = jnp.dot(left, right, preferred_element_type=jnp.float32)
+            total = term if total is None else total + term
+            first += size
+    half = kept.shape[1]
+    kept[...] = total[:, :half]
+    sent[...] = total[:, half:]
+
+
+def query_product(place, lefts, weights, rows, from_columns):
+    depth, columns = weights.shape[1:]
+    step = min(rows, 512)
+    if from_columns:
+        left_specs = [
+            pl.BlockSpec((step, depth), functools.partial(lambda j, i, place: (i, place[4 + j]), j))
+            for j in range(4)
+        ]
+    else:
+        left_specs = [pl.BlockSpec((step, depth), lambda i, place: (i, 0)) for _ in range(4)]
+    half = columns // 2
+    part = jax.ShapeDtypeStruct((rows, half), jnp.float32)
+    return pl.pallas_call(
+        functools.partial(product_body, k_sizes=(depth,)),
+        grid_spec=pltpu.PrefetchScalarGridSpec(
+            num_scalar_prefetch=1,
+            grid=(rows // step,),
+            in_specs=left_specs + [pl.BlockSpec(weights.shape, lambda i, place: (0, 0, 0))],
+            out_specs=[pl.BlockSpec((step, half), lambda i, place: (i, 0))] * 2,
+        ),
+        out_shape=[part, part],
+        name="query_product",
+    )(place, *lefts, weights)
+
+
+def out_body(place, *refs, k_sizes):
+    *lefts, weights, total_out = refs
+    total = None
+    for j in range(4):
+        first = 0
+        for i, size in enumerate(k_sizes):
+            left = lefts[i * 4 + j][...]
+            right = weights[place[j], first : first + size, :]
+            term = jnp.dot(left, right, preferred_element_type=jnp.float32)
+            total = term if total is None else total + term
+            first += size
+    total_out[...] = total
+
+
+def out_product(place, lefts, weights, k_sizes):
+    rows = lefts[0].shape[0]
+    columns = weights.shape[2]
+    step = rows // 2
+    left_specs = [
+        pl.BlockSpec((step, size), lambda i, place: (i, 0)) for size in k_sizes for _ in range(4)
+    ]
+    return pl.pallas_call(
+        functools.partial(out_body, k_sizes=k_sizes),
+        grid_spec=pltpu.PrefetchScalarGridSpec(
+            num_scalar_prefetch=1,
+            grid=(2,),
+            in_specs=left_specs + [pl.BlockSpec(weights.shape, lambda i, place: (0, 0, 0))],
+            out_specs=pl.BlockSpec((step, columns), lambda i, place: (i, 0)),
+        ),
+        out_shape=jax.ShapeDtypeStruct((rows, columns), jnp.float32),
+        name="out_product",
+    )(place, *lefts, weights)
+
+
+def attend_body(kept, received, keys, values, speaker, attended, *, audio_length, heads):
+    scale = 1.0 / HD**0.5
+    of_row = speaker[...]
+    lane = lax.broadcasted_iota(jnp.int32, (kept.shape[0], SPK * audio_length), 1)
+    of_key = jnp.where(lane < audio_length, 1, 2)
+    own_key = of_key == of_row
+    live = of_row > 0
+    for head in range(heads):
+        at = slice(head * HD, (head + 1) * HD)
+        query = (kept[:, at] + received[:, at]).astype(jnp.bfloat16)
+        scores = (
+            lax.dot_general(
+                query, keys[:, at], (((1,), (1,)), ((), ())), preferred_element_type=jnp.float32
+            )
+            * scale
+        )
+        scores = jnp.where(own_key, scores, -1e30)
+        scores = scores - jnp.max(scores, axis=-1, keepdims=True)
+        weights = jnp.exp(scores)
+        weights = (weights / jnp.sum(weights, axis=-1, keepdims=True)).astype(jnp.bfloat16)
+        blended = jnp.dot(weights, values[:, at], preferred_element_type=jnp.float32)
+        attended[:, at] = jnp.where(live, blended, 0.0).astype(jnp.bfloat16)
+
+
+def attend(kept, received, keys, values, speaker, audio_length, swap):
+    rows, columns = kept.shape
+    step = rows // 2 if swap else min(rows, 512)
+    count = rows // step
+    flip = (lambda i: (count - 1 - i, 0)) if swap else (lambda i: (i, 0))
+    at = lambda i: (i, 0)
+    whole = pl.BlockSpec(keys.shape, lambda i: (0, 0))
+    return pl.pallas_call(
+        functools.partial(attend_body, audio_length=audio_length, heads=columns // HD),
+        grid=(count,),
+        in_specs=[
+            pl.BlockSpec((step, columns), at),
+            pl.BlockSpec((step, columns), flip),
+            whole,
+            whole,
+            pl.BlockSpec((step, 1), at),
+        ],
+        out_specs=pl.BlockSpec((step, columns), at),
+        out_shape=jax.ShapeDtypeStruct((rows, columns), jnp.bfloat16),
+        name="attend",
+    )(kept, received, keys, values, speaker)
+
+
+def head_pieces(value):
+    over_y = send(value, ACROSS_Y)
+    both = send(jnp.concatenate([value, over_y], axis=0), ACROSS_CORE)
+    rows = value.shape[0]
+    return [value, both[:rows], over_y, both[rows:]]
+
+
+def plane_shards(video_rows, w_query, w_output, audio_tokens, w_key, w_value, row_lists, row_counts):
+    rows, width = video_rows.shape
+    block = w_query.shape[0]
+    columns = w_query.shape[1]
+    audio_width = audio_tokens.shape[2]
+    ctx = lax.axis_index("ctx").astype(jnp.int32)
+    h = lax.axis_index("head").astype(jnp.int32)
+    z, x = ctx // 2, ctx % 2
+    is_mid = (z == 1) | (z == 2)
+    z_mid = jnp.where(is_mid, z, z ^ 1)
+
+    query_weights = []
+    first = 0
+    for heads in QUERY_CHUNKS:
+        size = heads * HD
+        query_weights.append(
+            jnp.concatenate(
+                [
+                    lax.dynamic_slice(w_query, (0, x * block + first), (block, size)),
+                    lax.dynamic_slice(w_query, (0, (1 - x) * block + first), (block, size)),
+                ],
+                axis=1,
+            )
+        )
+        first += size
+    k_sizes = tuple(heads * HD for heads in QUERY_CHUNKS)
+
+    def video_block(at):
+        return lax.dynamic_slice(video_rows, (0, at * block), (rows, block))
+
+    quarter_own = video_block(2 * (z_mid ^ h) + x)
+    quarter_near = send(video_block(2 * (z_mid ^ h) + 1 - x), ACROSS_X)
+
+    position = jnp.arange(rows, dtype=jnp.int32)
+    named = (row_lists[:, :, None] == position[None, None, :]) & (
+        position[None, :, None] < row_counts[:, :, None]
+    )
+    speaker_of = jnp.sum(
+        jnp.any(named, axis=1) * jnp.array([[1], [2]], jnp.int32), axis=0
+    ).astype(jnp.bfloat16)
+    tokens = audio_tokens.shape[1]
+    gathered = lax.all_gather(
+        jnp.concatenate([audio_tokens.reshape(-1), speaker_of]), "ctx", axis=0
+    )
+    whole_audio = (
+        gathered[:, : SPK * tokens * audio_width]
+        .reshape(-1, SPK, tokens, audio_width)
+        .transpose(1, 0, 2, 3)
+        .reshape(-1, audio_width)
+    )
+    audio_length = whole_audio.shape[0] // SPK
+    speakers = gathered[:, SPK * tokens * audio_width :].astype(jnp.int32)
+    speaker_own = jnp.concatenate([speakers[ctx], speakers[ctx ^ 1]])[:, None]
+    speaker_guest = jnp.concatenate([speakers[ctx ^ 2], speakers[ctx ^ 3]])[:, None]
+    key_rows = add_rows(
+        whole_audio, lax.dynamic_slice(w_key, (0, x * block), (audio_width, block))
+    ).astype(jnp.bfloat16)
+    value_rows = add_rows(
+        whole_audio, lax.dynamic_slice(w_value, (0, x * block), (audio_width, block))
+    ).astype(jnp.bfloat16)
+
+    stacks = []
+    for piece in query_weights:
+        from_end = send(piece, END_TO_MID)
+        from_mid = send(piece, MID_TO_MID)
+        from_far = send(from_end, MID_TO_MID)
+        stacks.append(jnp.stack([piece, from_end, from_far, from_mid]))
+
+    guest = send(jnp.concatenate([quarter_own, quarter_near], axis=0), END_TO_MID)
+    near_pieces = head_pieces(quarter_near)
+    guest_pieces = head_pieces(guest)
+    order = jnp.arange(4, dtype=jnp.int32) ^ h
+    place = jnp.concatenate([order, 2 * (z_mid ^ order) + x])
+
+    attended = []
+    first = 0
+    for stack, size in zip(stacks, k_sizes):
+        at = slice(first, first + size)
+        guest_kept, guest_sent = query_product(place, guest_pieces, stack, 2 * rows, False)
+        guest_received = send(guest_sent, ACROSS_X)
+        own_kept, own_sent = query_product(place, [video_rows] * 4, stack, rows, True)
+        near_kept, near_sent = query_product(place, near_pieces, stack, rows, False)
+        plane_received = send(jnp.concatenate([own_sent, near_sent], axis=0), ACROSS_X)
+        guest_attended = attend(
+            guest_kept, guest_received, key_rows[:, at], value_rows[:, at], speaker_guest, audio_length, True
+        )
+        from_mid = send(guest_attended, MID_TO_END)
+        plane_attended = attend(
+            jnp.concatenate([own_kept, near_kept], axis=0),
+            plane_received,
+            key_rows[:, at],
+            value_rows[:, at],
+            speaker_own,
+            audio_length,
+            True,
+        )
+        attended.append(head_pieces(jnp.where(is_mid, plane_attended, from_mid)))
+        first += size
+
+    out_place = order ^ z
+    results = []
+    first = 0
+    for chunk in OUT_CHUNKS:
+        size = chunk * HD
+        piece = lax.slice_in_dim(w_output, first, first + size, axis=1)
+        near = send(piece, SWAP_END)
+        from_mid = send(piece, MID_TO_MID)
+        from_far = send(near, MID_TO_MID)
+        end_mid = send(from_mid, MID_TO_END)
+        end_far = send(from_far, MID_TO_END)
+        stack = jnp.stack(
+            [
+                piece,
+                near,
+                jnp.where(is_mid, from_far, end_mid),
+                jnp.where(is_mid, from_mid, end_far),
+            ]
+        )
+        lefts = [part for pieces in attended for part in pieces]
+        total = out_product(out_place, lefts, stack, k_sizes)
+        received = send(total[rows:], ACROSS_X)
+        results.append((total[:rows] + received).astype(jnp.bfloat16))
+        first += size
+    return jnp.concatenate(results, axis=1)
+
+
 def solution(mesh):
     in_specs = (
         P("ctx", None),
@@ -66,4 +352,6 @@
         P(None, "ctx"),
     )
     out_specs = P("ctx", "head")
+    planes = mesh.shape["ctx"] == 8 and mesh.shape["head"] == 4
+    shards = plane_shards if planes else plain_shards
     return jax.shard_map(shards, mesh=mesh, in_specs=in_specs, out_specs=out_specs, check_vma=False)

time: 439 us -> 483 us (1.10)
  waiting for transfers between devices: 323 us -> 162 us
  Pallas kernels: 0 us -> 89.9 us
  starting transfers between devices: 0.08 us -> 76.6 us
  blocking collectives: 32.9 us -> 84.8 us
  matrix products: 34.7 us -> 1.8 us
  other arithmetic: 21.6 us -> 38.7 us
  local copies, waits for them, and re-layouts: 13.9 us -> 26.8 us
  between operations: 13.3 us -> 0.67 us
    all_gather x3 -> x0, waiting for transfers between devices: 321 us -> none  [the longest x1 150 us: shards(): lax.all_gather(w_query, 'ctx', axis=0, tiled=True)]
    ppermute x0 -> x46, waiting for transfers between devices: none -> 162 us  [send(): return lax.ppermute(value, AXES, move)]
    pallas_call x0 -> x14, Pallas kernels: none -> 89.9 us  [the longest x6 44.9 us: query_product(): pl.pallas_call(functools.partial(product_body, k_sizes=(depth,)), grid_sp...]
    ppermute x0 -> x46, starting transfers between devices: none -> 76.6 us  [send(): return lax.ppermute(value, AXES, move)]
    all_gather x1, blocking collectives: 32.9 us -> 84.8 us  [plane_shards(): lax.all_gather(jnp.concatenate([audio_tokens.reshape(-1), speaker_of]), '...]
    dot_general x2, matrix products: 26.2 us -> 1.8 us  [add_rows(): return jnp.dot(left_rows, shard_piece, preferred_element_type=jnp.float32)]
    another operation x0 -> x16, other arithmetic: none -> 19.2 us  [the longest x12 10.1 us: plane_shards(): jnp.stack([piece, near, jnp.where(is_mid, from_far, end_mid), jnp.where(i...]
    scatter-add x2 -> x0, other arithmetic: 17 us -> none  [shards(): summed = summed.at[target].add(blended)]
  transfers between devices with their start and end apart: 3 -> 46, of which waited for: 3 -> 14; matrix products, arithmetic and copies ran while one was open for 13% -> 13% of each run, Pallas kernels for 0% -> 19%
where the time goes in v1:
time: 483 us; the launch traced here: 481 us
  waiting for transfers between devices  162 us (34%)
  Pallas kernels  89.9 us (19%)
  blocking collectives  84.8 us (18%)
  starting transfers between devices  76.6 us (16%)
  other arithmetic  38.7 us (8%)
  local copies, waits for them, and re-layouts  26.8 us (6%)
    ppermute x46, waiting for transfers between devices, send(): return lax.ppermute(value, AXES, move)  162 us
    all_gather x1, blocking collectives, plane_shards(): lax.all_gather(jnp.concatenate([audio_tokens.reshape(-1), speaker_of]), '...  84.8 us
    ppermute x46, starting transfers between devices, send(): return lax.ppermute(value, AXES, move)  76.6 us
    pallas_call x6, Pallas kernels, query_product(): pl.pallas_call(functools.partial(product_body, k_sizes=(depth,)), grid_sp...  44.9 us
    pallas_call x4, Pallas kernels, out_product(): pl.pallas_call(functools.partial(out_body, k_sizes=k_sizes), grid_spec=pl...  27.9 us
    pallas_call x4, Pallas kernels, attend(): pl.pallas_call(functools.partial(attend_body, audio_length=audio_length,...  17.1 us
    another operation x12, other arithmetic, plane_shards(): jnp.stack([piece, near, jnp.where(is_mid, from_far, end_mid), jnp.where(i...  10.1 us
  transfers between devices with their start and end apart: 46, of which 14 were waited for; matrix products, arithmetic and copies ran while one was open for 13% of the time, Pallas kernels for 19%

profile of v1, /device:TPU:0, one launch (start us, length us, event | category | flops | bytes accessed | tf_op | source)
XLA Modules:
  0.0 481.0 jit_solution(6142347665888110405)
XLA Ops:
  4.6 14.7 %collective-permute-done.3.refs_0_ = bf16[512,640]{1,0:T(8,128)(2,1)S(1)} collective-permute-done((bf16[512,640]{1,0:T(8,128)(2,1)S(1)}, bf16[512,640]{1,0:T(8,128)(2,1)S(1)}, u32[]{:S(2)}, u32[]{:S(2)}) %collective-permute-start.3) | collective-permute-done | bytes 655392 | tf_op jit(solution)/shard_map/ppermute | solution.py:85
  21.1 14.2 %collective-permute-done.4.refs_2_ = bf16[512,640]{1,0:T(8,128)(2,1)S(1)} collective-permute-done((bf16[512,640]{1,0:T(8,128)(2,1)S(1)}, bf16[512,640]{1,0:T(8,128)(2,1)S(1)}, u32[]{:S(2)}, u32[]{:S(2)}) %collective-permute-start.4) | collective-permute-done | bytes 655392 | tf_op jit(solution)/shard_map/ppermute | solution.py:85
  40.0 26.1 %collective-permute-done.7.refs_0_ = bf16[1024,640]{1,0:T(8,128)(2,1)S(1)} collective-permute-done((bf16[1024,640]{1,0:T(8,128)(2,1)S(1)}, bf16[1024,640]{1,0:T(8,128)(2,1)S(1)}, u32[]{:S(2)}, u32[]{:S(2)}) %collective-permute-start.7) | collective-permute-done | bytes 1310752 | tf_op jit(solution)/shard_map/ppermute | solution.py:85
  67.6 26.3 %collective-permute-done.8.refs_2_ = bf16[1024,640]{1,0:T(8,128)(2,1)S(1)} collective-permute-done((bf16[1024,640]{1,0:T(8,128)(2,1)S(1)}, bf16[1024,640]{1,0:T(8,128)(2,1)S(1)}, u32[]{:S(2)}, u32[]{:S(2)}) %collective-permute-start.8) | collective-permute-done | bytes 1310752 | tf_op jit(solution)/shard_map/ppermute | solution.py:85
  98.2 5.5 %collective-permute-start = (bf16[640,768]{1,0:T(8,128)(2,1)}, bf16[640,768]{1,0:T(8,128)(2,1)}, u32[]{:S(2)}, u32[]{:S(2)}) collective-permute-start(bf16[640,768]{1,0:T(8,128)(2,1)} %get-tuple-element.52), channel_id=1, source_target_pairs={{0,8},{1,9},{2,10},{3,11},{4,12},{5,13},{6,14},{7,15},{24,16},{25,... | collective-permute-start | bytes 2949128 | tf_op jit(solution)/shard_map/ppermute | solution.py:85
  109.3 15.4 %collective-permute-done = bf16[640,768]{1,0:T(8,128)(2,1)} collective-permute-done((bf16[640,768]{1,0:T(8,128)(2,1)}, bf16[640,768]{1,0:T(8,128)(2,1)}, u32[]{:S(2)}, u32[]{:S(2)}) %collective-permute-start) | collective-permute-done | bytes 983072 | tf_op jit(solution)/shard_map/ppermute | solution.py:85
  129.9 7.1 %collective-permute-start.14 = (bf16[640,512]{1,0:T(8,128)(2,1)}, bf16[640,512]{1,0:T(8,128)(2,1)}, u32[]{:S(2)}, u32[]{:S(2)}) collective-permute-start(bf16[640,512]{1,0:T(8,128)(2,1)} %get-tuple-element.54), channel_id=1, source_target_pairs={{0,8},{1,9},{2,10},{3,11},{4,12},{5,13},{6,14},{7,15},{24,16},{25,... | collective-permute-start | bytes 1966088 | tf_op jit(solution)/shard_map/ppermute | solution.py:85
  141.9 3.5 fusion.12
  145.4 10.1 %query_product.8 = (f32[1024,384]{1,0:T(8,128)}, f32[1024,384]{1,0:T(8,128)}) custom-call(s32[8]{0:T(128)} %pad_add_fusion.2.place, bf16[1024,640]{1,0:T(8,128)(2,1)} %copy-done.6, bf16[1024,640]{1,0:T(8,128)(2,1)} %get-tuple-element.32.refs_1_, bf16[1024,640]{1,0:T(8,128)(2,1)} %copy-done.7, bf16[1024,640]{1,0:T(8,128)(2,1)} %get-tuple-element.31.refs_3_, ...), custom_call_target="tpu_custom_call" | custom-call | tf_op jit(solution)/shard_map/query_product/pallas_call | solution.py:116
  156.9 84.8 %all-gather.1 = bf16[8,1,6656]{2,1,0:T(2,128)(2,1)S(1)} all-gather(bf16[1,1,6656]{2,1,0:T(2,128)(2,1)S(1)} %reshape.41), channel_id=2, replica_groups=mesh['ctx'=8,'head'=4] {'ctx'}, dimensions={0}, use_global_device_ids=true | all-gather | bytes 119808 | tf_op jit(solution)/shard_map/all_gather | solution.py:258
  245.2 7.4 %query_product.6 = (f32[512,384]{1,0:T(8,128)}, f32[512,384]{1,0:T(8,128)}) custom-call(s32[8]{0:T(128)} %pad_add_fusion.2.place, bf16[512,5120]{1,0:T(8,128)(2,1)} %refs_3_.3, bf16[512,5120]{1,0:T(8,128)(2,1)} %refs_3_.3, bf16[512,5120]{1,0:T(8,128)(2,1)} %refs_3_.3, bf16[512,5120]{1,0:T(8,128)(2,1)} %refs_3_.3, bf16[4,640,768]{2,1,0:T(8,128)(2,1)} %pad_maximum_fusion.refs_4_), custom_call_target="tpu_custom_call" | custom-call | tf_op jit(solution)/shard_map/query_product/pallas_call | solution.py:116
  255.1 7.3 %query_product.7 = (f32[512,384]{1,0:T(8,128)}, f32[512,384]{1,0:T(8,128)}) custom-call(s32[8]{0:T(128)} %pad_add_fusion.2.place, bf16[512,640]{1,0:T(8,128)(2,1)} %copy-done.10, bf16[512,640]{1,0:T(8,128)(2,1)} %get-tuple-element.48.refs_1_, bf16[512,640]{1,0:T(8,128)(2,1)} %copy-done.11, bf16[512,640]{1,0:T(8,128)(2,1)} %get-tuple-element.47.refs_3_, ...), custom_call_target="tpu_custom_call" | custom-call | tf_op jit(solution)/shard_map/query_product/pallas_call | solution.py:116
  275.5 8.0 %query_product.11 = (f32[1024,256]{1,0:T(8,128)}, f32[1024,256]{1,0:T(8,128)}) custom-call(s32[8]{0:T(128)} %pad_add_fusion.2.place, bf16[1024,640]{1,0:T(8,128)(2,1)} %copy-done.6, bf16[1024,640]{1,0:T(8,128)(2,1)} %get-tuple-element.32.refs_1_, bf16[1024,640]{1,0:T(8,128)(2,1)} %copy-done.7, bf16[1024,640]{1,0:T(8,128)(2,1)} %get-tuple-element.31.refs_3_, ...), custom_call_target="tpu_custom_call" | custom-call | tf_op jit(solution)/shard_map/query_product/pallas_call | solution.py:116
  288.9 6.0 %query_product.9 = (f32[512,256]{1,0:T(8,128)}, f32[512,256]{1,0:T(8,128)}) custom-call(s32[8]{0:T(128)} %pad_add_fusion.2.place, bf16[512,5120]{1,0:T(8,128)(2,1)} %refs_3_.3, bf16[512,5120]{1,0:T(8,128)(2,1)} %refs_3_.3, bf16[512,5120]{1,0:T(8,128)(2,1)} %refs_3_.3, bf16[512,5120]{1,0:T(8,128)(2,1)} %refs_3_.3, bf16[4,640,512]{2,1,0:T(8,128)(2,1)} %pad_maximum_fusion.2.refs_4_), custom_call_target="tpu_custom_call" | custom-call | tf_op jit(solution)/shard_map/query_product/pallas_call | solution.py:116
  294.9 6.1 %query_product.10 = (f32[512,256]{1,0:T(8,128)}, f32[512,256]{1,0:T(8,128)}) custom-call(s32[8]{0:T(128)} %pad_add_fusion.2.place, bf16[512,640]{1,0:T(8,128)(2,1)} %copy-done.10, bf16[512,640]{1,0:T(8,128)(2,1)} %get-tuple-element.48.refs_1_, bf16[512,640]{1,0:T(8,128)(2,1)} %copy-done.11, bf16[512,640]{1,0:T(8,128)(2,1)} %get-tuple-element.47.refs_3_, ...), custom_call_target="tpu_custom_call" | custom-call | tf_op jit(solution)/shard_map/query_product/pallas_call | solution.py:116
  303.1 4.6 attend.5
  316.0 15.2 %collective-permute-done.37 = bf16[640,256]{1,0:T(8,128)(2,1)S(1)} collective-permute-done((bf16[640,256]{1,0:T(8,128)(2,1)S(1)}, bf16[640,256]{1,0:T(8,128)(2,1)S(1)}, u32[]{:S(2)}, u32[]{:S(2)}) %collective-permute-start.37) | collective-permute-done | bytes 327712 | tf_op jit(solution)/shard_map/ppermute | solution.py:85
  333.6 4.0 attend.7
  342.9 4.6 attend.4
  352.8 4.0 attend.6
  356.8 4.1 collective-permute-start.28
  361.7 3.7 collective-permute-start.22
  371.4 5.8 %collective-permute-done.28 = bf16[640,384]{1,0:T(8,128)(2,1)S(1)} collective-permute-done((bf16[640,384]{1,0:T(8,128)(2,1)}, bf16[640,384]{1,0:T(8,128)(2,1)S(1)}, u32[]{:S(2)}, u32[]{:S(2)}) %collective-permute-start.28) | collective-permute-done | bytes 491552 | tf_op jit(solution)/shard_map/ppermute | solution.py:85
  379.2 8.5 %collective-permute-done.22 = bf16[640,384]{1,0:T(8,128)(2,1)S(1)} collective-permute-done((bf16[640,384]{1,0:T(8,128)(2,1)}, bf16[640,384]{1,0:T(8,128)(2,1)S(1)}, u32[]{:S(2)}, u32[]{:S(2)}) %collective-permute-start.22) | collective-permute-done | bytes 491552 | tf_op jit(solution)/shard_map/ppermute | solution.py:85
  399.2 5.1 %collective-permute-done.25 = bf16[640,384]{1,0:T(8,128)(2,1)S(1)} collective-permute-done((bf16[640,384]{1,0:T(8,128)(2,1)S(1)}, bf16[640,384]{1,0:T(8,128)(2,1)S(1)}, u32[]{:S(2)}, u32[]{:S(2)}) %collective-permute-start.25) | collective-permute-done | bytes 491552 | tf_op jit(solution)/shard_map/ppermute | solution.py:85
  404.4 10.5 %collective-permute-done.32 = bf16[640,384]{1,0:T(8,128)(2,1)S(1)} collective-permute-done((bf16[640,384]{1,0:T(8,128)(2,1)S(1)}, bf16[640,384]{1,0:T(8,128)(2,1)S(1)}, u32[]{:S(2)}, u32[]{:S(2)}) %collective-permute-start.32) | collective-permute-done | bytes 491552 | tf_op jit(solution)/shard_map/ppermute | solution.py:85
  417.3 6.2 %out_product.7 = f32[1024,256]{1,0:T(8,128)} custom-call(s32[4]{0:T(128)} %broadcast_xor_fusion.place, bf16[1024,384]{1,0:T(8,128)(2,1)} %copy-done.2, bf16[1024,384]{1,0:T(8,128)(2,1)} %get-tuple-element.46.refs_1_, bf16[1024,384]{1,0:T(8,128)(2,1)} %copy-done.3, bf16[1024,384]{1,0:T(8,128)(2,1)} %get-tuple-element.45.refs_3_, bf16[1024,256]{1,0:T(8,128)(2,1)} %copy-done.4, ...), custom_call_target="tpu_custom_call" | custom-call | tf_op jit(solution)/shard_map/out_product/pallas_call | solution.py:150
  428.4 6.0 %out_product.6 = f32[1024,256]{1,0:T(8,128)} custom-call(s32[4]{0:T(128)} %broadcast_xor_fusion.place, bf16[1024,384]{1,0:T(8,128)(2,1)} %copy-done.2, bf16[1024,384]{1,0:T(8,128)(2,1)} %get-tuple-element.46.refs_1_, bf16[1024,384]{1,0:T(8,128)(2,1)} %copy-done.3, bf16[1024,384]{1,0:T(8,128)(2,1)} %get-tuple-element.45.refs_3_, bf16[1024,256]{1,0:T(8,128)(2,1)} %copy-done.4, ...), custom_call_target="tpu_custom_call" | custom-call | tf_op jit(solution)/shard_map/out_product/pallas_call | solution.py:150
  436.9 7.8 %out_product.5 = f32[1024,384]{1,0:T(8,128)} custom-call(s32[4]{0:T(128)} %broadcast_xor_fusion.place, bf16[1024,384]{1,0:T(8,128)(2,1)} %copy-done.2, bf16[1024,384]{1,0:T(8,128)(2,1)} %get-tuple-element.46.refs_1_, bf16[1024,384]{1,0:T(8,128)(2,1)} %copy-done.3, bf16[1024,384]{1,0:T(8,128)(2,1)} %get-tuple-element.45.refs_3_, bf16[1024,256]{1,0:T(8,128)(2,1)} %copy-done.4, ...), custom_call_target="tpu_custom_call" | custom-call | tf_op jit(solution)/shard_map/out_product/pallas_call | solution.py:150
  450.2 7.9 %out_product.4 = f32[1024,384]{1,0:T(8,128)} custom-call(s32[4]{0:T(128)} %broadcast_xor_fusion.place, bf16[1024,384]{1,0:T(8,128)(2,1)} %copy-done.2, bf16[1024,384]{1,0:T(8,128)(2,1)} %get-tuple-element.46.refs_1_, bf16[1024,384]{1,0:T(8,128)(2,1)} %copy-done.3, bf16[1024,384]{1,0:T(8,128)(2,1)} %get-tuple-element.45.refs_3_, bf16[1024,256]{1,0:T(8,128)(2,1)} %copy-done.4, ...), custom_call_target="tpu_custom_call" | custom-call | tf_op jit(solution)/shard_map/out_product/pallas_call | solution.py:150
  462.3 4.3 collective-permute-done.33
  468.0 11.8 %collective-permute-done.27 = f32[512,384]{1,0:T(8,128)S(1)} collective-permute-done((f32[512,384]{1,0:T(8,128)S(1)}, f32[512,384]{1,0:T(8,128)S(1)}, u32[]{:S(2)}, u32[]{:S(2)}) %collective-permute-start.27) | collective-permute-done | bytes 786464 | tf_op jit(solution)/shard_map/ppermute | solution.py:85
  (229 shorter events, 123.9 us)
Async XLA Ops:
  36.5 29.6 %collective-permute-start.7 = (bf16[1024,640]{1,0:T(8,128)(2,1)S(1)}, bf16[1024,640]{1,0:T(8,128)(2,1)S(1)}, u32[]{:S(2)}, u32[]{:S(2)}) collective-permute-start(bf16[1024,640]{1,0:T(8,128)(2,1)S(1)} %get-tuple-element.55), channel_id=1, source_target_pairs={{0,8},{1,9},{2,10},{3,11},{4,12},{5,13},{6,14},{7,15},{24,16},{25,... | collective-permute-start | bytes 3932168 | tf_op jit(solution)/shard_map/ppermute | solution.py:85
  66.1 27.8 %collective-permute-start.8 = (bf16[1024,640]{1,0:T(8,128)(2,1)S(1)}, bf16[1024,640]{1,0:T(8,128)(2,1)S(1)}, u32[]{:S(2)}, u32[]{:S(2)}) collective-permute-start(bf16[1024,640]{1,0:T(8,128)(2,1)S(1)} %collective-permute-done.7.refs_0_), channel_id=1, source_target_pairs={{0,2},{1,3},{2,0},{3,1},{4,6},{5,7},{6,4},{7,5},{8,10},{9,11},{10,... | collective-permute-start | bytes 3932168 | tf_op jit(solution)/shard_map/ppermute | solution.py:85
  95.8 46.1 %collective-permute-start.9 = (bf16[2048,640]{1,0:T(8,128)(2,1)}, bf16[2048,640]{1,0:T(8,128)(2,1)}, u32[]{:S(2)}, u32[]{:S(2)}) collective-permute-start(bf16[2048,640]{1,0:T(8,128)(2,1)} %pad_maximum_fusion.1), channel_id=1, source_target_pairs={{0,1},{1,0},{2,3},{3,2},{4,5},{5,4},{6,7},{7,6},{8,9},{9,8},{10,11... | collective-permute-start | bytes 7864328 | tf_op jit(solution)/shard_map/ppermute | solution.py:85
  98.2 26.5 %collective-permute-start = (bf16[640,768]{1,0:T(8,128)(2,1)}, bf16[640,768]{1,0:T(8,128)(2,1)}, u32[]{:S(2)}, u32[]{:S(2)}) collective-permute-start(bf16[640,768]{1,0:T(8,128)(2,1)} %get-tuple-element.52), channel_id=1, source_target_pairs={{0,8},{1,9},{2,10},{3,11},{4,12},{5,13},{6,14},{7,15},{24,16},{25,... | collective-permute-start | bytes 2949128 | tf_op jit(solution)/shard_map/ppermute | solution.py:85
  103.7 26.2 %collective-permute-start.2 = (bf16[640,768]{1,0:T(8,128)(2,1)}, bf16[640,768]{1,0:T(8,128)(2,1)}, u32[]{:S(2)}, u32[]{:S(2)}) collective-permute-start(bf16[640,768]{1,0:T(8,128)(2,1)} %get-tuple-element.52), channel_id=1, source_target_pairs={{8,16},{9,17},{10,18},{11,19},{12,20},{13,21},{14,22},{15,23},{16,... | collective-permute-start | bytes 2949128 | tf_op jit(solution)/shard_map/ppermute | solution.py:85
  107.8 157.9 %collective-permute-start.16 = (bf16[640,512]{1,0:T(8,128)(2,1)}, bf16[640,512]{1,0:T(8,128)(2,1)}, u32[]{:S(2)}, u32[]{:S(2)}) collective-permute-start(bf16[640,512]{1,0:T(8,128)(2,1)} %get-tuple-element.54), channel_id=1, source_target_pairs={{8,16},{9,17},{10,18},{11,19},{12,20},{13,21},{14,22},{15,23},{16,... | collective-permute-start | bytes 1966088 | tf_op jit(solution)/shard_map/ppermute | solution.py:85
  129.2 123.4 %collective-permute-start.5 = (bf16[1024,640]{1,0:T(8,128)(2,1)}, bf16[1024,640]{1,0:T(8,128)(2,1)}, u32[]{:S(2)}, u32[]{:S(2)}) collective-permute-start(bf16[1024,640]{1,0:T(8,128)(2,1)} %get-tuple-element.56), channel_id=1, source_target_pairs={{0,1},{1,0},{2,3},{3,2},{4,5},{5,4},{6,7},{7,6},{8,9},{9,8},{10,11... | collective-permute-start | bytes 3932168 | tf_op jit(solution)/shard_map/ppermute | solution.py:85
  129.9 111.9 %collective-permute-start.14 = (bf16[640,512]{1,0:T(8,128)(2,1)}, bf16[640,512]{1,0:T(8,128)(2,1)}, u32[]{:S(2)}, u32[]{:S(2)}) collective-permute-start(bf16[640,512]{1,0:T(8,128)(2,1)} %get-tuple-element.54), channel_id=1, source_target_pairs={{0,8},{1,9},{2,10},{3,11},{4,12},{5,13},{6,14},{7,15},{24,16},{25,... | collective-permute-start | bytes 1966088 | tf_op jit(solution)/shard_map/ppermute | solution.py:85
  137.0 127.9 %collective-permute-start.42 = (bf16[640,256]{1,0:T(8,128)(2,1)}, bf16[640,256]{1,0:T(8,128)(2,1)}, u32[]{:S(2)}, u32[]{:S(2)}) collective-permute-start(bf16[640,256]{1,0:T(8,128)(2,1)} %get-tuple-element.39), channel_id=1, source_target_pairs={{8,16},{9,17},{10,18},{11,19},{12,20},{13,21},{14,22},{15,23},{16,... | collective-permute-start | bytes 983048 | tf_op jit(solution)/shard_map/ppermute | solution.py:85
  155.4 131.0 %collective-permute-start.10 = (f32[1024,384]{1,0:T(8,128)}, f32[1024,384]{1,0:T(8,128)}, u32[]{:S(2)}, u32[]{:S(2)}) collective-permute-start(f32[1024,384]{1,0:T(8,128)} %get-tuple-element.22), channel_id=1, source_target_pairs={{0,4},{1,5},{2,6},{3,7},{4,0},{5,1},{6,2},{7,3},{8,12},{9,13},{10,... | collective-permute-start | bytes 4718600 | tf_op jit(solution)/shard_map/ppermute | solution.py:85
  241.8 27.1 %collective-permute-start.15 = (bf16[640,512]{1,0:T(8,128)(2,1)}, bf16[640,512]{1,0:T(8,128)(2,1)}, u32[]{:S(2)}, u32[]{:S(2)}) collective-permute-start(bf16[640,512]{1,0:T(8,128)(2,1)} %collective-permute-done.14), channel_id=1, source_target_pairs={{8,16},{9,17},{10,18},{11,19},{12,20},{13,21},{14,22},{15,23},{16,... | collective-permute-start | bytes 1966088 | tf_op jit(solution)/shard_map/ppermute | solution.py:85
  252.6 30.9 %collective-permute-start.40 = (bf16[640,256]{1,0:T(8,128)(2,1)S(1)}, bf16[640,256]{1,0:T(8,128)(2,1)S(1)}, u32[]{:S(2)}, u32[]{:S(2)}) collective-permute-start(bf16[640,256]{1,0:T(8,128)(2,1)S(1)} %copy-done.37), channel_id=1, source_target_pairs={{0,8},{1,9},{2,10},{3,11},{4,12},{5,13},{6,14},{7,15},{8,0},{9,1},... | collective-permute-start | bytes 983048 | tf_op jit(solution)/shard_map/ppermute | solution.py:85
  265.6 20.6 %collective-permute-start.34 = (bf16[640,256]{1,0:T(8,128)(2,1)S(1)}, bf16[640,256]{1,0:T(8,128)(2,1)S(1)}, u32[]{:S(2)}, u32[]{:S(2)}) collective-permute-start(bf16[640,256]{1,0:T(8,128)(2,1)S(1)} %copy-done.36), channel_id=1, source_target_pairs={{0,8},{1,9},{2,10},{3,11},{4,12},{5,13},{6,14},{7,15},{8,0},{9,1},... | collective-permute-start | bytes 983048 | tf_op jit(solution)/shard_map/ppermute | solution.py:85
  268.9 72.6 %collective-permute-start.6 = (f32[1024,384]{1,0:T(8,128)}, f32[1024,384]{1,0:T(8,128)}, u32[]{:S(2)}, u32[]{:S(2)}) collective-permute-start(f32[1024,384]{1,0:T(8,128)} %pad_maximum_fusion.6), channel_id=1, source_target_pairs={{0,4},{1,5},{2,6},{3,7},{4,0},{5,1},{6,2},{7,3},{8,12},{9,13},{10,... | collective-permute-start | bytes 4718600 | tf_op jit(solution)/shard_map/ppermute | solution.py:85
  283.5 24.1 %collective-permute-start.41 = (bf16[640,256]{1,0:T(8,128)(2,1)S(1)}, bf16[640,256]{1,0:T(8,128)(2,1)}, u32[]{:S(2)}, u32[]{:S(2)}) collective-permute-start(bf16[640,256]{1,0:T(8,128)(2,1)S(1)} %collective-permute-done.40), channel_id=1, source_target_pairs={{8,16},{9,17},{10,18},{11,19},{12,20},{13,21},{14,22},{15,23},{16,... | collective-permute-start | bytes 983048 | tf_op jit(solution)/shard_map/ppermute | solution.py:85
  284.9 24.6 %collective-permute-start.43 = (bf16[640,256]{1,0:T(8,128)(2,1)}, bf16[640,256]{1,0:T(8,128)(2,1)}, u32[]{:S(2)}, u32[]{:S(2)}) collective-permute-start(bf16[640,256]{1,0:T(8,128)(2,1)} %collective-permute-done.42), channel_id=1, source_target_pairs={{8,0},{9,1},{10,2},{11,3},{12,4},{13,5},{14,6},{15,7},{16,24},{17,... | collective-permute-start | bytes 983048 | tf_op jit(solution)/shard_map/ppermute | solution.py:85
  286.2 46.4 %collective-permute-start.18 = (f32[1024,256]{1,0:T(8,128)}, f32[1024,256]{1,0:T(8,128)S(1)}, u32[]{:S(2)}, u32[]{:S(2)}) collective-permute-start(f32[1024,256]{1,0:T(8,128)} %get-tuple-element.28), channel_id=1, source_target_pairs={{0,4},{1,5},{2,6},{3,7},{4,0},{5,1},{6,2},{7,3},{8,12},{9,13},{10,... | collective-permute-start | bytes 3145736 | tf_op jit(solution)/shard_map/ppermute | solution.py:85
  286.4 26.6 %collective-permute-start.35 = (bf16[640,256]{1,0:T(8,128)(2,1)S(1)}, bf16[640,256]{1,0:T(8,128)(2,1)}, u32[]{:S(2)}, u32[]{:S(2)}) collective-permute-start(bf16[640,256]{1,0:T(8,128)(2,1)S(1)} %collective-permute-done.34), channel_id=1, source_target_pairs={{8,16},{9,17},{10,18},{11,19},{12,20},{13,21},{14,22},{15,23},{16,... | collective-permute-start | bytes 983048 | tf_op jit(solution)/shard_map/ppermute | solution.py:85
  307.6 42.5 %collective-permute-start.17 = (f32[1024,256]{1,0:T(8,128)}, f32[1024,256]{1,0:T(8,128)}, u32[]{:S(2)}, u32[]{:S(2)}) collective-permute-start(f32[1024,256]{1,0:T(8,128)} %pad_maximum_fusion.14), channel_id=1, source_target_pairs={{0,4},{1,5},{2,6},{3,7},{4,0},{5,1},{6,2},{7,3},{8,12},{9,13},{10,... | collective-permute-start | bytes 3145736 | tf_op jit(solution)/shard_map/ppermute | solution.py:85
  309.5 37.9 %collective-permute-start.11 = (bf16[1024,384]{1,0:T(8,128)(2,1)}, bf16[1024,384]{1,0:T(8,128)(2,1)}, u32[]{:S(2)}, u32[]{:S(2)}) collective-permute-start(bf16[1024,384]{1,0:T(8,128)(2,1)} %attend.5), channel_id=1, source_target_pairs={{8,0},{9,1},{10,2},{11,3},{12,4},{13,5},{14,6},{15,7},{16,24},{17,... | collective-permute-start | bytes 2359304 | tf_op jit(solution)/shard_map/ppermute | solution.py:85
  331.2 29.8 %collective-permute-start.30 = (bf16[640,384]{1,0:T(8,128)(2,1)}, bf16[640,384]{1,0:T(8,128)(2,1)}, u32[]{:S(2)}, u32[]{:S(2)}) collective-permute-start(bf16[640,384]{1,0:T(8,128)(2,1)} %get-tuple-element.35), channel_id=1, source_target_pairs={{8,16},{9,17},{10,18},{11,19},{12,20},{13,21},{14,22},{15,23},{16,... | collective-permute-start | bytes 1474568 | tf_op jit(solution)/shard_map/ppermute | solution.py:85
  350.1 39.0 %collective-permute-start.12 = (bf16[1024,384]{1,0:T(8,128)(2,1)S(1)}, bf16[1024,384]{1,0:T(8,128)(2,1)S(1)}, u32[]{:S(2)}, u32[]{:S(2)}) collective-permute-start(bf16[1024,384]{1,0:T(8,128)(2,1)S(1)} %broadcast_select_fusion.refs_0_), channel_id=1, source_target_pairs={{0,2},{1,3},{2,0},{3,1},{4,6},{5,7},{6,4},{7,5},{8,10},{9,11},{10,... | collective-permute-start | bytes 2359304 | tf_op jit(solution)/shard_map/ppermute | solution.py:85
  356.8 20.4 %collective-permute-start.28 = (bf16[640,384]{1,0:T(8,128)(2,1)}, bf16[640,384]{1,0:T(8,128)(2,1)S(1)}, u32[]{:S(2)}, u32[]{:S(2)}) collective-permute-start(bf16[640,384]{1,0:T(8,128)(2,1)} %get-tuple-element.35), channel_id=1, source_target_pairs={{0,8},{1,9},{2,10},{3,11},{4,12},{5,13},{6,14},{7,15},{8,0},{9,1},... | collective-permute-start | bytes 1474568 | tf_op jit(solution)/shard_map/ppermute | solution.py:85
  361.7 26.0 %collective-permute-start.22 = (bf16[640,384]{1,0:T(8,128)(2,1)}, bf16[640,384]{1,0:T(8,128)(2,1)S(1)}, u32[]{:S(2)}, u32[]{:S(2)}) collective-permute-start(bf16[640,384]{1,0:T(8,128)(2,1)} %get-tuple-element.36), channel_id=1, source_target_pairs={{0,8},{1,9},{2,10},{3,11},{4,12},{5,13},{6,14},{7,15},{8,0},{9,1},... | collective-permute-start | bytes 1474568 | tf_op jit(solution)/shard_map/ppermute | solution.py:85
  366.7 23.9 %collective-permute-start.20 = (bf16[1024,256]{1,0:T(8,128)(2,1)S(1)}, bf16[1024,256]{1,0:T(8,128)(2,1)S(1)}, u32[]{:S(2)}, u32[]{:S(2)}) collective-permute-start(bf16[1024,256]{1,0:T(8,128)(2,1)S(1)} %broadcast_select_fusion.1.refs_4_), channel_id=1, source_target_pairs={{0,2},{1,3},{2,0},{3,1},{4,6},{5,7},{6,4},{7,5},{8,10},{9,11},{10,... | collective-permute-start | bytes 1572872 | tf_op jit(solution)/shard_map/ppermute | solution.py:85
  390.7 25.4 %collective-permute-start.13 = (bf16[2048,384]{1,0:T(8,128)(2,1)S(1)}, bf16[2048,384]{1,0:T(8,128)(2,1)S(1)}, u32[]{:S(2)}, u32[]{:S(2)}) collective-permute-start(bf16[2048,384]{1,0:T(8,128)(2,1)S(1)} %pad_maximum_fusion.7), channel_id=1, source_target_pairs={{0,1},{1,0},{2,3},{3,2},{4,5},{5,4},{6,7},{7,6},{8,9},{9,8},{10,11... | collective-permute-start | bytes 4718600 | tf_op jit(solution)/shard_map/ppermute | solution.py:85
  390.9 24.1 %collective-permute-start.21 = (bf16[2048,256]{1,0:T(8,128)(2,1)S(1)}, bf16[2048,256]{1,0:T(8,128)(2,1)S(1)}, u32[]{:S(2)}, u32[]{:S(2)}) collective-permute-start(bf16[2048,256]{1,0:T(8,128)(2,1)S(1)} %pad_maximum_fusion.15), channel_id=1, source_target_pairs={{0,1},{1,0},{2,3},{3,2},{4,5},{5,4},{6,7},{7,6},{8,9},{9,8},{10,11... | collective-permute-start | bytes 3145736 | tf_op jit(solution)/shard_map/ppermute | solution.py:85
  397.6 49.9 %collective-permute-start.26 = (bf16[640,384]{1,0:T(8,128)(2,1)}, bf16[640,384]{1,0:T(8,128)(2,1)}, u32[]{:S(2)}, u32[]{:S(2)}) collective-permute-start(bf16[640,384]{1,0:T(8,128)(2,1)} %collective-permute-done.23), channel_id=1, source_target_pairs={{8,0},{9,1},{10,2},{11,3},{12,4},{13,5},{14,6},{15,7},{16,24},{17,... | collective-permute-start | bytes 1474568 | tf_op jit(solution)/shard_map/ppermute | solution.py:85
  425.4 34.7 %collective-permute-start.45 = (f32[512,256]{1,0:T(8,128)}, f32[512,256]{1,0:T(8,128)}, u32[]{:S(2)}, u32[]{:S(2)}) collective-permute-start(f32[512,256]{1,0:T(8,128)} %slice.129), channel_id=1, source_target_pairs={{0,4},{1,5},{2,6},{3,7},{4,0},{5,1},{6,2},{7,3},{8,12},{9,13},{10,... | collective-permute-start | bytes 1572872 | tf_op jit(solution)/shard_map/ppermute | solution.py:85
  436.3 24.9 %collective-permute-start.39 = (f32[512,256]{1,0:T(8,128)}, f32[512,256]{1,0:T(8,128)}, u32[]{:S(2)}, u32[]{:S(2)}) collective-permute-start(f32[512,256]{1,0:T(8,128)} %slice.127), channel_id=1, source_target_pairs={{0,4},{1,5},{2,6},{3,7},{4,0},{5,1},{6,2},{7,3},{8,12},{9,13},{10,... | collective-permute-start | bytes 1572872 | tf_op jit(solution)/shard_map/ppermute | solution.py:85
  446.0 20.7 %collective-permute-start.33 = (f32[512,384]{1,0:T(8,128)S(1)}, f32[512,384]{1,0:T(8,128)}, u32[]{:S(2)}, u32[]{:S(2)}) collective-permute-start(f32[512,384]{1,0:T(8,128)S(1)} %slice.125), channel_id=1, source_target_pairs={{0,4},{1,5},{2,6},{3,7},{4,0},{5,1},{6,2},{7,3},{8,12},{9,13},{10,... | collective-permute-start | bytes 2359304 | tf_op jit(solution)/shard_map/ppermute | solution.py:85
  459.4 20.3 %collective-permute-start.27 = (f32[512,384]{1,0:T(8,128)S(1)}, f32[512,384]{1,0:T(8,128)S(1)}, u32[]{:S(2)}, u32[]{:S(2)}) collective-permute-start(f32[512,384]{1,0:T(8,128)S(1)} %slice.123), channel_id=1, source_target_pairs={{0,4},{1,5},{2,6},{3,7},{4,0},{5,1},{6,2},{7,3},{8,12},{9,13},{10,... | collective-permute-start | bytes 2359304 | tf_op jit(solution)/shard_map/ppermute | solution.py:85
  (56 other events, 962.1 us)

commit v2 on v0

--- a/solution.py
+++ b/solution.py
@@ -1,17 +1,24 @@
+import functools
+
 import jax
 import jax.numpy as jnp
 from jax import lax
+from jax.experimental import pallas as pl
+from jax.experimental.pallas import tpu as pltpu
 from jax.sharding import PartitionSpec as P
 
 HD = 128
 SPK = 2
+AXES = ("ctx", "head")
+QUERY_CHUNKS = (3, 2)
+OUT_CHUNKS = (6, 4)
 
 
 def add_rows(left_rows, shard_piece):
     return jnp.dot(left_rows, shard_piece, preferred_element_type=jnp.float32)
 
 
-def shards(video_rows, w_query, w_output, audio_tokens, w_key, w_value, row_lists, row_counts):
+def plain_shards(video_rows, w_query, w_output, audio_tokens, w_key, w_value, row_lists, row_counts):
     rows_dev = video_rows.shape[0]
     columns = w_query.shape[1]
     heads_dev = columns // HD
@@ -54,6 +61,267 @@
     return result.astype(jnp.bfloat16)
 
 
+def pairs(planes, move):
+    found = []
+    for z in range(planes):
+        for x in range(2):
+            for h in range(4):
+                to = move(z, x, h)
+                found.append(((2 * z + x) * 4 + h, (2 * to[0] + to[1]) * 4 + to[2]))
+    return found
+
+
+ACROSS_X = pairs(4, lambda z, x, h: (z, 1 - x, h))
+ACROSS_Y = pairs(4, lambda z, x, h: (z, x, h ^ 2))
+ACROSS_CORE = pairs(4, lambda z, x, h: (z, x, h ^ 1))
+ONE_ALONG = pairs(4, lambda z, x, h: (z ^ 1, x, h))
+TWO_ALONG = pairs(4, lambda z, x, h: (z ^ 2, x, h))
+SAME_X = [[0, 2, 4, 6], [1, 3, 5, 7]]
+
+
+def send(value, move):
+    return lax.ppermute(value, AXES, move)
+
+
+def along_z(value):
+    return lax.all_gather(value, "ctx", axis=0, axis_index_groups=SAME_X)
+
+
+def product(place, lefts, weights, k_sizes):
+    total = None
+    for j in range(4):
+        first = 0
+        for i, size in enumerate(k_sizes):
+            right = weights[place[j], first : first + size, :]
+            term = jnp.dot(lefts[i * 4 + j][...], right, preferred_element_type=jnp.float32)
+            total = term if total is None else total + term
+            first += size
+    return total
+
+
+def query_body(place, *refs):
+    own, near = refs[:4], refs[4:8]
+    weights, kept, sent = refs[8:]
+    half = kept.shape[1]
+
+    def write(lefts):
+        total = product(place, lefts, weights, (weights.shape[1],))
+        kept[...] = total[:, :half]
+        sent[...] = total[:, half:]
+
+    first_group = pl.program_id(0) < pl.num_programs(0) // 2
+    pl.when(first_group)(lambda: write(own))
+    pl.when(jnp.logical_not(first_group))(lambda: write(near))
+
+
+def query_product(place, video_rows, near, weights):
+    rows = video_rows.shape[0]
+    depth, columns = weights.shape[1:]
+    step = rows // 2
+    own_specs = [
+        pl.BlockSpec(
+            (step, depth),
+            functools.partial(lambda j, i, place: (jnp.minimum(i, 1), place[4 + j]), j),
+        )
+        for j in range(4)
+    ]
+    near_specs = [
+        pl.BlockSpec((step, depth), lambda i, place: (jnp.maximum(i - 2, 0), 0)) for _ in range(4)
+    ]
+    half = columns // 2
+    part = jax.ShapeDtypeStruct((2 * rows, half), jnp.float32)
+    return pl.pallas_call(
+        query_body,
+        grid_spec=pltpu.PrefetchScalarGridSpec(
+            num_scalar_prefetch=1,
+            grid=(4,),
+            in_specs=own_specs
+            + near_specs
+            + [pl.BlockSpec(weights.shape, lambda i, place: (0, 0, 0))],
+            out_specs=[pl.BlockSpec((step, half), lambda i, place: (i, 0))] * 2,
+        ),
+        out_shape=[part, part],
+        cost_estimate=pl.CostEstimate(
+            flops=16 * rows * depth * columns,
+            transcendentals=0,
+            bytes_accessed=8 * (2 * rows + columns) * depth + 8 * rows * columns,
+        ),
+        name="query_product",
+    )(place, *([video_rows] * 4), *near, weights)
+
+
+def out_body(place, *refs, k_sizes):
+    *lefts, weights, kept, sent = refs
+    total = product(place, lefts, weights, k_sizes)
+    pl.when(pl.program_id(0) < 2)(lambda: kept.__setitem__(..., total))
+    pl.when(pl.program_id(0) >= 2)(lambda: sent.__setitem__(..., total))
+
+
+def out_product(place, lefts, weights, k_sizes):
+    rows = lefts[0].shape[0]
+    columns = weights.shape[2]
+    step = rows // 4
+    left_specs = [
+        pl.BlockSpec((step, size), lambda i, place: (i, 0)) for size in k_sizes for _ in range(4)
+    ]
+    part = jax.ShapeDtypeStruct((rows // 2, columns), jnp.float32)
+    return pl.pallas_call(
+        functools.partial(out_body, k_sizes=k_sizes),
+        grid_spec=pltpu.PrefetchScalarGridSpec(
+            num_scalar_prefetch=1,
+            grid=(4,),
+            in_specs=left_specs + [pl.BlockSpec(weights.shape, lambda i, place: (0, 0, 0))],
+            out_specs=[
+                pl.BlockSpec((step, columns), lambda i, place: (jnp.minimum(i, 1), 0)),
+                pl.BlockSpec((step, columns), lambda i, place: (jnp.maximum(i - 2, 0), 0)),
+            ],
+        ),
+        out_shape=[part, part],
+        cost_estimate=pl.CostEstimate(
+            flops=8 * rows * sum(k_sizes) * columns,
+            transcendentals=0,
+            bytes_accessed=8 * (rows + columns) * sum(k_sizes) + 4 * rows * columns,
+        ),
+        name="out_product",
+    )(place, *lefts, weights)
+
+
+def attend_body(kept, received, keys, values, speaker, attended, *, audio_length, heads):
+    scale = 1.0 / HD**0.5
+    of_row = speaker[...]
+    lane = lax.broadcasted_iota(jnp.int32, (kept.shape[0], SPK * audio_length), 1)
+    of_key = jnp.where(lane < audio_length, 1, 2)
+    own_key = of_key == of_row
+    live = of_row > 0
+    for head in range(heads):
+        at = slice(head * HD, (head + 1) * HD)
+        query = (kept[:, at] + received[:, at]).astype(jnp.bfloat16)
+        scores = (
+            lax.dot_general(
+                query, keys[:, at], (((1,), (1,)), ((), ())), preferred_element_type=jnp.float32
+            )
+            * scale
+        )
+        scores = jnp.where(own_key, scores, -1e30)
+        scores = scores - jnp.max(scores, axis=-1, keepdims=True)
+        weights = jnp.exp(scores)
+        weights = (weights / jnp.sum(weights, axis=-1, keepdims=True)).astype(jnp.bfloat16)
+        blended = jnp.dot(weights, values[:, at], preferred_element_type=jnp.float32)
+        attended[:, at] = jnp.where(live, blended, 0.0).astype(jnp.bfloat16)
+
+
+def attend(kept, received, keys, values, speaker, audio_length):
+    rows, columns = kept.shape
+    step = rows // 4
+    at = lambda i: (i, 0)
+    whole = pl.BlockSpec(keys.shape, lambda i: (0, 0))
+    return pl.pallas_call(
+        functools.partial(attend_body, audio_length=audio_length, heads=columns // HD),
+        grid=(4,),
+        in_specs=[
+            pl.BlockSpec((step, columns), at),
+            pl.BlockSpec((step, columns), lambda i: ((i + 2) % 4, 0)),
+            whole,
+            whole,
+            pl.BlockSpec((step, 1), at),
+        ],
+        out_specs=pl.BlockSpec((step, columns), at),
+        out_shape=jax.ShapeDtypeStruct((rows, columns), jnp.bfloat16),
+        cost_estimate=pl.CostEstimate(
+            flops=4 * rows * columns * SPK * audio_length,
+            transcendentals=rows * SPK * audio_length * columns // HD,
+            bytes_accessed=10 * rows * columns,
+        ),
+        name="attend",
+    )(kept, received, keys, values, speaker)
+
+
+def head_pieces(value):
+    over_y = send(value, ACROSS_Y)
+    return [value, send(value, ACROSS_CORE), over_y, send(over_y, ACROSS_CORE)]
+
+
+def plane_shards(video_rows, w_query, w_output, audio_tokens, w_key, w_value, row_lists, row_counts):
+    rows = video_rows.shape[0]
+    block = w_query.shape[0]
+    audio_width = audio_tokens.shape[2]
+    ctx = lax.axis_index("ctx").astype(jnp.int32)
+    h = lax.axis_index("head").astype(jnp.int32)
+    x = ctx % 2
+    k_sizes = tuple(heads * HD for heads in QUERY_CHUNKS)
+
+    query_weights = []
+    first = 0
+    for size in k_sizes:
+        query_weights.append(
+            along_z(
+                jnp.concatenate(
+                    [
+                        lax.dynamic_slice(w_query, (0, x * block + first), (block, size)),
+                        lax.dynamic_slice(w_query, (0, (1 - x) * block + first), (block, size)),
+                    ],
+                    axis=1,
+                )
+            )
+        )
+        first += size
+
+    near = head_pieces(
+        send(
+            lax.dynamic_slice(video_rows, (0, (2 * h + 1 - x) * block), (rows, block)), ACROSS_X
+        )
+    )
+    order = jnp.arange(4, dtype=jnp.int32) ^ h
+    place = jnp.concatenate([order, 2 * order + x])
+
+    position = jnp.arange(rows, dtype=jnp.int32)
+    named = (row_lists[:, :, None] == position[None, None, :]) & (
+        position[None, :, None] < row_counts[:, :, None]
+    )
+    speaker_of = jnp.sum(
+        jnp.any(named, axis=1) * jnp.array([[1], [2]], jnp.int32), axis=0
+    ).astype(jnp.bfloat16)
+    tokens = audio_tokens.shape[1]
+    gathered = jnp.concatenate([audio_tokens.reshape(-1), speaker_of])[None]
+    for move in (ACROSS_X, ONE_ALONG, TWO_ALONG):
+        gathered = jnp.concatenate([gathered, send(gathered, move)], axis=0)
+    whole_audio = (
+        gathered[:, : SPK * tokens * audio_width]
+        .reshape(-1, SPK, tokens, audio_width)
+        .transpose(1, 0, 2, 3)
+        .reshape(-1, audio_width)
+    )
+    audio_length = whole_audio.shape[0] // SPK
+    speaker = gathered[:2, SPK * tokens * audio_width :].astype(jnp.int32).reshape(-1, 1)
+    key_rows = add_rows(
+        whole_audio, lax.dynamic_slice(w_key, (0, x * block), (audio_width, block))
+    ).astype(jnp.bfloat16)
+    value_rows = add_rows(
+        whole_audio, lax.dynamic_slice(w_value, (0, x * block), (audio_width, block))
+    ).astype(jnp.bfloat16)
+
+    attended = []
+    first = 0
+    for weights, size in zip(query_weights, k_sizes):
+        at = slice(first, first + size)
+        kept, sent = query_product(place, video_rows, near, weights)
+        received = send(sent, ACROSS_X)
+        attended += head_pieces(
+            attend(kept, received, key_rows[:, at], value_rows[:, at], speaker, audio_length)
+        )
+        first += size
+
+    results = []
+    first = 0
+    for heads in OUT_CHUNKS:
+        size = heads * HD
+        weights = along_z(lax.slice_in_dim(w_output, first, first + size, axis=1))
+        kept, sent = out_product(place, attended, weights, k_sizes)
+        results.append((kept + send(sent, ACROSS_X)).astype(jnp.bfloat16))
+        first += size
+    return jnp.concatenate(results, axis=1)
+
+
 def solution(mesh):
     in_specs = (
         P("ctx", None),
@@ -66,4 +334,6 @@
         P(None, "ctx"),
     )
     out_specs = P("ctx", "head")
+    planes = mesh.shape["ctx"] == 8 and mesh.shape["head"] == 4
+    shards = plane_shards if planes else plain_shards
     return jax.shard_map(shards, mesh=mesh, in_specs=in_specs, out_specs=out_specs, check_vma=False)

time: 439 us -> 322 us (0.73)
  waiting for transfers between devices: 323 us -> 210 us
  Pallas kernels: 0 us -> 50.1 us
  blocking collectives: 32.9 us -> 0 us
  matrix products: 34.7 us -> 2.75 us
  starting transfers between devices: 0.08 us -> 18.9 us
  other arithmetic: 21.6 us -> 9.07 us
    all_gather x3 -> x4, waiting for transfers between devices: 321 us -> 143 us  [along_z(): return lax.all_gather(value, 'ctx', axis=0, axis_index_groups=SAME_X)]
    ppermute x0 -> x17, waiting for transfers between devices: none -> 66.7 us  [send(): return lax.ppermute(value, AXES, move)]
    pallas_call x0 -> x6, Pallas kernels: none -> 50.1 us  [the longest x2 19.6 us: out_product(): pl.pallas_call(functools.partial(out_body, k_sizes=k_sizes), grid_spec=pl...]
    all_gather x1 -> x0, blocking collectives: 32.9 us -> none  [shards(): whole_audio = lax.all_gather(audio_tokens, 'ctx', axis=1, tiled=True)]
    dot_general x2, matrix products: 26.2 us -> 2.75 us  [add_rows(): return jnp.dot(left_rows, shard_piece, preferred_element_type=jnp.float32)]
    ppermute x0 -> x17, starting transfers between devices: none -> 18.8 us  [send(): return lax.ppermute(value, AXES, move)]
    scatter-add x2 -> x0, other arithmetic: 17 us -> none  [shards(): summed = summed.at[target].add(blended)]
    dot_general x6 -> x0, matrix products: 8.43 us -> none  [the longest x2 4.04 us: shards(): jnp.einsum('hrk,khd->rhd', weights, value_block, preferred_element_type=j...]
  transfers between devices with their start and end apart: 3 -> 21, of which waited for: 3 -> 10; matrix products, arithmetic and copies ran while one was open for 13% -> 7% of each run, Pallas kernels for 0% -> 16%
where the time goes in v2:
time: 322 us; the launch traced here: 321 us
  waiting for transfers between devices  210 us (65%)
  Pallas kernels  50.1 us (16%)
  starting transfers between devices  18.9 us (6%)
  local copies, waits for them, and re-layouts  16.5 us (5%)
  between operations  13.4 us (4%)
  other arithmetic  9.07 us (3%)
    all_gather x4, waiting for transfers between devices, along_z(): return lax.all_gather(value, 'ctx', axis=0, axis_index_groups=SAME_X)  143 us
    ppermute x17, waiting for transfers between devices, send(): return lax.ppermute(value, AXES, move)  66.7 us
    pallas_call x2, Pallas kernels, out_product(): pl.pallas_call(functools.partial(out_body, k_sizes=k_sizes), grid_spec=pl...  19.6 us
    pallas_call x2, Pallas kernels, query_product(): pl.pallas_call(query_body, grid_spec=pltpu.PrefetchScalarGridSpec(num_sca...  19.5 us
    ppermute x17, starting transfers between devices, send(): return lax.ppermute(value, AXES, move)  18.8 us
    pallas_call x2, Pallas kernels, attend(): pl.pallas_call(functools.partial(attend_body, audio_length=audio_length,...  11 us
  transfers between devices with their start and end apart: 21, of which 10 were waited for; matrix products, arithmetic and copies ran while one was open for 7% of the time, Pallas kernels for 16%

profile of v2, /device:TPU:0, one launch (start us, length us, event | category | flops | bytes accessed | tf_op | source)
XLA Modules:
  0.0 320.9 jit_solution(2035780133409779176)
XLA Ops:
  11.2 2.2 slice.30
  14.7 3.0 collective-permute-start
  17.7 14.7 %collective-permute-done.refs_4_ = bf16[512,640]{1,0:T(8,128)(2,1)S(1)} collective-permute-done((bf16[512,640]{1,0:T(8,128)(2,1)S(1)}, bf16[512,640]{1,0:T(8,128)(2,1)S(1)}, u32[]{:S(2)}, u32[]{:S(2)}) %collective-permute-start) | collective-permute-done | bytes 655392 | tf_op jit(solution)/shard_map/ppermute | solution.py:83
  32.4 1.8 collective-permute-start.2
  34.9 1.6 collective-permute-start.5
  36.4 2.0 slice.31
  39.1 9.4 %collective-permute-done.2.refs_6_ = bf16[512,640]{1,0:T(8,128)(2,1)S(1)} collective-permute-done((bf16[512,640]{1,0:T(8,128)(2,1)S(1)}, bf16[512,640]{1,0:T(8,128)(2,1)S(1)}, u32[]{:S(2)}, u32[]{:S(2)}) %collective-permute-start.2) | collective-permute-done | bytes 655392 | tf_op jit(solution)/shard_map/ppermute | solution.py:83
  49.2 1.5 collective-permute-start.6
  51.8 36.5 %all-gather.9.cloned.1.call-done = bf16[2560,768]{1,0:T(8,128)(2,1)} async-done(((bf16[640,768]{1,0:T(8,128)(2,1)}), bf16[2560,768]{1,0:T(8,128)(2,1)}) %all-gather.9.cloned.1.call-update) | async-done | bytes 3932176 | tf_op jit(solution)/shard_map/all_gather | solution.py:87
  88.3 10.7 %query_product.2 = (f32[1024,384]{1,0:T(8,128)}, f32[1024,384]{1,0:T(8,128)}) custom-call(s32[8]{0:T(128)} %pad_add_fusion.place, bf16[512,5120]{1,0:T(8,128)(2,1)} %refs_3_.3, bf16[512,5120]{1,0:T(8,128)(2,1)} %refs_3_.3, bf16[512,5120]{1,0:T(8,128)(2,1)} %refs_3_.3, bf16[512,5120]{1,0:T(8,128)(2,1)} %refs_3_.3, bf16[512,640]{1,0:T(8,128)(2,1)} %copy-done.1, ...), custom_call_target="tpu_custom_call" | custom-call | flops 4026531840 | bytes 12320768 | tf_op jit(solution)/shard_map/query_product/pallas_call | solution.py:133
  99.0 1.6 collective-permute-start.4
  100.6 1.5 pad_maximum_fusion.6
  102.0 1.5 collective-permute-start.7
  103.5 42.6 %all-gather.11.cloned.1.call-done = bf16[2560,512]{1,0:T(8,128)(2,1)} async-done(((bf16[640,512]{1,0:T(8,128)(2,1)}), bf16[2560,512]{1,0:T(8,128)(2,1)}) %all-gather.11.cloned.1.call-update) | async-done | bytes 2621456 | tf_op jit(solution)/shard_map/all_gather | solution.py:87
  146.1 8.9 %query_product.3 = (f32[1024,256]{1,0:T(8,128)}, f32[1024,256]{1,0:T(8,128)}) custom-call(s32[8]{0:T(128)} %pad_add_fusion.place, bf16[512,5120]{1,0:T(8,128)(2,1)} %refs_3_.3, bf16[512,5120]{1,0:T(8,128)(2,1)} %refs_3_.3, bf16[512,5120]{1,0:T(8,128)(2,1)} %refs_3_.3, bf16[512,5120]{1,0:T(8,128)(2,1)} %refs_3_.3, bf16[512,640]{1,0:T(8,128)(2,1)} %copy-done.1, ...), custom_call_target="tpu_custom_call" | custom-call | flops 2684354560 | bytes 9961472 | tf_op jit(solution)/shard_map/query_product/pallas_call | solution.py:133
  155.0 1.4 collective-permute-start.11
  158.0 1.5 reshape.44
  161.4 1.6 convolution_convert_fusion
  164.9 5.7 %attend.2.refs_0_ = bf16[1024,384]{1,0:T(8,128)(2,1)} custom-call(f32[1024,384]{1,0:T(8,128)} %get-tuple-element.13.kept, f32[1024,384]{1,0:T(8,128)} %copy-done.3, bf16[64,384]{1,0:T(8,128)(2,1)} %slice.32.keys, bf16[64,384]{1,0:T(8,128)(2,1)} %slice.33.values, s32[1024,1]{1,0:T(8,128)} %bitcast.16), custom_call_target="tpu_custom_call" | custom-call | flops 100663296 | bytes 3932160 | tf_op jit(solution)/shard_map/attend/pallas_call | solution.py:218
  170.5 1.5 collective-permute-start.9
  174.7 5.4 %collective-permute-done.11.received = f32[1024,256]{1,0:T(8,128)} collective-permute-done((f32[1024,256]{1,0:T(8,128)}, f32[1024,256]{1,0:T(8,128)}, u32[]{:S(2)}, u32[]{:S(2)}) %collective-permute-start.11) | collective-permute-done | bytes 1048608 | tf_op jit(solution)/shard_map/ppermute | solution.py:83
  180.1 5.3 %attend.3.refs_4_ = bf16[1024,256]{1,0:T(8,128)(2,1)} custom-call(f32[1024,256]{1,0:T(8,128)} %get-tuple-element.15.kept, f32[1024,256]{1,0:T(8,128)} %collective-permute-done.11.received, bf16[64,256]{1,0:T(8,128)(2,1)} %slice.36.keys, bf16[64,256]{1,0:T(8,128)(2,1)} %slice.37.values, s32[1024,1]{1,0:T(8,128)} %bitcast.17), custom_call_target="tpu_custom_call" | custom-call | flops 67108864 | bytes 2621440 | tf_op jit(solution)/shard_map/attend/pallas_call | solution.py:218
  185.4 1.5 collective-permute-start.13
  186.9 4.4 %collective-permute-done.9.refs_2_ = bf16[1024,384]{1,0:T(8,128)(2,1)S(1)} collective-permute-done((bf16[1024,384]{1,0:T(8,128)(2,1)}, bf16[1024,384]{1,0:T(8,128)(2,1)S(1)}, u32[]{:S(2)}, u32[]{:S(2)}) %collective-permute-start.9) | collective-permute-done | bytes 786464 | tf_op jit(solution)/shard_map/ppermute | solution.py:83
  191.7 9.3 %collective-permute-done.13.refs_6_ = bf16[1024,256]{1,0:T(8,128)(2,1)} collective-permute-done((bf16[1024,256]{1,0:T(8,128)(2,1)}, bf16[1024,256]{1,0:T(8,128)(2,1)}, u32[]{:S(2)}, u32[]{:S(2)}) %collective-permute-start.13) | collective-permute-done | bytes 524320 | tf_op jit(solution)/shard_map/ppermute | solution.py:83
  201.0 21.8 %all-gather.13.cloned.1.call-done = bf16[2560,768]{1,0:T(8,128)(2,1)} async-done(((bf16[640,768]{1,0:T(8,128)(2,1)}), bf16[2560,768]{1,0:T(8,128)(2,1)}) %all-gather.13.cloned.1.call-update) | async-done | bytes 3932176 | tf_op jit(solution)/shard_map/all_gather | solution.py:87
  222.8 10.8 %out_product.2 = (f32[512,768]{1,0:T(8,128)}, f32[512,768]{1,0:T(8,128)}) custom-call(s32[8]{0:T(128)} %pad_add_fusion.place, bf16[1024,384]{1,0:T(8,128)(2,1)} %attend.2.refs_0_, bf16[1024,384]{1,0:T(8,128)(2,1)} %collective-permute-done.8.refs_1_, bf16[1024,384]{1,0:T(8,128)(2,1)} %copy-done.14, bf16[1024,384]{1,0:T(8,128)(2,1)} %collective-permute-done.10.refs_3_, ...), custom_call_target="tpu_custom_call" | custom-call | flops 4026531840 | bytes 12320768 | tf_op jit(solution)/shard_map/out_product/pallas_call | solution.py:168
  233.6 1.4 collective-permute-start.15
  235.1 42.6 %all-gather.15.cloned.1.call-done = bf16[2560,512]{1,0:T(8,128)(2,1)} async-done(((bf16[640,512]{1,0:T(8,128)(2,1)}), bf16[2560,512]{1,0:T(8,128)(2,1)}) %all-gather.15.cloned.1.call-update) | async-done | bytes 2621456 | tf_op jit(solution)/shard_map/all_gather | solution.py:87
  277.6 8.8 %out_product.3 = (f32[512,512]{1,0:T(8,128)}, f32[512,512]{1,0:T(8,128)}) custom-call(s32[8]{0:T(128)} %pad_add_fusion.place, bf16[1024,384]{1,0:T(8,128)(2,1)} %attend.2.refs_0_, bf16[1024,384]{1,0:T(8,128)(2,1)} %collective-permute-done.8.refs_1_, bf16[1024,384]{1,0:T(8,128)(2,1)} %copy-done.14, bf16[1024,384]{1,0:T(8,128)(2,1)} %collective-permute-done.10.refs_3_, ...), custom_call_target="tpu_custom_call" | custom-call | flops 2684354560 | bytes 9961472 | tf_op jit(solution)/shard_map/out_product/pallas_call | solution.py:168
  286.5 1.5 collective-permute-start.16
  288.0 23.6 %collective-permute-done.16 = f32[512,512]{1,0:T(8,128)S(1)} collective-permute-done((f32[512,512]{1,0:T(8,128)}, f32[512,512]{1,0:T(8,128)S(1)}, u32[]{:S(2)}, u32[]{:S(2)}) %collective-permute-start.16) | collective-permute-done | bytes 1048608 | tf_op jit(solution)/shard_map/ppermute | solution.py:83
  (83 shorter events, 20.2 us)
Async XLA Ops:
  6.5 153.0 %copy-start = (bf16[768,1280]{1,0:T(8,128)(2,1)S(1)}, bf16[768,1280]{1,0:T(8,128)(2,1)}, u32[]{:S(2)}) copy-start(bf16[768,1280]{1,0:T(8,128)(2,1)} %param.13) | copy-start | bytes 5898244
  6.5 81.8 %all-gather.9.cloned.1.call-start = ((), (), s32[]{:S(2)}) async-start(), calls=%async_computation | async-start | bytes 4915200 | tf_op jit(solution)/shard_map/all_gather | solution.py:87
  9.0 137.1 %all-gather.11.cloned.1.call-start = ((), (), s32[]{:S(2)}) async-start(), calls=%async_computation.1 | async-start | bytes 3276800 | tf_op jit(solution)/shard_map/all_gather | solution.py:87
  11.1 23.1 %copy-start.12 = (s32[2,1]{0,1:T(1,128)S(1)}, s32[2,1]{0,1:T(1,128)}, u32[]{:S(2)}) copy-start(s32[2,1]{0,1:T(1,128)} %param.16) | copy-start | bytes 28
  11.1 23.1 %copy-start.10 = (bf16[2,4,768]{2,1,0:T(4,128)(2,1)S(1)}, bf16[2,4,768]{2,1,0:T(4,128)(2,1)}, u32[]{:S(2)}) copy-start(bf16[2,4,768]{2,1,0:T(4,128)(2,1)} %param.12) | copy-start | bytes 36868
  11.1 23.1 %copy-start.11 = (s32[2,512]{1,0:T(2,128)S(1)}, s32[2,512]{1,0:T(2,128)}, u32[]{:S(2)}) copy-start(s32[2,512]{1,0:T(2,128)} %param.15) | copy-start | bytes 12292
  11.1 23.6 %copy-start.13 = (s32[2]{0:T(128)S(1)}, s32[2]{0:T(128)}, u32[]{:S(2)}) copy-start(s32[2]{0:T(128)} %constant.44) | copy-start | bytes 28
  11.2 211.6 %all-gather.13.cloned.1.call-start = ((), (), s32[]{:S(2)}) async-start(), calls=%async_computation.2 | async-start | bytes 4915200 | tf_op jit(solution)/shard_map/all_gather | solution.py:87
  13.4 264.2 %all-gather.15.cloned.1.call-start = ((), (), s32[]{:S(2)}) async-start(), calls=%async_computation.3 | async-start | bytes 3276800 | tf_op jit(solution)/shard_map/all_gather | solution.py:87
  14.7 17.7 %collective-permute-start = (bf16[512,640]{1,0:T(8,128)(2,1)S(1)}, bf16[512,640]{1,0:T(8,128)(2,1)S(1)}, u32[]{:S(2)}, u32[]{:S(2)}) collective-permute-start(bf16[512,640]{1,0:T(8,128)(2,1)S(1)} %constant_dynamic-slice_fusion.4), channel_id=1, source_target_pairs={{0,4},{1,5},{2,6},{3,7},{4,0},{5,1},{6,2},{7,3},{8,12},{9,13},{10,... | collective-permute-start | bytes 1966088 | tf_op jit(solution)/shard_map/ppermute | solution.py:83
  32.4 55.9 %copy-start.1 = (bf16[512,640]{1,0:T(8,128)(2,1)}, bf16[512,640]{1,0:T(8,128)(2,1)S(1)}, u32[]{:S(2)}) copy-start(bf16[512,640]{1,0:T(8,128)(2,1)S(1)} %collective-permute-done.refs_4_) | copy-start | bytes 1966084
  32.4 16.0 %collective-permute-start.2 = (bf16[512,640]{1,0:T(8,128)(2,1)S(1)}, bf16[512,640]{1,0:T(8,128)(2,1)S(1)}, u32[]{:S(2)}, u32[]{:S(2)}) collective-permute-start(bf16[512,640]{1,0:T(8,128)(2,1)S(1)} %collective-permute-done.refs_4_), channel_id=1, source_target_pairs={{0,2},{1,3},{2,0},{3,1},{4,6},{5,7},{6,4},{7,5},{8,10},{9,11},{10,... | collective-permute-start | bytes 1966088 | tf_op jit(solution)/shard_map/ppermute | solution.py:83
  34.9 64.1 %copy-start.6 = (bf16[1,6656]{1,0:T(2,128)(2,1)}, bf16[1,6656]{1,0:T(2,128)(2,1)S(1)}, u32[]{:S(2)}) copy-start(bf16[1,6656]{1,0:T(2,128)(2,1)S(1)} %broadcast_in_dim.2) | copy-start | bytes 39940
  34.9 13.6 %collective-permute-start.5 = (bf16[1,6656]{1,0:T(2,128)(2,1)S(1)}, bf16[1,6656]{1,0:T(2,128)(2,1)S(1)}, u32[]{:S(2)}, u32[]{:S(2)}) collective-permute-start(bf16[1,6656]{1,0:T(2,128)(2,1)S(1)} %broadcast_in_dim.2), channel_id=1, source_target_pairs={{0,4},{1,5},{2,6},{3,7},{4,0},{5,1},{6,2},{7,3},{8,12},{9,13},{10,... | collective-permute-start | bytes 39944 | tf_op jit(solution)/shard_map/ppermute | solution.py:83
  39.1 12.8 %collective-permute-start.1 = (bf16[512,640]{1,0:T(8,128)(2,1)S(1)}, bf16[512,640]{1,0:T(8,128)(2,1)}, u32[]{:S(2)}, u32[]{:S(2)}) collective-permute-start(bf16[512,640]{1,0:T(8,128)(2,1)S(1)} %collective-permute-done.refs_4_), channel_id=1, source_target_pairs={{0,1},{1,0},{2,3},{3,2},{4,5},{5,4},{6,7},{7,6},{8,9},{9,8},{10,11... | collective-permute-start | bytes 1966088 | tf_op jit(solution)/shard_map/ppermute | solution.py:83
  48.4 39.9 %copy-start.2 = (bf16[512,640]{1,0:T(8,128)(2,1)}, bf16[512,640]{1,0:T(8,128)(2,1)S(1)}, u32[]{:S(2)}) copy-start(bf16[512,640]{1,0:T(8,128)(2,1)S(1)} %collective-permute-done.2.refs_6_) | copy-start | bytes 1966084
  48.4 3.4 %collective-permute-start.3 = (bf16[512,640]{1,0:T(8,128)(2,1)S(1)}, bf16[512,640]{1,0:T(8,128)(2,1)}, u32[]{:S(2)}, u32[]{:S(2)}) collective-permute-start(bf16[512,640]{1,0:T(8,128)(2,1)S(1)} %collective-permute-done.2.refs_6_), channel_id=1, source_target_pairs={{0,1},{1,0},{2,3},{3,2},{4,5},{5,4},{6,7},{7,6},{8,9},{9,8},{10,11... | collective-permute-start | bytes 1966088 | tf_op jit(solution)/shard_map/ppermute | solution.py:83
  48.4 50.5 %copy-start.7 = (bf16[1,6656]{1,0:T(2,128)(2,1)}, bf16[1,6656]{1,0:T(2,128)(2,1)S(1)}, u32[]{:S(2)}) copy-start(bf16[1,6656]{1,0:T(2,128)(2,1)S(1)} %collective-permute-done.5) | copy-start | bytes 39940
  49.2 51.3 %collective-permute-start.6 = (bf16[2,6656]{1,0:T(2,128)(2,1)}, bf16[2,6656]{1,0:T(2,128)(2,1)}, u32[]{:S(2)}, u32[]{:S(2)}) collective-permute-start(bf16[2,6656]{1,0:T(2,128)(2,1)} %pad_maximum_fusion.8), channel_id=1, source_target_pairs={{0,8},{1,9},{2,10},{3,11},{4,12},{5,13},{6,14},{7,15},{8,0},{9,1},... | collective-permute-start | bytes 79880 | tf_op jit(solution)/shard_map/ppermute | solution.py:83
  99.0 64.7 %collective-permute-start.4 = (f32[1024,384]{1,0:T(8,128)}, f32[1024,384]{1,0:T(8,128)S(1)}, u32[]{:S(2)}, u32[]{:S(2)}) collective-permute-start(f32[1024,384]{1,0:T(8,128)} %get-tuple-element.14), channel_id=1, source_target_pairs={{0,4},{1,5},{2,6},{3,7},{4,0},{5,1},{6,2},{7,3},{8,12},{9,13},{10,... | collective-permute-start | bytes 4718600 | tf_op jit(solution)/shard_map/ppermute | solution.py:83
  102.0 54.4 %collective-permute-start.7 = (bf16[4,6656]{1,0:T(4,128)(2,1)}, bf16[4,6656]{1,0:T(4,128)(2,1)}, u32[]{:S(2)}, u32[]{:S(2)}) collective-permute-start(bf16[4,6656]{1,0:T(4,128)(2,1)} %pad_maximum_fusion.6), channel_id=1, source_target_pairs={{0,16},{1,17},{2,18},{3,19},{4,20},{5,21},{6,22},{7,23},{8,24},{9,... | collective-permute-start | bytes 159752 | tf_op jit(solution)/shard_map/ppermute | solution.py:83
  155.0 25.1 %collective-permute-start.11 = (f32[1024,256]{1,0:T(8,128)}, f32[1024,256]{1,0:T(8,128)}, u32[]{:S(2)}, u32[]{:S(2)}) collective-permute-start(f32[1024,256]{1,0:T(8,128)} %get-tuple-element.16), channel_id=1, source_target_pairs={{0,4},{1,5},{2,6},{3,7},{4,0},{5,1},{6,2},{7,3},{8,12},{9,13},{10,... | collective-permute-start | bytes 3145736 | tf_op jit(solution)/shard_map/ppermute | solution.py:83
  170.5 20.7 %collective-permute-start.9 = (bf16[1024,384]{1,0:T(8,128)(2,1)}, bf16[1024,384]{1,0:T(8,128)(2,1)S(1)}, u32[]{:S(2)}, u32[]{:S(2)}) collective-permute-start(bf16[1024,384]{1,0:T(8,128)(2,1)} %attend.2.refs_0_), channel_id=1, source_target_pairs={{0,2},{1,3},{2,0},{3,1},{4,6},{5,7},{6,4},{7,5},{8,10},{9,11},{10,... | collective-permute-start | bytes 2359304 | tf_op jit(solution)/shard_map/ppermute | solution.py:83
  185.4 15.7 %collective-permute-start.13 = (bf16[1024,256]{1,0:T(8,128)(2,1)}, bf16[1024,256]{1,0:T(8,128)(2,1)}, u32[]{:S(2)}, u32[]{:S(2)}) collective-permute-start(bf16[1024,256]{1,0:T(8,128)(2,1)} %attend.3.refs_4_), channel_id=1, source_target_pairs={{0,2},{1,3},{2,0},{3,1},{4,6},{5,7},{6,4},{7,5},{8,10},{9,11},{10,... | collective-permute-start | bytes 1572872 | tf_op jit(solution)/shard_map/ppermute | solution.py:83
  186.9 36.0 %collective-permute-start.8 = (bf16[1024,384]{1,0:T(8,128)(2,1)S(1)}, bf16[1024,384]{1,0:T(8,128)(2,1)}, u32[]{:S(2)}, u32[]{:S(2)}) collective-permute-start(bf16[1024,384]{1,0:T(8,128)(2,1)S(1)} %copy-done.5), channel_id=1, source_target_pairs={{0,1},{1,0},{2,3},{3,2},{4,5},{5,4},{6,7},{7,6},{8,9},{9,8},{10,11... | collective-permute-start | bytes 2359304 | tf_op jit(solution)/shard_map/ppermute | solution.py:83
  191.2 31.6 %copy-start.14 = (bf16[1024,384]{1,0:T(8,128)(2,1)}, bf16[1024,384]{1,0:T(8,128)(2,1)S(1)}, u32[]{:S(2)}) copy-start(bf16[1024,384]{1,0:T(8,128)(2,1)S(1)} %collective-permute-done.9.refs_2_) | copy-start | bytes 2359300
  191.2 31.6 %collective-permute-start.10 = (bf16[1024,384]{1,0:T(8,128)(2,1)S(1)}, bf16[1024,384]{1,0:T(8,128)(2,1)}, u32[]{:S(2)}, u32[]{:S(2)}) collective-permute-start(bf16[1024,384]{1,0:T(8,128)(2,1)S(1)} %collective-permute-done.9.refs_2_), channel_id=1, source_target_pairs={{0,1},{1,0},{2,3},{3,2},{4,5},{5,4},{6,7},{7,6},{8,9},{9,8},{10,11... | collective-permute-start | bytes 2359304 | tf_op jit(solution)/shard_map/ppermute | solution.py:83
  191.2 9.8 %collective-permute-start.12 = (bf16[1024,256]{1,0:T(8,128)(2,1)}, bf16[1024,256]{1,0:T(8,128)(2,1)}, u32[]{:S(2)}, u32[]{:S(2)}) collective-permute-start(bf16[1024,256]{1,0:T(8,128)(2,1)} %attend.3.refs_4_), channel_id=1, source_target_pairs={{0,1},{1,0},{2,3},{3,2},{4,5},{5,4},{6,7},{7,6},{8,9},{9,8},{10,11... | collective-permute-start | bytes 1572872 | tf_op jit(solution)/shard_map/ppermute | solution.py:83
  201.0 21.8 %collective-permute-start.14 = (bf16[1024,256]{1,0:T(8,128)(2,1)}, bf16[1024,256]{1,0:T(8,128)(2,1)}, u32[]{:S(2)}, u32[]{:S(2)}) collective-permute-start(bf16[1024,256]{1,0:T(8,128)(2,1)} %collective-permute-done.13.refs_6_), channel_id=1, source_target_pairs={{0,1},{1,0},{2,3},{3,2},{4,5},{5,4},{6,7},{7,6},{8,9},{9,8},{10,11... | collective-permute-start | bytes 1572872 | tf_op jit(solution)/shard_map/ppermute | solution.py:83
  233.6 79.3 %collective-permute-start.15 = (f32[512,768]{1,0:T(8,128)}, f32[512,768]{1,0:T(8,128)S(1)}, u32[]{:S(2)}, u32[]{:S(2)}) collective-permute-start(f32[512,768]{1,0:T(8,128)} %get-tuple-element.18), channel_id=1, source_target_pairs={{0,4},{1,5},{2,6},{3,7},{4,0},{5,1},{6,2},{7,3},{8,12},{9,13},{10,... | collective-permute-start | bytes 4718600 | tf_op jit(solution)/shard_map/ppermute | solution.py:83
  286.5 26.5 %copy-start.4 = (f32[512,768]{1,0:T(8,128)S(1)}, f32[512,768]{1,0:T(8,128)}, u32[]{:S(2)}) copy-start(f32[512,768]{1,0:T(8,128)} %get-tuple-element.17) | copy-start | bytes 4718596
  286.5 25.1 %collective-permute-start.16 = (f32[512,512]{1,0:T(8,128)}, f32[512,512]{1,0:T(8,128)S(1)}, u32[]{:S(2)}, u32[]{:S(2)}) collective-permute-start(f32[512,512]{1,0:T(8,128)} %get-tuple-element.20), channel_id=1, source_target_pairs={{0,4},{1,5},{2,6},{3,7},{4,0},{5,1},{6,2},{7,3},{8,12},{9,13},{10,... | collective-permute-start | bytes 3145736 | tf_op jit(solution)/shard_map/ppermute | solution.py:83
  (4 other events, 21.1 us)
Sparse Core Ops, SparseCore 0:
  9.1 79.1 all-gather.8
  89.9 56.1 all-gather.10
  147.7 75.0 all-gather.12
  224.2 53.3 all-gather.14

commit v3 on v2

--- a/solution.py
+++ b/solution.py
@@ -10,8 +10,7 @@
 HD = 128
 SPK = 2
 AXES = ("ctx", "head")
-QUERY_CHUNKS = (3, 2)
-OUT_CHUNKS = (6, 4)
+OUT_CHUNKS = (7, 3)
 
 
 def add_rows(left_rows, shard_piece):
@@ -87,58 +86,100 @@
     return lax.all_gather(value, "ctx", axis=0, axis_index_groups=SAME_X)
 
 
-def product(place, lefts, weights, k_sizes):
-    total = None
-    for j in range(4):
-        first = 0
-        for i, size in enumerate(k_sizes):
-            right = weights[place[j], first : first + size, :]
-            term = jnp.dot(lefts[i * 4 + j][...], right, preferred_element_type=jnp.float32)
-            total = term if total is None else total + term
-            first += size
-    return total
-
-
 def query_body(place, *refs):
-    own, near = refs[:4], refs[4:8]
-    weights, kept, sent = refs[8:]
-    half = kept.shape[1]
-
-    def write(lefts):
-        total = product(place, lefts, weights, (weights.shape[1],))
-        kept[...] = total[:, :half]
-        sent[...] = total[:, half:]
-
-    first_group = pl.program_id(0) < pl.num_programs(0) // 2
-    pl.when(first_group)(lambda: write(own))
-    pl.when(jnp.logical_not(first_group))(lambda: write(near))
-
-
-def query_product(place, video_rows, near, weights):
-    rows = video_rows.shape[0]
+    *lefts, keep_weights, send_weights, kept, sent = refs
+    if len(lefts) == 4:
+        values = [left[...] for left in lefts]
+        lefts = [jnp.concatenate(values[:2], axis=1), jnp.concatenate(values[2:], axis=1)]
+    else:
+        lefts = [left[...] for left in lefts]
+
+    def total(weights):
+        first = jnp.dot(lefts[0], weights[place[0]], preferred_element_type=jnp.float32)
+        second = jnp.dot(lefts[1], weights[place[1]], preferred_element_type=jnp.float32)
+        return first + second
+
+    kept[...] = total(keep_weights)
+    sent[...] = total(send_weights)
+
+
+def query_product(place, lefts, weights):
+    rows = lefts[0].shape[0]
     depth, columns = weights.shape[1:]
     step = rows // 2
-    own_specs = [
-        pl.BlockSpec(
-            (step, depth),
-            functools.partial(lambda j, i, place: (jnp.minimum(i, 1), place[4 + j]), j),
-        )
-        for j in range(4)
-    ]
-    near_specs = [
-        pl.BlockSpec((step, depth), lambda i, place: (jnp.maximum(i - 2, 0), 0)) for _ in range(4)
-    ]
     half = columns // 2
-    part = jax.ShapeDtypeStruct((2 * rows, half), jnp.float32)
+    if len(lefts) == 1:
+        left_specs = [
+            pl.BlockSpec((step, depth // 2), functools.partial(lambda j, i, place: (i, place[4 + j]), j))
+            for j in range(4)
+        ]
+        lefts = lefts * 4
+    else:
+        left_specs = [pl.BlockSpec((step, depth), lambda i, place: (i, 0))] * 2
+    part = jax.ShapeDtypeStruct((rows, half), jnp.float32)
     return pl.pallas_call(
         query_body,
         grid_spec=pltpu.PrefetchScalarGridSpec(
             num_scalar_prefetch=1,
+            grid=(2,),
+            in_specs=left_specs
+            + [
+                pl.BlockSpec((2, depth, half), lambda i, place: (0, 0, place[2])),
+                pl.BlockSpec((2, depth, half), lambda i, place: (0, 0, place[3])),
+            ],
+            out_specs=[pl.BlockSpec((step, half), lambda i, place: (i, 0))] * 2,
+        ),
+        out_shape=[part, part],
+        cost_estimate=pl.CostEstimate(
+            flops=4 * rows * depth * columns,
+            transcendentals=0,
+            bytes_accessed=4 * (rows + columns) * depth + 4 * rows * columns,
+        ),
+        name="query_product",
+    )(place, *lefts, weights, weights)
+
+
+def out_product(place, groups, weights):
+    rows, depth = groups[0][0].shape
+    columns = weights.shape[2]
+    step = rows // 2
+
+    def body(place, *refs):
+        own, near, rest = refs[:4], refs[4:8], refs[8:]
+        weights, kept, sent = rest
+
+        def total(lefts):
+            found = None
+            for j in range(4):
+                term = jnp.dot(lefts[j][...], weights[place[j]], preferred_element_type=jnp.float32)
+                found = term if found is None else found + term
+            return found
+
+        pl.when(pl.program_id(0) < 2)(lambda: sent.__setitem__(..., total(near)))
+        pl.when(pl.program_id(0) >= 2)(lambda: kept.__setitem__(..., total(own)))
+
+    early = lambda i: jnp.minimum(i, 1)
+    late = lambda i: jnp.maximum(i - 2, 0)
+    specs = lambda at: [
+        pl.BlockSpec(
+            (step, depth), functools.partial(lambda skip, i, place: (at(i) + skip, 0), skip)
+        )
+        for skip in (0, 0, 0, 2)
+    ]
+    pieces = [piece for own, core, over_y in groups for piece in (own, core, over_y, core)]
+    part = jax.ShapeDtypeStruct((rows, columns), jnp.float32)
+    return pl.pallas_call(
+        body,
+        grid_spec=pltpu.PrefetchScalarGridSpec(
+            num_scalar_prefetch=1,
             grid=(4,),
-            in_specs=own_specs
-            + near_specs
+            in_specs=specs(late)
+            + specs(early)
             + [pl.BlockSpec(weights.shape, lambda i, place: (0, 0, 0))],
-            out_specs=[pl.BlockSpec((step, half), lambda i, place: (i, 0))] * 2,
+            out_specs=[
+                pl.BlockSpec((step, columns), lambda i, place: (late(i), 0)),
+                pl.BlockSpec((step, columns), lambda i, place: (early(i), 0)),
+            ],
         ),
         out_shape=[part, part],
         cost_estimate=pl.CostEstimate(
@@ -146,44 +187,8 @@
             transcendentals=0,
             bytes_accessed=8 * (2 * rows + columns) * depth + 8 * rows * columns,
         ),
-        name="query_product",
-    )(place, *([video_rows] * 4), *near, weights)
-
-
-def out_body(place, *refs, k_sizes):
-    *lefts, weights, kept, sent = refs
-    total = product(place, lefts, weights, k_sizes)
-    pl.when(pl.program_id(0) < 2)(lambda: kept.__setitem__(..., total))
-    pl.when(pl.program_id(0) >= 2)(lambda: sent.__setitem__(..., total))
-
-
-def out_product(place, lefts, weights, k_sizes):
-    rows = lefts[0].shape[0]
-    columns = weights.shape[2]
-    step = rows // 4
-    left_specs = [
-        pl.BlockSpec((step, size), lambda i, place: (i, 0)) for size in k_sizes for _ in range(4)
-    ]
-    part = jax.ShapeDtypeStruct((rows // 2, columns), jnp.float32)
-    return pl.pallas_call(
-        functools.partial(out_body, k_sizes=k_sizes),
-        grid_spec=pltpu.PrefetchScalarGridSpec(
-            num_scalar_prefetch=1,
-            grid=(4,),
-            in_specs=left_specs + [pl.BlockSpec(weights.shape, lambda i, place: (0, 0, 0))],
-            out_specs=[
-                pl.BlockSpec((step, columns), lambda i, place: (jnp.minimum(i, 1), 0)),
-                pl.BlockSpec((step, columns), lambda i, place: (jnp.maximum(i - 2, 0), 0)),
-            ],
-        ),
-        out_shape=[part, part],
-        cost_estimate=pl.CostEstimate(
-            flops=8 * rows * sum(k_sizes) * columns,
-            transcendentals=0,
-            bytes_accessed=8 * (rows + columns) * sum(k_sizes) + 4 * rows * columns,
-        ),
         name="out_product",
-    )(place, *lefts, weights)
+    )(place, *pieces, weights)
 
 
 def attend_body(kept, received, keys, values, speaker, attended, *, audio_length, heads):
@@ -212,15 +217,15 @@
 
 def attend(kept, received, keys, values, speaker, audio_length):
     rows, columns = kept.shape
-    step = rows // 4
+    step = rows // 2
     at = lambda i: (i, 0)
     whole = pl.BlockSpec(keys.shape, lambda i: (0, 0))
     return pl.pallas_call(
         functools.partial(attend_body, audio_length=audio_length, heads=columns // HD),
-        grid=(4,),
+        grid=(2,),
         in_specs=[
             pl.BlockSpec((step, columns), at),
-            pl.BlockSpec((step, columns), lambda i: ((i + 2) % 4, 0)),
+            pl.BlockSpec((step, columns), at),
             whole,
             whole,
             pl.BlockSpec((step, 1), at),
@@ -238,7 +243,7 @@
 
 def head_pieces(value):
     over_y = send(value, ACROSS_Y)
-    return [value, send(value, ACROSS_CORE), over_y, send(over_y, ACROSS_CORE)]
+    return value, send(jnp.concatenate([value, over_y], axis=0), ACROSS_CORE), over_y
 
 
 def plane_shards(video_rows, w_query, w_output, audio_tokens, w_key, w_value, row_lists, row_counts):
@@ -248,31 +253,21 @@
     ctx = lax.axis_index("ctx").astype(jnp.int32)
     h = lax.axis_index("head").astype(jnp.int32)
     x = ctx % 2
-    k_sizes = tuple(heads * HD for heads in QUERY_CHUNKS)
-
-    query_weights = []
-    first = 0
-    for size in k_sizes:
-        query_weights.append(
-            along_z(
-                jnp.concatenate(
-                    [
-                        lax.dynamic_slice(w_query, (0, x * block + first), (block, size)),
-                        lax.dynamic_slice(w_query, (0, (1 - x) * block + first), (block, size)),
-                    ],
-                    axis=1,
-                )
-            )
-        )
-        first += size
-
-    near = head_pieces(
-        send(
-            lax.dynamic_slice(video_rows, (0, (2 * h + 1 - x) * block), (rows, block)), ACROSS_X
-        )
-    )
-    order = jnp.arange(4, dtype=jnp.int32) ^ h
-    place = jnp.concatenate([order, 2 * order + x])
+    core = h % 2
+
+    query_weights = along_z(w_query).reshape(2, 2 * block, -1)
+
+    near_block = lambda plane: lax.dynamic_slice(
+        video_rows, (0, (2 * plane + 1 - x) * block), (rows, block)
+    )
+    near_half = send(
+        jnp.concatenate([near_block(2 * core), near_block(2 * core + 1)], axis=1), ACROSS_X
+    )
+    near = [near_half, send(near_half, ACROSS_CORE)]
+    planes = jnp.arange(4, dtype=jnp.int32)
+    sides = jnp.stack([x, 1 - x])
+    near_place = jnp.concatenate([jnp.stack([core, 1 - core]), sides])
+    own_place = jnp.concatenate([planes[:2], sides, 2 * planes + x])
 
     position = jnp.arange(rows, dtype=jnp.int32)
     named = (row_lists[:, :, None] == position[None, None, :]) & (
@@ -292,31 +287,28 @@
         .reshape(-1, audio_width)
     )
     audio_length = whole_audio.shape[0] // SPK
-    speaker = gathered[:2, SPK * tokens * audio_width :].astype(jnp.int32).reshape(-1, 1)
-    key_rows = add_rows(
-        whole_audio, lax.dynamic_slice(w_key, (0, x * block), (audio_width, block))
-    ).astype(jnp.bfloat16)
-    value_rows = add_rows(
-        whole_audio, lax.dynamic_slice(w_value, (0, x * block), (audio_width, block))
-    ).astype(jnp.bfloat16)
-
-    attended = []
-    first = 0
-    for weights, size in zip(query_weights, k_sizes):
-        at = slice(first, first + size)
-        kept, sent = query_product(place, video_rows, near, weights)
-        received = send(sent, ACROSS_X)
-        attended += head_pieces(
-            attend(kept, received, key_rows[:, at], value_rows[:, at], speaker, audio_length)
+    speakers = gathered[:2, SPK * tokens * audio_width :].astype(jnp.int32)
+    own_block = lambda weights: lax.dynamic_slice(weights, (0, x * block), (audio_width, block))
+    key_rows = add_rows(whole_audio, own_block(w_key)).astype(jnp.bfloat16)
+    value_rows = add_rows(whole_audio, own_block(w_value)).astype(jnp.bfloat16)
+
+    near_kept, near_sent = query_product(near_place, near, query_weights)
+    own_received = send(near_sent, ACROSS_X)
+    own_kept, own_sent = query_product(own_place, [video_rows], query_weights)
+    near_received = send(own_sent, ACROSS_X)
+    attended = [
+        head_pieces(
+            attend(kept, received, key_rows, value_rows, speakers[side][:, None], audio_length)
         )
-        first += size
+        for side, kept, received in ((0, own_kept, own_received), (1, near_kept, near_received))
+    ]
 
     results = []
     first = 0
     for heads in OUT_CHUNKS:
         size = heads * HD
         weights = along_z(lax.slice_in_dim(w_output, first, first + size, axis=1))
-        kept, sent = out_product(place, attended, weights, k_sizes)
+        kept, sent = out_product(planes ^ h, attended, weights)
         results.append((kept + send(sent, ACROSS_X)).astype(jnp.bfloat16))
         first += size
     return jnp.concatenate(results, axis=1)

time: 322 us -> 313 us (0.972)
  local copies, waits for them, and re-layouts: 16.5 us -> 9.67 us
  starting transfers between devices: 18.9 us -> 13.1 us
  other arithmetic: 9.07 us -> 12.6 us
    ppermute x17 -> x13, waiting for transfers between devices: 66.7 us -> 112 us  [send(): return lax.ppermute(value, AXES, move)]
    all_gather x4 -> x3, waiting for transfers between devices: 143 us -> 99.8 us  [along_z(): return lax.all_gather(value, 'ctx', axis=0, axis_index_groups=SAME_X)]
    ppermute x17 -> x13, starting transfers between devices: 18.8 us -> 13 us  [send(): return lax.ppermute(value, AXES, move)]
    concatenate x3 -> x5, other arithmetic: 2.48 us -> 6.96 us  [the longest x2 4.54 us: head_pieces(): jnp.concatenate([value, over_y], axis=0)]
    slice x4 -> x0, local copies, waits for them, and re-layouts: 4.04 us -> none  [the longest x2 2.02 us: plane_shards(): key_rows[:, at]]
  transfers between devices with their start and end apart: 21 -> 16, of which waited for: 10 -> 10; matrix products, arithmetic and copies ran while one was open for 7% -> 6% of each run, Pallas kernels for 16% -> 15%
where the time goes in v3:
time: 313 us
  waiting for transfers between devices  213 us (68%)
  Pallas kernels  48 us (15%)
  between operations  13.3 us (4%)
  starting transfers between devices  13.1 us (4%)
  other arithmetic  12.6 us (4%)
  local copies, waits for them, and re-layouts  9.67 us (3%)
    ppermute x13, waiting for transfers between devices, send(): return lax.ppermute(value, AXES, move)  112 us
    all_gather x3, waiting for transfers between devices, along_z(): return lax.all_gather(value, 'ctx', axis=0, axis_index_groups=SAME_X)  99.8 us
    pallas_call x2, Pallas kernels, out_product(): pl.pallas_call(body, grid_spec=pltpu.PrefetchScalarGridSpec(num_scalar_pr...  20.7 us
    pallas_call x2, Pallas kernels, query_product(): pl.pallas_call(query_body, grid_spec=pltpu.PrefetchScalarGridSpec(num_sca...  18.9 us
    ppermute x13, starting transfers between devices, send(): return lax.ppermute(value, AXES, move)  13 us
    pallas_call x2, Pallas kernels, attend(): pl.pallas_call(functools.partial(attend_body, audio_length=audio_length,...  8.44 us
  transfers between devices with their start and end apart: 16, of which 10 were waited for; matrix products, arithmetic and copies ran while one was open for 6% of the time, Pallas kernels for 15%

profile of v3, /device:TPU:0, one launch (start us, length us, event | category | flops | bytes accessed | tf_op | source)
XLA Modules:
  0.0 312.7 jit_solution(3788931224456777848)
XLA Ops:
  7.3 2.4 slice.26
  9.8 1.4 constant_dynamic-slice_fusion.1
  11.3 1.2 pad_maximum_fusion
  12.4 2.9 collective-permute-start
  17.4 27.2 %collective-permute-done.refs_0_ = bf16[512,1280]{1,0:T(8,128)(2,1)S(1)} collective-permute-done((bf16[512,1280]{1,0:T(8,128)(2,1)}, bf16[512,1280]{1,0:T(8,128)(2,1)S(1)}, u32[]{:S(2)}, u32[]{:S(2)}) %collective-permute-start) | collective-permute-done | bytes 1310752 | tf_op jit(solution)/shard_map/ppermute | solution.py:82
  45.0 1.9 collective-permute-start.4
  46.9 6.6 %collective-permute-done.4 = bf16[2,6656]{1,0:T(2,128)(2,1)S(1)} collective-permute-done((bf16[2,6656]{1,0:T(2,128)(2,1)S(1)}, bf16[2,6656]{1,0:T(2,128)(2,1)S(1)}, u32[]{:S(2)}, u32[]{:S(2)}) %collective-permute-start.4) | collective-permute-done | bytes 26656 | tf_op jit(solution)/shard_map/ppermute | solution.py:82
  53.6 79.9 %all-gather.7.cloned.1.call-done = bf16[2560,1280]{1,0:T(8,128)(2,1)} async-done(((bf16[640,1280]{1,0:T(8,128)(2,1)}), bf16[2560,1280]{1,0:T(8,128)(2,1)}) %all-gather.7.cloned.1.call-update) | async-done | bytes 6553616 | tf_op jit(solution)/shard_map/all_gather | solution.py:86
  133.5 9.6 %query_product.2 = (f32[512,640]{1,0:T(8,128)}, f32[512,640]{1,0:T(8,128)}) custom-call(s32[8]{0:T(128)} %pad_add_fusion.place, bf16[512,5120]{1,0:T(8,128)(2,1)} %refs_3_.1, bf16[512,5120]{1,0:T(8,128)(2,1)} %refs_3_.1, bf16[512,5120]{1,0:T(8,128)(2,1)} %refs_3_.1, bf16[512,5120]{1,0:T(8,128)(2,1)} %refs_3_.1, bf16[2,1280,1280]{2,1,0:T(8,128)(2,1)} %bitcast.19, ...), custom_call_target="tpu_custom_call" | custom-call | flops 3355443200 | bytes 11796480 | tf_op jit(solution)/shard_map/query_product/pallas_call | solution.py:120
  143.1 1.5 collective-permute-start.8
  144.7 9.3 %query_product.3 = (f32[512,640]{1,0:T(8,128)}, f32[512,640]{1,0:T(8,128)}) custom-call(s32[4]{0:T(128)} %pad_add_fusion.1.place, bf16[512,1280]{1,0:T(8,128)(2,1)} %copy-done.5, bf16[512,1280]{1,0:T(8,128)(2,1)} %collective-permute-done.1.refs_1_, bf16[2,1280,1280]{2,1,0:T(8,128)(2,1)} %bitcast.21, bf16[2,1280,1280]{2,1,0:T(8,128)(2,1)} %bitcast.22), custom_call_target="tpu_custom_call" | custom-call | flops 3355443200 | bytes 11796480 | tf_op jit(solution)/shard_map/query_product/pallas_call | solution.py:120
  156.6 2.1 convolution_convert_fusion.1.keys
  158.7 16.5 %collective-permute-done.8.received = f32[512,640]{1,0:T(8,128)} collective-permute-done((f32[512,640]{1,0:T(8,128)}, f32[512,640]{1,0:T(8,128)}, u32[]{:S(2)}, u32[]{:S(2)}) %collective-permute-start.8) | collective-permute-done | bytes 1310752 | tf_op jit(solution)/shard_map/ppermute | solution.py:82
  175.1 4.2 %attend.3.refs_4_ = bf16[512,640]{1,0:T(8,128)(2,1)} custom-call(f32[512,640]{1,0:T(8,128)} %get-tuple-element.15.kept, f32[512,640]{1,0:T(8,128)} %collective-permute-done.8.received, bf16[64,640]{1,0:T(8,128)(2,1)} %convolution_convert_fusion.1.keys, bf16[64,640]{1,0:T(8,128)(2,1)} %convolution_convert_fusion.values, s32[512,1]{1,0:T(8,128)} %copy.15.speaker), custom_call_target="tpu_custom_call" | custom-call | flops 83886080 | bytes 3276800 | tf_op jit(solution)/shard_map/attend/pallas_call | solution.py:223
  179.3 1.5 collective-permute-start.9
  181.7 20.6 %collective-permute-done.2.received = f32[512,640]{1,0:T(8,128)S(1)} collective-permute-done((f32[512,640]{1,0:T(8,128)}, f32[512,640]{1,0:T(8,128)S(1)}, u32[]{:S(2)}, u32[]{:S(2)}) %collective-permute-start.2) | collective-permute-done | bytes 1310752 | tf_op jit(solution)/shard_map/ppermute | solution.py:82
  203.3 4.3 %attend.2.refs_0_ = bf16[512,640]{1,0:T(8,128)(2,1)} custom-call(f32[512,640]{1,0:T(8,128)} %get-tuple-element.13.kept, f32[512,640]{1,0:T(8,128)} %copy-done.6, bf16[64,640]{1,0:T(8,128)(2,1)} %convolution_convert_fusion.1.keys, bf16[64,640]{1,0:T(8,128)(2,1)} %convolution_convert_fusion.values, s32[512,1]{1,0:T(8,128)} %copy.14.speaker), custom_call_target="tpu_custom_call" | custom-call | flops 83886080 | bytes 3276800 | tf_op jit(solution)/shard_map/attend/pallas_call | solution.py:223
  207.6 1.5 collective-permute-start.6
  209.0 1.9 slice.27
  211.0 2.3 pad_maximum_fusion.2
  213.2 10.6 %collective-permute-done.6.refs_2_ = bf16[512,640]{1,0:T(8,128)(2,1)} collective-permute-done((bf16[512,640]{1,0:T(8,128)(2,1)}, bf16[512,640]{1,0:T(8,128)(2,1)}, u32[]{:S(2)}, u32[]{:S(2)}) %collective-permute-start.6) | collective-permute-done | bytes 655392 | tf_op jit(solution)/shard_map/ppermute | solution.py:82
  223.8 2.3 pad_maximum_fusion.1
  226.6 2.7 collective-permute-done.7.refs_1_.refs_3_
  230.4 12.4 %out_product.2 = (f32[512,896]{1,0:T(8,128)}, f32[512,896]{1,0:T(8,128)}) custom-call(s32[4]{0:T(128)} %iota_xor_fusion.place, bf16[512,640]{1,0:T(8,128)(2,1)} %attend.2.refs_0_, bf16[1024,640]{1,0:T(8,128)(2,1)} %copy-done.3, bf16[512,640]{1,0:T(8,128)(2,1)} %collective-permute-done.6.refs_2_, bf16[1024,640]{1,0:T(8,128)(2,1)} %copy-done.3, ...), custom_call_target="tpu_custom_call" | custom-call | flops 4697620480 | bytes 13500416 | tf_op jit(solution)/shard_map/out_product/pallas_call | solution.py:171
  242.8 1.5 collective-permute-start.11
  244.3 19.9 %all-gather.11.cloned.1.call-done = bf16[2560,384]{1,0:T(8,128)(2,1)} async-done(((bf16[640,384]{1,0:T(8,128)(2,1)}), bf16[2560,384]{1,0:T(8,128)(2,1)}) %all-gather.11.cloned.1.call-update) | async-done | bytes 1966096 | tf_op jit(solution)/shard_map/all_gather | solution.py:86
  264.2 8.2 %out_product.3 = (f32[512,384]{1,0:T(8,128)}, f32[512,384]{1,0:T(8,128)}) custom-call(s32[4]{0:T(128)} %iota_xor_fusion.place, bf16[512,640]{1,0:T(8,128)(2,1)} %attend.2.refs_0_, bf16[1024,640]{1,0:T(8,128)(2,1)} %copy-done.3, bf16[512,640]{1,0:T(8,128)(2,1)} %collective-permute-done.6.refs_2_, bf16[1024,640]{1,0:T(8,128)(2,1)} %copy-done.3, ...), custom_call_target="tpu_custom_call" | custom-call | flops 2013265920 | bytes 8781824 | tf_op jit(solution)/shard_map/out_product/pallas_call | solution.py:171
  272.4 1.5 collective-permute-start.12
  274.0 28.0 %collective-permute-done.12 = f32[512,384]{1,0:T(8,128)S(1)} collective-permute-done((f32[512,384]{1,0:T(8,128)}, f32[512,384]{1,0:T(8,128)S(1)}, u32[]{:S(2)}, u32[]{:S(2)}) %collective-permute-start.12) | collective-permute-done | bytes 786464 | tf_op jit(solution)/shard_map/ppermute | solution.py:82
  301.9 1.3 add_convert_fusion.1
  303.2 1.8 add_convert_fusion
  305.0 1.2 pad_maximum_fusion.3
  (63 shorter events, 9.5 us)
Async XLA Ops:
  6.5 149.1 %copy-start = (bf16[768,1280]{1,0:T(8,128)(2,1)S(1)}, bf16[768,1280]{1,0:T(8,128)(2,1)}, u32[]{:S(2)}) copy-start(bf16[768,1280]{1,0:T(8,128)(2,1)} %param.14) | copy-start | bytes 5898244
  6.5 127.0 %all-gather.7.cloned.1.call-start = ((), (), s32[]{:S(2)}) async-start(), calls=%async_computation | async-start | bytes 8192000 | tf_op jit(solution)/shard_map/all_gather | solution.py:86
  7.3 219.4 %all-gather.9.cloned.1.call-start = ((), (), s32[]{:S(2)}) async-start(), calls=%async_computation.1 | async-start | bytes 5734400 | tf_op jit(solution)/shard_map/all_gather | solution.py:86
  9.7 254.5 %all-gather.11.cloned.1.call-start = ((), (), s32[]{:S(2)}) async-start(), calls=%async_computation.2 | async-start | bytes 2457600 | tf_op jit(solution)/shard_map/all_gather | solution.py:86
  11.2 4.1 %copy-start.7 = (bf16[2,4,768]{2,1,0:T(4,128)(2,1)S(1)}, bf16[2,4,768]{2,1,0:T(4,128)(2,1)}, u32[]{:S(2)}) copy-start(bf16[2,4,768]{2,1,0:T(4,128)(2,1)} %param.12) | copy-start | bytes 36868
  11.2 4.1 %copy-start.9 = (s32[2,1]{0,1:T(1,128)S(1)}, s32[2,1]{0,1:T(1,128)}, u32[]{:S(2)}) copy-start(s32[2,1]{0,1:T(1,128)} %param.16) | copy-start | bytes 28
  11.2 4.2 %copy-start.8 = (s32[2,512]{1,0:T(2,128)S(1)}, s32[2,512]{1,0:T(2,128)}, u32[]{:S(2)}) copy-start(s32[2,512]{1,0:T(2,128)} %param.15) | copy-start | bytes 12292
  11.2 4.7 %copy-start.10 = (s32[2]{0:T(128)S(1)}, s32[2]{0:T(128)}, u32[]{:S(2)}) copy-start(s32[2]{0:T(128)} %constant.45) | copy-start | bytes 28
  12.4 32.2 %collective-permute-start = (bf16[512,1280]{1,0:T(8,128)(2,1)}, bf16[512,1280]{1,0:T(8,128)(2,1)S(1)}, u32[]{:S(2)}, u32[]{:S(2)}) collective-permute-start(bf16[512,1280]{1,0:T(8,128)(2,1)} %pad_maximum_fusion), channel_id=1, source_target_pairs={{0,4},{1,5},{2,6},{3,7},{4,0},{5,1},{6,2},{7,3},{8,12},{9,13},{10,... | collective-permute-start | bytes 3932168 | tf_op jit(solution)/shard_map/ppermute | solution.py:82
  16.0 28.9 %collective-permute-start.3 = (bf16[1,6656]{1,0:T(2,128)(2,1)S(1)}, bf16[1,6656]{1,0:T(2,128)(2,1)S(1)}, u32[]{:S(2)}, u32[]{:S(2)}) collective-permute-start(bf16[1,6656]{1,0:T(2,128)(2,1)S(1)} %broadcast_in_dim.2), channel_id=1, source_target_pairs={{0,4},{1,5},{2,6},{3,7},{4,0},{5,1},{6,2},{7,3},{8,12},{9,13},{10,... | collective-permute-start | bytes 39944 | tf_op jit(solution)/shard_map/ppermute | solution.py:82
  44.6 98.5 %copy-start.5 = (bf16[512,1280]{1,0:T(8,128)(2,1)}, bf16[512,1280]{1,0:T(8,128)(2,1)S(1)}, u32[]{:S(2)}) copy-start(bf16[512,1280]{1,0:T(8,128)(2,1)S(1)} %collective-permute-done.refs_0_) | copy-start | bytes 3932164
  44.6 100.0 %collective-permute-start.1 = (bf16[512,1280]{1,0:T(8,128)(2,1)S(1)}, bf16[512,1280]{1,0:T(8,128)(2,1)}, u32[]{:S(2)}, u32[]{:S(2)}) collective-permute-start(bf16[512,1280]{1,0:T(8,128)(2,1)S(1)} %collective-permute-done.refs_0_), channel_id=1, source_target_pairs={{0,1},{1,0},{2,3},{3,2},{4,5},{5,4},{6,7},{7,6},{8,9},{9,8},{10,11... | collective-permute-start | bytes 3932168 | tf_op jit(solution)/shard_map/ppermute | solution.py:82
  45.0 8.5 %collective-permute-start.4 = (bf16[2,6656]{1,0:T(2,128)(2,1)S(1)}, bf16[2,6656]{1,0:T(2,128)(2,1)S(1)}, u32[]{:S(2)}, u32[]{:S(2)}) collective-permute-start(bf16[2,6656]{1,0:T(2,128)(2,1)S(1)} %pad_maximum_fusion.9), channel_id=1, source_target_pairs={{0,8},{1,9},{2,10},{3,11},{4,12},{5,13},{6,14},{7,15},{8,0},{9,1},... | collective-permute-start | bytes 79880 | tf_op jit(solution)/shard_map/ppermute | solution.py:82
  53.5 101.9 %collective-permute-start.5 = (bf16[4,6656]{1,0:T(4,128)(2,1)S(1)}, bf16[4,6656]{1,0:T(4,128)(2,1)S(1)}, u32[]{:S(2)}, u32[]{:S(2)}) collective-permute-start(bf16[4,6656]{1,0:T(4,128)(2,1)S(1)} %pad_maximum_fusion.7), channel_id=1, source_target_pairs={{0,16},{1,17},{2,18},{3,19},{4,20},{5,21},{6,22},{7,23},{8,24},{9,... | collective-permute-start | bytes 159752 | tf_op jit(solution)/shard_map/ppermute | solution.py:82
  143.1 32.0 %collective-permute-start.8 = (f32[512,640]{1,0:T(8,128)}, f32[512,640]{1,0:T(8,128)}, u32[]{:S(2)}, u32[]{:S(2)}) collective-permute-start(f32[512,640]{1,0:T(8,128)} %get-tuple-element.16), channel_id=1, source_target_pairs={{0,4},{1,5},{2,6},{3,7},{4,0},{5,1},{6,2},{7,3},{8,12},{9,13},{10,... | collective-permute-start | bytes 3932168 | tf_op jit(solution)/shard_map/ppermute | solution.py:82
  154.0 48.2 %collective-permute-start.2 = (f32[512,640]{1,0:T(8,128)}, f32[512,640]{1,0:T(8,128)S(1)}, u32[]{:S(2)}, u32[]{:S(2)}) collective-permute-start(f32[512,640]{1,0:T(8,128)} %get-tuple-element.14), channel_id=1, source_target_pairs={{0,4},{1,5},{2,6},{3,7},{4,0},{5,1},{6,2},{7,3},{8,12},{9,13},{10,... | collective-permute-start | bytes 3932168 | tf_op jit(solution)/shard_map/ppermute | solution.py:82
  179.3 31.6 %collective-permute-start.9 = (bf16[512,640]{1,0:T(8,128)(2,1)}, bf16[512,640]{1,0:T(8,128)(2,1)}, u32[]{:S(2)}, u32[]{:S(2)}) collective-permute-start(bf16[512,640]{1,0:T(8,128)(2,1)} %attend.3.refs_4_), channel_id=1, source_target_pairs={{0,2},{1,3},{2,0},{3,1},{4,6},{5,7},{6,4},{7,5},{8,10},{9,11},{10,... | collective-permute-start | bytes 1966088 | tf_op jit(solution)/shard_map/ppermute | solution.py:82
  202.2 1.1 copy-start.6
  203.3 7.6 %copy-start.1 = (bf16[512,640]{1,0:T(8,128)(2,1)S(1)}, bf16[512,640]{1,0:T(8,128)(2,1)}, u32[]{:S(2)}) copy-start(bf16[512,640]{1,0:T(8,128)(2,1)} %attend.3.refs_4_) | copy-start | bytes 1966084
  207.6 16.3 %copy-start.2 = (bf16[512,640]{1,0:T(8,128)(2,1)S(1)}, bf16[512,640]{1,0:T(8,128)(2,1)}, u32[]{:S(2)}) copy-start(bf16[512,640]{1,0:T(8,128)(2,1)} %attend.2.refs_0_) | copy-start | bytes 1966084
  207.6 16.3 %collective-permute-start.6 = (bf16[512,640]{1,0:T(8,128)(2,1)}, bf16[512,640]{1,0:T(8,128)(2,1)}, u32[]{:S(2)}, u32[]{:S(2)}) collective-permute-start(bf16[512,640]{1,0:T(8,128)(2,1)} %attend.2.refs_0_), channel_id=1, source_target_pairs={{0,2},{1,3},{2,0},{3,1},{4,6},{5,7},{6,4},{7,5},{8,10},{9,11},{10,... | collective-permute-start | bytes 1966088 | tf_op jit(solution)/shard_map/ppermute | solution.py:82
  213.2 13.4 %collective-permute-start.10 = (bf16[1024,640]{1,0:T(8,128)(2,1)}, bf16[1024,640]{1,0:T(8,128)(2,1)}, u32[]{:S(2)}, u32[]{:S(2)}) collective-permute-start(bf16[1024,640]{1,0:T(8,128)(2,1)} %pad_maximum_fusion.2), channel_id=1, source_target_pairs={{0,1},{1,0},{2,3},{3,2},{4,5},{5,4},{6,7},{7,6},{8,9},{9,8},{10,11... | collective-permute-start | bytes 3932168 | tf_op jit(solution)/shard_map/ppermute | solution.py:82
  226.1 3.2 %collective-permute-start.7 = (bf16[1024,640]{1,0:T(8,128)(2,1)}, bf16[1024,640]{1,0:T(8,128)(2,1)S(1)}, u32[]{:S(2)}, u32[]{:S(2)}) collective-permute-start(bf16[1024,640]{1,0:T(8,128)(2,1)} %pad_maximum_fusion.1), channel_id=1, source_target_pairs={{0,1},{1,0},{2,3},{3,2},{4,5},{5,4},{6,7},{7,6},{8,9},{9,8},{10,11... | collective-permute-start | bytes 3932168 | tf_op jit(solution)/shard_map/ppermute | solution.py:82
  229.3 1.1 copy-start.3
  242.8 60.4 %collective-permute-start.11 = (f32[512,896]{1,0:T(8,128)}, f32[512,896]{1,0:T(8,128)}, u32[]{:S(2)}, u32[]{:S(2)}) collective-permute-start(f32[512,896]{1,0:T(8,128)} %get-tuple-element.18), channel_id=1, source_target_pairs={{0,4},{1,5},{2,6},{3,7},{4,0},{5,1},{6,2},{7,3},{8,12},{9,13},{10,... | collective-permute-start | bytes 5505032 | tf_op jit(solution)/shard_map/ppermute | solution.py:82
  272.4 30.8 %copy-start.4 = (f32[512,896]{1,0:T(8,128)S(1)}, f32[512,896]{1,0:T(8,128)}, u32[]{:S(2)}) copy-start(f32[512,896]{1,0:T(8,128)} %get-tuple-element.17) | copy-start | bytes 5505028
  272.4 29.5 %collective-permute-start.12 = (f32[512,384]{1,0:T(8,128)}, f32[512,384]{1,0:T(8,128)S(1)}, u32[]{:S(2)}, u32[]{:S(2)}) collective-permute-start(f32[512,384]{1,0:T(8,128)} %get-tuple-element.20), channel_id=1, source_target_pairs={{0,4},{1,5},{2,6},{3,7},{4,0},{5,1},{6,2},{7,3},{8,12},{9,13},{10,... | collective-permute-start | bytes 2359304 | tf_op jit(solution)/shard_map/ppermute | solution.py:82
Sparse Core Ops, SparseCore 0:
  8.9 124.5 all-gather.6
  135.1 85.3 all-gather.8
  222.1 42.0 all-gather.10

commit v4 on v3

--- a/solution.py
+++ b/solution.py
@@ -10,7 +10,8 @@
 HD = 128
 SPK = 2
 AXES = ("ctx", "head")
-OUT_CHUNKS = (7, 3)
+HOPPED = 2
+GATHERED = (6, 2)
 
 
 def add_rows(left_rows, shard_piece):
@@ -75,6 +76,8 @@
 ACROSS_CORE = pairs(4, lambda z, x, h: (z, x, h ^ 1))
 ONE_ALONG = pairs(4, lambda z, x, h: (z ^ 1, x, h))
 TWO_ALONG = pairs(4, lambda z, x, h: (z ^ 2, x, h))
+MID_TO_END = [pair for pair in ONE_ALONG if pair[0] // 8 in (1, 2)]
+MID_TO_MID = pairs(4, lambda z, x, h: (3 - z if z in (1, 2) else z, x, h))
 SAME_X = [[0, 2, 4, 6], [1, 3, 5, 7]]
 
 
@@ -84,6 +87,37 @@
 
 def along_z(value):
     return lax.all_gather(value, "ctx", axis=0, axis_index_groups=SAME_X)
+
+
+def diagonal(groups):
+    shape = (groups * 128, 128)
+    row = lax.broadcasted_iota(jnp.int32, shape, 0) % 128
+    return row == lax.broadcasted_iota(jnp.int32, shape, 1)
+
+
+def pack(value, packed):
+    rows, columns = value.shape
+    groups = rows // 128
+    peak = jnp.max(jnp.abs(value), axis=1, keepdims=True)
+    power = jnp.clip(jnp.floor(jnp.log2(jnp.maximum(peak, 1e-30))) + 1.0, -90.0, 120.0)
+    scaled = jnp.clip(jnp.round(value * jnp.exp2(15.0 - power)), -32767.0, 32767.0)
+    packed[:rows, :] = scaled.astype(jnp.int32).astype(jnp.int16)
+    spread = jnp.where(diagonal(groups), power, 0.0).reshape(groups, 128, 128).sum(axis=1)
+    spread = jnp.concatenate([spread, jnp.zeros((16 - groups, 128), jnp.float32)], axis=0)
+    packed[rows:, :128] = spread.astype(jnp.int32).astype(jnp.int16)
+    packed[rows:, 128:] = jnp.zeros((16, columns - 128), jnp.int16)
+
+
+def row_scale(packed):
+    groups = (packed.shape[0] - 16) // 128
+    spread = packed[groups * 128 :, :128].astype(jnp.int32).astype(jnp.float32)[:groups]
+    spread = jnp.broadcast_to(spread[:, None, :], (groups, 128, 128)).reshape(groups * 128, 128)
+    power = jnp.sum(jnp.where(diagonal(groups), spread, 0.0), axis=1, keepdims=True)
+    return jnp.exp2(power - 15.0)
+
+
+def unpack(packed, at, scale):
+    return packed[: packed.shape[0] - 16, at].astype(jnp.int32).astype(jnp.float32) * scale
 
 
 def query_body(place, *refs):
@@ -100,7 +134,7 @@
         return first + second
 
     kept[...] = total(keep_weights)
-    sent[...] = total(send_weights)
+    pack(total(send_weights), sent)
 
 
 def query_product(place, lefts, weights):
@@ -116,7 +150,10 @@
         lefts = lefts * 4
     else:
         left_specs = [pl.BlockSpec((step, depth), lambda i, place: (i, 0))] * 2
-    part = jax.ShapeDtypeStruct((rows, half), jnp.float32)
+    out_shape = [
+        jax.ShapeDtypeStruct((rows, half), jnp.float32),
+        jax.ShapeDtypeStruct((2 * (step + 16), half), jnp.int16),
+    ]
     return pl.pallas_call(
         query_body,
         grid_spec=pltpu.PrefetchScalarGridSpec(
@@ -127,9 +164,12 @@
                 pl.BlockSpec((2, depth, half), lambda i, place: (0, 0, place[2])),
                 pl.BlockSpec((2, depth, half), lambda i, place: (0, 0, place[3])),
             ],
-            out_specs=[pl.BlockSpec((step, half), lambda i, place: (i, 0))] * 2,
-        ),
-        out_shape=[part, part],
+            out_specs=[
+                pl.BlockSpec((step, half), lambda i, place: (i, 0)),
+                pl.BlockSpec((step + 16, half), lambda i, place: (i, 0)),
+            ],
+        ),
+        out_shape=out_shape,
         cost_estimate=pl.CostEstimate(
             flops=4 * rows * depth * columns,
             transcendentals=0,
@@ -155,7 +195,7 @@
                 found = term if found is None else found + term
             return found
 
-        pl.when(pl.program_id(0) < 2)(lambda: sent.__setitem__(..., total(near)))
+        pl.when(pl.program_id(0) < 2)(lambda: pack(total(near), sent))
         pl.when(pl.program_id(0) >= 2)(lambda: kept.__setitem__(..., total(own)))
 
     early = lambda i: jnp.minimum(i, 1)
@@ -167,7 +207,10 @@
         for skip in (0, 0, 0, 2)
     ]
     pieces = [piece for own, core, over_y in groups for piece in (own, core, over_y, core)]
-    part = jax.ShapeDtypeStruct((rows, columns), jnp.float32)
+    out_shape = [
+        jax.ShapeDtypeStruct((rows, columns), jnp.float32),
+        jax.ShapeDtypeStruct((2 * (step + 16), columns), jnp.int16),
+    ]
     return pl.pallas_call(
         body,
         grid_spec=pltpu.PrefetchScalarGridSpec(
@@ -178,10 +221,10 @@
             + [pl.BlockSpec(weights.shape, lambda i, place: (0, 0, 0))],
             out_specs=[
                 pl.BlockSpec((step, columns), lambda i, place: (late(i), 0)),
-                pl.BlockSpec((step, columns), lambda i, place: (early(i), 0)),
+                pl.BlockSpec((step + 16, columns), lambda i, place: (early(i), 0)),
             ],
         ),
-        out_shape=[part, part],
+        out_shape=out_shape,
         cost_estimate=pl.CostEstimate(
             flops=16 * rows * depth * columns,
             transcendentals=0,
@@ -198,9 +241,10 @@
     of_key = jnp.where(lane < audio_length, 1, 2)
     own_key = of_key == of_row
     live = of_row > 0
+    received_scale = row_scale(received)
     for head in range(heads):
         at = slice(head * HD, (head + 1) * HD)
-        query = (kept[:, at] + received[:, at]).astype(jnp.bfloat16)
+        query = (kept[:, at] + unpack(received, at, received_scale)).astype(jnp.bfloat16)
         scores = (
             lax.dot_general(
                 query, keys[:, at], (((1,), (1,)), ((), ())), preferred_element_type=jnp.float32
@@ -225,7 +269,7 @@
         grid=(2,),
         in_specs=[
             pl.BlockSpec((step, columns), at),
-            pl.BlockSpec((step, columns), at),
+            pl.BlockSpec((step + 16, columns), at),
             whole,
             whole,
             pl.BlockSpec((step, 1), at),
@@ -241,6 +285,37 @@
     )(kept, received, keys, values, speaker)
 
 
+def finish_body(kept, received, scales, *refs):
+    refs[-1][...] = (kept[...] + unpack(received, slice(None), row_scale(scales))).astype(
+        jnp.bfloat16
+    )
+
+
+def finish(kept, received, first, whole, result):
+    rows, columns = kept.shape
+    step = rows // 2
+    width = 2 * HD
+    at = lambda i, j: (i, j)
+    given = [] if result is None else [result]
+    return pl.pallas_call(
+        finish_body,
+        grid=(2, columns // width),
+        in_specs=[
+            pl.BlockSpec((step, width), at),
+            pl.BlockSpec((step + 16, width), at),
+            pl.BlockSpec((step + 16, 128), lambda i, j: (i, 0)),
+        ]
+        + [pl.BlockSpec(memory_space=pl.ANY)] * len(given),
+        out_specs=pl.BlockSpec((step, width), lambda i, j: (i, first // width + j)),
+        out_shape=jax.ShapeDtypeStruct((rows, whole), jnp.bfloat16),
+        input_output_aliases={3: 0} if given else {},
+        cost_estimate=pl.CostEstimate(
+            flops=2 * rows * columns, transcendentals=0, bytes_accessed=8 * rows * columns
+        ),
+        name="finish",
+    )(kept, received, received, *given)
+
+
 def head_pieces(value):
     over_y = send(value, ACROSS_Y)
     return value, send(jnp.concatenate([value, over_y], axis=0), ACROSS_CORE), over_y
@@ -256,6 +331,21 @@
     core = h % 2
 
     query_weights = along_z(w_query).reshape(2, 2 * block, -1)
+
+    z = ctx // 2
+    is_mid = (z == 1) | (z == 2)
+    hopped = HOPPED * HD
+    if hopped:
+        piece = w_output[:, :hopped]
+        swapped = send(piece, ONE_ALONG)
+        opposite = send(piece, MID_TO_MID)
+        last = send(swapped, MID_TO_MID)
+        to_end = send(opposite, MID_TO_END)
+        last_to_end = send(last, MID_TO_END)
+        third = jnp.where(is_mid, last, to_end)
+        fourth = jnp.where(is_mid, opposite, last_to_end)
+        hopped_weights = jnp.stack([piece, swapped, third, fourth])
+        query_weights, hopped_weights = lax.optimization_barrier((query_weights, hopped_weights))
 
     near_block = lambda plane: lax.dynamic_slice(
         video_rows, (0, (2 * plane + 1 - x) * block), (rows, block)
@@ -303,15 +393,17 @@
         for side, kept, received in ((0, own_kept, own_received), (1, near_kept, near_received))
     ]
 
-    results = []
-    first = 0
-    for heads in OUT_CHUNKS:
+    chunks = [(hopped_weights, planes ^ h ^ z, 0)] if hopped else []
+    first = hopped
+    for heads in GATHERED:
         size = heads * HD
-        weights = along_z(lax.slice_in_dim(w_output, first, first + size, axis=1))
-        kept, sent = out_product(planes ^ h, attended, weights)
-        results.append((kept + send(sent, ACROSS_X)).astype(jnp.bfloat16))
+        chunks.append((along_z(w_output[:, first : first + size]), planes ^ h, first))
         first += size
-    return jnp.concatenate(results, axis=1)
+    result = None
+    for weights, out_place, first in chunks:
+        kept, sent = out_product(out_place, attended, weights)
+        result = finish(kept, send(sent, ACROSS_X), first, w_output.shape[1], result)
+    return result
 
 
 def solution(mesh):

time: 313 us -> 283 us (0.904)
  waiting for transfers between devices: 213 us -> 129 us
  starting transfers between devices: 13.1 us -> 53.9 us
  Pallas kernels: 48 us -> 62.5 us
  other arithmetic: 12.6 us -> 9.07 us
    all_gather x3, waiting for transfers between devices: 99.8 us -> 55.5 us  [along_z(): return lax.all_gather(value, 'ctx', axis=0, axis_index_groups=SAME_X)]
    ppermute x13 -> x19, starting transfers between devices: 13 us -> 53.8 us  [send(): return lax.ppermute(value, AXES, move)]
    ppermute x13 -> x19, waiting for transfers between devices: 112 us -> 72.5 us  [send(): return lax.ppermute(value, AXES, move)]
    pallas_call x0 -> x3, Pallas kernels: none -> 8.9 us  [finish(): pl.pallas_call(finish_body, grid=(2, columns // width), in_specs=[pl.Bloc...]
    pallas_call x2 -> x3, Pallas kernels: 20.7 us -> 25.3 us  [out_product(): pl.pallas_call(body, grid_spec=pltpu.PrefetchScalarGridSpec(num_scalar_pr...]
  transfers between devices with their start and end apart: 16 -> 22, of which waited for: 10 -> 8; matrix products, arithmetic and copies ran while one was open for 6% -> 7% of each run, Pallas kernels for 15% -> 21%
where the time goes in v4:
time: 283 us; the launch traced here: 282 us
  waiting for transfers between devices  129 us (46%)
  Pallas kernels  62.5 us (22%)
  starting transfers between devices  53.9 us (19%)
  between operations  13.3 us (5%)
  local copies, waits for them, and re-layouts  11.6 us (4%)
  other arithmetic  9.07 us (3%)
  matrix products  3.06 us (1%)
    ppermute x19, waiting for transfers between devices, send(): return lax.ppermute(value, AXES, move)  72.5 us
    all_gather x3, waiting for transfers between devices, along_z(): return lax.all_gather(value, 'ctx', axis=0, axis_index_groups=SAME_X)  55.5 us
    ppermute x19, starting transfers between devices, send(): return lax.ppermute(value, AXES, move)  53.8 us
    pallas_call x3, Pallas kernels, out_product(): pl.pallas_call(body, grid_spec=pltpu.PrefetchScalarGridSpec(num_scalar_pr...  25.3 us
    pallas_call x2, Pallas kernels, query_product(): pl.pallas_call(query_body, grid_spec=pltpu.PrefetchScalarGridSpec(num_sca...  19.4 us
    pallas_call x2, Pallas kernels, attend(): pl.pallas_call(functools.partial(attend_body, audio_length=audio_length,...  8.92 us
    pallas_call x3, Pallas kernels, finish(): pl.pallas_call(finish_body, grid=(2, columns // width), in_specs=[pl.Bloc...  8.9 us
  transfers between devices with their start and end apart: 22, of which 8 were waited for; matrix products, arithmetic and copies ran while one was open for 7% of the time, Pallas kernels for 21%

profile of v4, /device:TPU:0, one launch (start us, length us, event | category | flops | bytes accessed | tf_op | source)
XLA Modules:
  0.0 282.1 jit_solution(5285582135966296686)
XLA Ops:
  7.3 2.1 fusion.8
  9.4 3.0 %collective-permute-start = (bf16[640,256]{1,0:T(8,128)(2,1)}, bf16[640,256]{1,0:T(8,128)(2,1)}, u32[]{:S(2)}, u32[]{:S(2)}) collective-permute-start(bf16[640,256]{1,0:T(8,128)(2,1)} %get-tuple-element.33), channel_id=1, source_target_pairs={{0,8},{1,9},{2,10},{3,11},{4,12},{5,13},{6,14},{7,15},{8,0},{9,1},... | collective-permute-start | bytes 983048 | tf_op jit(solution)/shard_map/ppermute | solution.py:85
  12.4 3.9 %collective-permute-start.2 = (bf16[640,256]{1,0:T(8,128)(2,1)}, bf16[640,256]{1,0:T(8,128)(2,1)}, u32[]{:S(2)}, u32[]{:S(2)}) collective-permute-start(bf16[640,256]{1,0:T(8,128)(2,1)} %get-tuple-element.33), channel_id=1, source_target_pairs={{0,0},{1,1},{2,2},{3,3},{4,4},{5,5},{6,6},{7,7},{8,16},{9,17},{10,... | collective-permute-start | bytes 983048 | tf_op jit(solution)/shard_map/ppermute | solution.py:85
  18.8 1.6 collective-permute-start.5
  24.3 25.7 %collective-permute-done.8 = bf16[1,6656]{1,0:T(2,128)(2,1)S(1)} collective-permute-done((bf16[1,6656]{1,0:T(2,128)(2,1)S(1)}, bf16[1,6656]{1,0:T(2,128)(2,1)S(1)}, u32[]{:S(2)}, u32[]{:S(2)}) %collective-permute-start.8) | collective-permute-done | bytes 13344 | tf_op jit(solution)/shard_map/ppermute | solution.py:85
  51.0 3.9 %collective-permute-start.1 = (bf16[640,256]{1,0:T(8,128)(2,1)}, bf16[640,256]{1,0:T(8,128)(2,1)}, u32[]{:S(2)}, u32[]{:S(2)}) collective-permute-start(bf16[640,256]{1,0:T(8,128)(2,1)} %collective-permute-done), channel_id=1, source_target_pairs={{0,0},{1,1},{2,2},{3,3},{4,4},{5,5},{6,6},{7,7},{8,16},{9,17},{10,... | collective-permute-start | bytes 983048 | tf_op jit(solution)/shard_map/ppermute | solution.py:85
  55.8 1.4 collective-permute-start.3
  58.8 28.0 %collective-permute-start.10 = (bf16[4,6656]{1,0:T(4,128)(2,1)S(1)}, bf16[4,6656]{1,0:T(4,128)(2,1)S(1)}, u32[]{:S(2)}, u32[]{:S(2)}) collective-permute-start(bf16[4,6656]{1,0:T(4,128)(2,1)S(1)} %pad_maximum_fusion.7), channel_id=1, source_target_pairs={{0,16},{1,17},{2,18},{3,19},{4,20},{5,21},{6,22},{7,23},{8,24},{9,... | collective-permute-start | bytes 159752 | tf_op jit(solution)/shard_map/ppermute | solution.py:85
  86.8 23.7 %collective-permute-done.4 = bf16[640,256]{1,0:T(8,128)(2,1)S(1)} collective-permute-done((bf16[640,256]{1,0:T(8,128)(2,1)}, bf16[640,256]{1,0:T(8,128)(2,1)S(1)}, u32[]{:S(2)}, u32[]{:S(2)}) %collective-permute-start.4) | collective-permute-done | bytes 327712 | tf_op jit(solution)/shard_map/ppermute | solution.py:85
  110.6 2.2 pad_maximum_fusion.refs_8_
  112.8 32.0 %all-gather.7.cloned.1.call-done = bf16[2560,1280]{1,0:T(8,128)(2,1)} async-done(((bf16[640,1280]{1,0:T(8,128)(2,1)}), bf16[2560,1280]{1,0:T(8,128)(2,1)}) %all-gather.7.cloned.1.call-update) | async-done | bytes 6553616 | tf_op jit(solution)/shard_map/all_gather | solution.py:89
  144.7 9.9 %query_product.2 = (f32[512,640]{1,0:T(8,128)}, s16[544,640]{1,0:T(8,128)(2,1)}) custom-call(s32[8]{0:T(128)} %pad_add_fusion.place, bf16[512,5120]{1,0:T(8,128)(2,1)} %refs_3_.1, bf16[512,5120]{1,0:T(8,128)(2,1)} %refs_3_.1, bf16[512,5120]{1,0:T(8,128)(2,1)} %refs_3_.1, bf16[512,5120]{1,0:T(8,128)(2,1)} %refs_3_.1, bf16[2,1280,1280]{2,1,0:T(8,128)(2,1)} %bitcast.26, ...), custom_call_target="tpu_custom_call" | custom-call | flops 3355443200 | bytes 11796480 | tf_op jit(solution)/shard_map/query_product/pallas_call | solution.py:157
  154.6 1.5 collective-permute-start.13
  156.1 9.5 %query_product.3 = (f32[512,640]{1,0:T(8,128)}, s16[544,640]{1,0:T(8,128)(2,1)}) custom-call(s32[4]{0:T(128)} %pad_add_fusion.1.place, bf16[512,1280]{1,0:T(8,128)(2,1)} %copy-done.8, bf16[512,1280]{1,0:T(8,128)(2,1)} %collective-permute-done.6.refs_1_, bf16[2,1280,1280]{2,1,0:T(8,128)(2,1)} %bitcast.28, bf16[2,1280,1280]{2,1,0:T(8,128)(2,1)} %bitcast.29), custom_call_target="tpu_custom_call" | custom-call | flops 3355443200 | bytes 11796480 | tf_op jit(solution)/shard_map/query_product/pallas_call | solution.py:157
  167.5 2.1 convolution_convert_fusion.1.keys
  169.6 3.8 %collective-permute-done.13.received = s16[544,640]{1,0:T(8,128)(2,1)} collective-permute-done((s16[544,640]{1,0:T(8,128)(2,1)}, s16[544,640]{1,0:T(8,128)(2,1)}, u32[]{:S(2)}, u32[]{:S(2)}) %collective-permute-start.13) | collective-permute-done | bytes 696352 | tf_op jit(solution)/shard_map/ppermute | solution.py:85
  173.4 4.4 %attend.3.refs_4_ = bf16[512,640]{1,0:T(8,128)(2,1)} custom-call(f32[512,640]{1,0:T(8,128)} %get-tuple-element.20.kept, s16[544,640]{1,0:T(8,128)(2,1)} %collective-permute-done.13.received, bf16[64,640]{1,0:T(8,128)(2,1)} %convolution_convert_fusion.1.keys, bf16[64,640]{1,0:T(8,128)(2,1)} %convolution_convert_fusion.values, s32[512,1]{1,0:T(8,128)} %copy.17.speaker), custom_call_target="tpu_custom_call" | custom-call | flops 83886080 | bytes 3276800 | tf_op jit(solution)/shard_map/attend/pallas_call | solution.py:267
  177.9 1.5 collective-permute-start.14
  180.2 6.9 %collective-permute-done.7.received = s16[544,640]{1,0:T(8,128)(2,1)S(1)} collective-permute-done((s16[544,640]{1,0:T(8,128)(2,1)}, s16[544,640]{1,0:T(8,128)(2,1)S(1)}, u32[]{:S(2)}, u32[]{:S(2)}) %collective-permute-start.7) | collective-permute-done | bytes 696352 | tf_op jit(solution)/shard_map/ppermute | solution.py:85
  188.0 4.5 %attend.2.refs_0_ = bf16[512,640]{1,0:T(8,128)(2,1)} custom-call(f32[512,640]{1,0:T(8,128)} %get-tuple-element.18.kept, s16[544,640]{1,0:T(8,128)(2,1)} %copy-done.12, bf16[64,640]{1,0:T(8,128)(2,1)} %convolution_convert_fusion.1.keys, bf16[64,640]{1,0:T(8,128)(2,1)} %convolution_convert_fusion.values, s32[512,1]{1,0:T(8,128)} %copy.16.speaker), custom_call_target="tpu_custom_call" | custom-call | flops 83886080 | bytes 3276800 | tf_op jit(solution)/shard_map/attend/pallas_call | solution.py:267
  192.5 1.5 collective-permute-start.11
  196.1 12.3 %collective-permute-done.11.refs_2_ = bf16[512,640]{1,0:T(8,128)(2,1)S(1)} collective-permute-done((bf16[512,640]{1,0:T(8,128)(2,1)}, bf16[512,640]{1,0:T(8,128)(2,1)S(1)}, u32[]{:S(2)}, u32[]{:S(2)}) %collective-permute-start.11) | collective-permute-done | bytes 655392 | tf_op jit(solution)/shard_map/ppermute | solution.py:85
  210.2 12.6 %all-gather.11.cloned.1.call-done = bf16[2560,768]{1,0:T(8,128)(2,1)} async-done(((bf16[640,768]{1,0:T(8,128)(2,1)}), bf16[2560,768]{1,0:T(8,128)(2,1)}) %all-gather.11.cloned.1.call-update) | async-done | bytes 3932176 | tf_op jit(solution)/shard_map/all_gather | solution.py:89
  223.9 11.0 %out_product.4 = (f32[512,768]{1,0:T(8,128)}, s16[544,768]{1,0:T(8,128)(2,1)}) custom-call(s32[4]{0:T(128)} %iota_xor_fusion.place, bf16[512,640]{1,0:T(8,128)(2,1)} %attend.2.refs_0_, bf16[1024,640]{1,0:T(8,128)(2,1)} %collective-permute-done.12.refs_1_.refs_3_, bf16[512,640]{1,0:T(8,128)(2,1)} %copy-done.5, ...), custom_call_target="tpu_custom_call" | custom-call | flops 4026531840 | bytes 12320768 | tf_op jit(solution)/shard_map/out_product/pallas_call | solution.py:214
  234.9 1.5 collective-permute-start.17
  237.0 7.1 %out_product.5 = (f32[512,256]{1,0:T(8,128)}, s16[544,256]{1,0:T(8,128)(2,1)}) custom-call(s32[4]{0:T(128)} %broadcast_xor_fusion.place, bf16[512,640]{1,0:T(8,128)(2,1)} %attend.2.refs_0_, bf16[1024,640]{1,0:T(8,128)(2,1)} %collective-permute-done.12.refs_1_.refs_3_, bf16[512,640]{1,0:T(8,128)(2,1)} %copy-done.5, ...), custom_call_target="tpu_custom_call" | custom-call | flops 1342177280 | bytes 7602176 | tf_op jit(solution)/shard_map/out_product/pallas_call | solution.py:214
  244.7 10.9 %all-gather.9.cloned.1.call-done = bf16[2560,256]{1,0:T(8,128)(2,1)} async-done(((bf16[640,256]{1,0:T(8,128)(2,1)}), bf16[2560,256]{1,0:T(8,128)(2,1)}) %all-gather.9.cloned.1.call-update) | async-done | bytes 1310736 | tf_op jit(solution)/shard_map/all_gather | solution.py:89
  255.7 7.1 %out_product.3 = (f32[512,256]{1,0:T(8,128)}, s16[544,256]{1,0:T(8,128)(2,1)}) custom-call(s32[4]{0:T(128)} %iota_xor_fusion.place, bf16[512,640]{1,0:T(8,128)(2,1)} %attend.2.refs_0_, bf16[1024,640]{1,0:T(8,128)(2,1)} %collective-permute-done.12.refs_1_.refs_3_, bf16[512,640]{1,0:T(8,128)(2,1)} %copy-done.5, ...), custom_call_target="tpu_custom_call" | custom-call | flops 1342177280 | bytes 7602176 | tf_op jit(solution)/shard_map/out_product/pallas_call | solution.py:214
  262.8 1.5 collective-permute-start.16
  265.0 2.0 finish.3.refs_0_
  268.0 4.9 %finish.4.refs_0_ = bf16[512,1280]{1,0:T(8,128)(2,1)} custom-call(f32[512,768]{1,0:T(8,128)} %get-tuple-element.24.kept, s16[544,768]{1,0:T(8,128)(2,1)} %copy-done.6, s16[544,768]{1,0:T(8,128)(2,1)} %copy-done.6, bf16[512,1280]{1,0:T(8,128)(2,1)} %finish.3.refs_0_), custom_call_target="tpu_custom_call", output_to_operand_aliasing={{}: (3, {})} | custom-call | flops 786432 | bytes 3145728 | tf_op jit(solution)/shard_map/finish/pallas_call | solution.py:300
  273.6 2.0 finish.5
  (92 shorter events, 22.7 us)
Async XLA Ops:
  6.5 160.0 %copy-start = (bf16[768,1280]{1,0:T(8,128)(2,1)S(1)}, bf16[768,1280]{1,0:T(8,128)(2,1)}, u32[]{:S(2)}) copy-start(bf16[768,1280]{1,0:T(8,128)(2,1)} %param.14) | copy-start | bytes 5898244
  6.5 138.2 %all-gather.7.cloned.1.call-start = ((), (), s32[]{:S(2)}) async-start(), calls=%async_computation | async-start | bytes 8192000 | tf_op jit(solution)/shard_map/all_gather | solution.py:89
  7.3 215.5 %all-gather.11.cloned.1.call-start = ((), (), s32[]{:S(2)}) async-start(), calls=%async_computation.2 | async-start | bytes 4915200 | tf_op jit(solution)/shard_map/all_gather | solution.py:89
  9.4 41.7 %collective-permute-start = (bf16[640,256]{1,0:T(8,128)(2,1)}, bf16[640,256]{1,0:T(8,128)(2,1)}, u32[]{:S(2)}, u32[]{:S(2)}) collective-permute-start(bf16[640,256]{1,0:T(8,128)(2,1)} %get-tuple-element.33), channel_id=1, source_target_pairs={{0,8},{1,9},{2,10},{3,11},{4,12},{5,13},{6,14},{7,15},{8,0},{9,1},... | collective-permute-start | bytes 983048 | tf_op jit(solution)/shard_map/ppermute | solution.py:85
  12.4 43.4 %collective-permute-start.2 = (bf16[640,256]{1,0:T(8,128)(2,1)}, bf16[640,256]{1,0:T(8,128)(2,1)}, u32[]{:S(2)}, u32[]{:S(2)}) collective-permute-start(bf16[640,256]{1,0:T(8,128)(2,1)} %get-tuple-element.33), channel_id=1, source_target_pairs={{0,0},{1,1},{2,2},{3,3},{4,4},{5,5},{6,6},{7,7},{8,16},{9,17},{10,... | collective-permute-start | bytes 983048 | tf_op jit(solution)/shard_map/ppermute | solution.py:85
  17.7 2.7 copy-start.7
  18.8 2.7 copy-start.15
  18.8 2.8 copy-start.14
  18.8 3.2 %copy-start.16 = (s32[2]{0:T(128)S(1)}, s32[2]{0:T(128)}, u32[]{:S(2)}) copy-start(s32[2]{0:T(128)} %constant.56) | copy-start | bytes 28
  18.8 3.3 %copy-start.13 = (bf16[2,4,768]{2,1,0:T(4,128)(2,1)S(1)}, bf16[2,4,768]{2,1,0:T(4,128)(2,1)}, u32[]{:S(2)}) copy-start(bf16[2,4,768]{2,1,0:T(4,128)(2,1)} %param.12) | copy-start | bytes 36868
  18.8 39.7 %collective-permute-start.5 = (bf16[512,1280]{1,0:T(8,128)(2,1)}, bf16[512,1280]{1,0:T(8,128)(2,1)S(1)}, u32[]{:S(2)}, u32[]{:S(2)}) collective-permute-start(bf16[512,1280]{1,0:T(8,128)(2,1)} %pad_maximum_fusion.1), channel_id=1, source_target_pairs={{0,4},{1,5},{2,6},{3,7},{4,0},{5,1},{6,2},{7,3},{8,12},{9,13},{10,... | collective-permute-start | bytes 3932168 | tf_op jit(solution)/shard_map/ppermute | solution.py:85
  21.5 234.2 %all-gather.9.cloned.1.call-start = ((), (), s32[]{:S(2)}) async-start(), calls=%async_computation.1 | async-start | bytes 1638400 | tf_op jit(solution)/shard_map/all_gather | solution.py:89
  22.2 27.7 %collective-permute-start.8 = (bf16[1,6656]{1,0:T(2,128)(2,1)S(1)}, bf16[1,6656]{1,0:T(2,128)(2,1)S(1)}, u32[]{:S(2)}, u32[]{:S(2)}) collective-permute-start(bf16[1,6656]{1,0:T(2,128)(2,1)S(1)} %broadcast_in_dim.2), channel_id=1, source_target_pairs={{0,4},{1,5},{2,6},{3,7},{4,0},{5,1},{6,2},{7,3},{8,12},{9,13},{10,... | collective-permute-start | bytes 39944 | tf_op jit(solution)/shard_map/ppermute | solution.py:85
  50.0 8.7 %collective-permute-start.9 = (bf16[2,6656]{1,0:T(2,128)(2,1)S(1)}, bf16[2,6656]{1,0:T(2,128)(2,1)S(1)}, u32[]{:S(2)}, u32[]{:S(2)}) collective-permute-start(bf16[2,6656]{1,0:T(2,128)(2,1)S(1)} %pad_maximum_fusion.9), channel_id=1, source_target_pairs={{0,8},{1,9},{2,10},{3,11},{4,12},{5,13},{6,14},{7,15},{8,0},{9,1},... | collective-permute-start | bytes 79880 | tf_op jit(solution)/shard_map/ppermute | solution.py:85
  51.0 6.2 %collective-permute-start.1 = (bf16[640,256]{1,0:T(8,128)(2,1)}, bf16[640,256]{1,0:T(8,128)(2,1)}, u32[]{:S(2)}, u32[]{:S(2)}) collective-permute-start(bf16[640,256]{1,0:T(8,128)(2,1)} %collective-permute-done), channel_id=1, source_target_pairs={{0,0},{1,1},{2,2},{3,3},{4,4},{5,5},{6,6},{7,7},{8,16},{9,17},{10,... | collective-permute-start | bytes 983048 | tf_op jit(solution)/shard_map/ppermute | solution.py:85
  55.8 54.8 %copy-start.9 = (bf16[1,640,256]{2,1,0:T(8,128)(2,1)S(1)}, bf16[1,640,256]{2,1,0:T(8,128)(2,1)}, u32[]{:S(2)}) copy-start(bf16[1,640,256]{2,1,0:T(8,128)(2,1)} %get-tuple-element.32) | copy-start | bytes 983044
  55.8 31.0 %collective-permute-start.3 = (bf16[640,256]{1,0:T(8,128)(2,1)}, bf16[640,256]{1,0:T(8,128)(2,1)S(1)}, u32[]{:S(2)}, u32[]{:S(2)}) collective-permute-start(bf16[640,256]{1,0:T(8,128)(2,1)} %collective-permute-done.2), channel_id=1, source_target_pairs={{8,0},{9,1},{10,2},{11,3},{12,4},{13,5},{14,6},{15,7},{16,24},{17,... | collective-permute-start | bytes 983048 | tf_op jit(solution)/shard_map/ppermute | solution.py:85
  57.3 53.3 %collective-permute-start.4 = (bf16[640,256]{1,0:T(8,128)(2,1)}, bf16[640,256]{1,0:T(8,128)(2,1)S(1)}, u32[]{:S(2)}, u32[]{:S(2)}) collective-permute-start(bf16[640,256]{1,0:T(8,128)(2,1)} %collective-permute-done.1), channel_id=1, source_target_pairs={{8,0},{9,1},{10,2},{11,3},{12,4},{13,5},{14,6},{15,7},{16,24},{17,... | collective-permute-start | bytes 983048 | tf_op jit(solution)/shard_map/ppermute | solution.py:85
  58.6 54.2 %copy-start.8 = (bf16[512,1280]{1,0:T(8,128)(2,1)}, bf16[512,1280]{1,0:T(8,128)(2,1)S(1)}, u32[]{:S(2)}) copy-start(bf16[512,1280]{1,0:T(8,128)(2,1)S(1)} %collective-permute-done.5.refs_0_) | copy-start | bytes 3932164
  58.6 97.5 %collective-permute-start.6 = (bf16[512,1280]{1,0:T(8,128)(2,1)S(1)}, bf16[512,1280]{1,0:T(8,128)(2,1)}, u32[]{:S(2)}, u32[]{:S(2)}) collective-permute-start(bf16[512,1280]{1,0:T(8,128)(2,1)S(1)} %collective-permute-done.5.refs_0_), channel_id=1, source_target_pairs={{0,1},{1,0},{2,3},{3,2},{4,5},{5,4},{6,7},{7,6},{8,9},{9,8},{10,11... | collective-permute-start | bytes 3932168 | tf_op jit(solution)/shard_map/ppermute | solution.py:85
  58.8 107.6 %collective-permute-start.10 = (bf16[4,6656]{1,0:T(4,128)(2,1)S(1)}, bf16[4,6656]{1,0:T(4,128)(2,1)S(1)}, u32[]{:S(2)}, u32[]{:S(2)}) collective-permute-start(bf16[4,6656]{1,0:T(4,128)(2,1)S(1)} %pad_maximum_fusion.7), channel_id=1, source_target_pairs={{0,16},{1,17},{2,18},{3,19},{4,20},{5,21},{6,22},{7,23},{8,24},{9,... | collective-permute-start | bytes 159752 | tf_op jit(solution)/shard_map/ppermute | solution.py:85
  154.6 18.8 %collective-permute-start.13 = (s16[544,640]{1,0:T(8,128)(2,1)}, s16[544,640]{1,0:T(8,128)(2,1)}, u32[]{:S(2)}, u32[]{:S(2)}) collective-permute-start(s16[544,640]{1,0:T(8,128)(2,1)} %get-tuple-element.21), channel_id=1, source_target_pairs={{0,4},{1,5},{2,6},{3,7},{4,0},{5,1},{6,2},{7,3},{8,12},{9,13},{10,... | collective-permute-start | bytes 2088968 | tf_op jit(solution)/shard_map/ppermute | solution.py:85
  165.6 21.5 %collective-permute-start.7 = (s16[544,640]{1,0:T(8,128)(2,1)}, s16[544,640]{1,0:T(8,128)(2,1)S(1)}, u32[]{:S(2)}, u32[]{:S(2)}) collective-permute-start(s16[544,640]{1,0:T(8,128)(2,1)} %get-tuple-element.19), channel_id=1, source_target_pairs={{0,4},{1,5},{2,6},{3,7},{4,0},{5,1},{6,2},{7,3},{8,12},{9,13},{10,... | collective-permute-start | bytes 2088968 | tf_op jit(solution)/shard_map/ppermute | solution.py:85
  177.9 16.1 %collective-permute-start.14 = (bf16[512,640]{1,0:T(8,128)(2,1)}, bf16[512,640]{1,0:T(8,128)(2,1)S(1)}, u32[]{:S(2)}, u32[]{:S(2)}) collective-permute-start(bf16[512,640]{1,0:T(8,128)(2,1)} %attend.3.refs_4_), channel_id=1, source_target_pairs={{0,2},{1,3},{2,0},{3,1},{4,6},{5,7},{6,4},{7,5},{8,10},{9,11},{10,... | collective-permute-start | bytes 1966088 | tf_op jit(solution)/shard_map/ppermute | solution.py:85
  188.0 6.9 %copy-start.2 = (bf16[512,640]{1,0:T(8,128)(2,1)S(1)}, bf16[512,640]{1,0:T(8,128)(2,1)}, u32[]{:S(2)}) copy-start(bf16[512,640]{1,0:T(8,128)(2,1)} %attend.3.refs_4_) | copy-start | bytes 1966084
  192.5 15.9 %copy-start.3 = (bf16[512,640]{1,0:T(8,128)(2,1)S(1)}, bf16[512,640]{1,0:T(8,128)(2,1)}, u32[]{:S(2)}) copy-start(bf16[512,640]{1,0:T(8,128)(2,1)} %attend.2.refs_0_) | copy-start | bytes 1966084
  192.5 15.9 %collective-permute-start.11 = (bf16[512,640]{1,0:T(8,128)(2,1)}, bf16[512,640]{1,0:T(8,128)(2,1)S(1)}, u32[]{:S(2)}, u32[]{:S(2)}) collective-permute-start(bf16[512,640]{1,0:T(8,128)(2,1)} %attend.2.refs_0_), channel_id=1, source_target_pairs={{0,2},{1,3},{2,0},{3,1},{4,6},{5,7},{6,4},{7,5},{8,10},{9,11},{10,... | collective-permute-start | bytes 1966088 | tf_op jit(solution)/shard_map/ppermute | solution.py:85
  196.1 26.7 %collective-permute-start.15 = (bf16[1024,640]{1,0:T(8,128)(2,1)}, bf16[1024,640]{1,0:T(8,128)(2,1)S(1)}, u32[]{:S(2)}, u32[]{:S(2)}) collective-permute-start(bf16[1024,640]{1,0:T(8,128)(2,1)} %pad_maximum_fusion.3), channel_id=1, source_target_pairs={{0,1},{1,0},{2,3},{3,2},{4,5},{5,4},{6,7},{7,6},{8,9},{9,8},{10,11... | collective-permute-start | bytes 3932168 | tf_op jit(solution)/shard_map/ppermute | solution.py:85
  209.7 13.1 %collective-permute-start.12 = (bf16[1024,640]{1,0:T(8,128)(2,1)}, bf16[1024,640]{1,0:T(8,128)(2,1)}, u32[]{:S(2)}, u32[]{:S(2)}) collective-permute-start(bf16[1024,640]{1,0:T(8,128)(2,1)} %pad_maximum_fusion.2), channel_id=1, source_target_pairs={{0,1},{1,0},{2,3},{3,2},{4,5},{5,4},{6,7},{7,6},{8,9},{9,8},{10,11... | collective-permute-start | bytes 3932168 | tf_op jit(solution)/shard_map/ppermute | solution.py:85
  234.9 32.1 %collective-permute-start.17 = (s16[544,768]{1,0:T(8,128)(2,1)}, s16[544,768]{1,0:T(8,128)(2,1)S(1)}, u32[]{:S(2)}, u32[]{:S(2)}) collective-permute-start(s16[544,768]{1,0:T(8,128)(2,1)} %get-tuple-element.25), channel_id=1, source_target_pairs={{0,4},{1,5},{2,6},{3,7},{4,0},{5,1},{6,2},{7,3},{8,12},{9,13},{10,... | collective-permute-start | bytes 2506760 | tf_op jit(solution)/shard_map/ppermute | solution.py:85
  244.1 20.2 %collective-permute-start.18 = (s16[544,256]{1,0:T(8,128)(2,1)}, s16[544,256]{1,0:T(8,128)(2,1)S(1)}, u32[]{:S(2)}, u32[]{:S(2)}) collective-permute-start(s16[544,256]{1,0:T(8,128)(2,1)} %get-tuple-element.28), channel_id=1, source_target_pairs={{0,4},{1,5},{2,6},{3,7},{4,0},{5,1},{6,2},{7,3},{8,12},{9,13},{10,... | collective-permute-start | bytes 835592 | tf_op jit(solution)/shard_map/ppermute | solution.py:85
  262.8 10.1 %collective-permute-start.16 = (s16[544,256]{1,0:T(8,128)(2,1)}, s16[544,256]{1,0:T(8,128)(2,1)S(1)}, u32[]{:S(2)}, u32[]{:S(2)}) collective-permute-start(s16[544,256]{1,0:T(8,128)(2,1)} %get-tuple-element.23), channel_id=1, source_target_pairs={{0,4},{1,5},{2,6},{3,7},{4,0},{5,1},{6,2},{7,3},{8,12},{9,13},{10,... | collective-permute-start | bytes 835592 | tf_op jit(solution)/shard_map/ppermute | solution.py:85
  (7 other events, 6.5 us)
Sparse Core Ops, SparseCore 0:
  8.9 135.7 all-gather.6
  146.3 76.4 all-gather.10
  224.4 31.2 all-gather.8

commit v5 on v2

--- a/solution.py
+++ b/solution.py
@@ -10,8 +10,8 @@
 HD = 128
 SPK = 2
 AXES = ("ctx", "head")
-QUERY_CHUNKS = (3, 2)
-OUT_CHUNKS = (6, 4)
+GATHERED_HEADS = 3
+OUT_CHUNKS = (8, 2)
 
 
 def add_rows(left_rows, shard_piece):
@@ -76,6 +76,8 @@
 ACROSS_CORE = pairs(4, lambda z, x, h: (z, x, h ^ 1))
 ONE_ALONG = pairs(4, lambda z, x, h: (z ^ 1, x, h))
 TWO_ALONG = pairs(4, lambda z, x, h: (z ^ 2, x, h))
+MID_TO_END = [pair for pair in ONE_ALONG if pair[0] // 8 in (1, 2)]
+MID_TO_MID = pairs(4, lambda z, x, h: (3 - z if z in (1, 2) else z, x, h))
 SAME_X = [[0, 2, 4, 6], [1, 3, 5, 7]]
 
 
@@ -87,7 +89,99 @@
     return lax.all_gather(value, "ctx", axis=0, axis_index_groups=SAME_X)
 
 
-def product(place, lefts, weights, k_sizes):
+def diagonal(groups):
+    shape = (groups * 128, 128)
+    row = lax.broadcasted_iota(jnp.int32, shape, 0) % 128
+    return row == lax.broadcasted_iota(jnp.int32, shape, 1)
+
+
+def pack(value, packed):
+    rows, columns = value.shape
+    groups = rows // 128
+    peak = jnp.max(jnp.abs(value), axis=1, keepdims=True)
+    power = jnp.clip(jnp.floor(jnp.log2(jnp.maximum(peak, 1e-30))) + 1.0, -90.0, 120.0)
+    scaled = jnp.clip(jnp.round(value * jnp.exp2(15.0 - power)), -32767.0, 32767.0)
+    packed[:rows, :] = scaled.astype(jnp.int32).astype(jnp.int16)
+    spread = jnp.where(diagonal(groups), power, 0.0).reshape(groups, 128, 128).sum(axis=1)
+    spread = jnp.concatenate([spread, jnp.zeros((16 - groups, 128), jnp.float32)], axis=0)
+    packed[rows:, :128] = spread.astype(jnp.int32).astype(jnp.int16)
+    packed[rows:, 128:] = jnp.zeros((16, columns - 128), jnp.int16)
+
+
+def row_scale(packed):
+    groups = (packed.shape[0] - 16) // 128
+    spread = packed[groups * 128 :, :128].astype(jnp.int32).astype(jnp.float32)[:groups]
+    spread = jnp.broadcast_to(spread[:, None, :], (groups, 128, 128)).reshape(groups * 128, 128)
+    power = jnp.sum(jnp.where(diagonal(groups), spread, 0.0), axis=1, keepdims=True)
+    return jnp.exp2(power - 15.0)
+
+
+def unpack(packed, scale):
+    return packed[: packed.shape[0] - 16, :].astype(jnp.int32).astype(jnp.float32) * scale
+
+
+def query_body(place, *refs):
+    own, near, (keep_weights, send_weights, kept, sent) = refs[:4], refs[4:8], refs[8:]
+
+    def write(lefts):
+        for weights, result in ((send_weights, sent), (keep_weights, kept)):
+            total = None
+            for j in range(4):
+                term = jnp.dot(
+                    lefts[j][...], weights[place[6 + j]], preferred_element_type=jnp.float32
+                )
+                total = term if total is None else total + term
+            result[...] = total
+
+    first_group = pl.program_id(0) < pl.num_programs(0) // 2
+    pl.when(first_group)(lambda: write(own))
+    pl.when(jnp.logical_not(first_group))(lambda: write(near))
+
+
+def query_product(place, video_rows, near, weights):
+    rows = video_rows.shape[0]
+    depth, columns = weights.shape[1:]
+    step = rows // 2
+    half = columns // 2
+    own_specs = [
+        pl.BlockSpec(
+            (step, depth),
+            functools.partial(lambda j, i, place: (jnp.minimum(i, 1), place[j]), j),
+        )
+        for j in range(4)
+    ]
+    near_specs = [
+        pl.BlockSpec(
+            (step, depth), functools.partial(lambda j, i, place: (jnp.maximum(i - 2, 0), j % 2), j)
+        )
+        for j in range(4)
+    ]
+    part = jax.ShapeDtypeStruct((2 * rows, half), jnp.float32)
+    return pl.pallas_call(
+        query_body,
+        grid_spec=pltpu.PrefetchScalarGridSpec(
+            num_scalar_prefetch=1,
+            grid=(4,),
+            in_specs=own_specs
+            + near_specs
+            + [
+                pl.BlockSpec((4, depth, half), lambda i, place: (0, 0, place[4])),
+                pl.BlockSpec((4, depth, half), lambda i, place: (0, 0, place[5])),
+            ],
+            out_specs=[pl.BlockSpec((step, half), lambda i, place: (i, 0))] * 2,
+        ),
+        out_shape=[part, part],
+        cost_estimate=pl.CostEstimate(
+            flops=16 * rows * depth * columns,
+            transcendentals=0,
+            bytes_accessed=8 * (2 * rows + columns) * depth + 8 * rows * columns,
+        ),
+        name="query_product",
+    )(place, *([video_rows] * 4), near[0], near[0], near[1], near[1], weights, weights)
+
+
+def out_body(place, *refs, k_sizes):
+    *lefts, weights, kept, sent = refs
     total = None
     for j in range(4):
         first = 0
@@ -96,75 +190,23 @@
             term = jnp.dot(lefts[i * 4 + j][...], right, preferred_element_type=jnp.float32)
             total = term if total is None else total + term
             first += size
-    return total
-
-
-def query_body(place, *refs):
-    own, near = refs[:4], refs[4:8]
-    weights, kept, sent = refs[8:]
-    half = kept.shape[1]
-
-    def write(lefts):
-        total = product(place, lefts, weights, (weights.shape[1],))
-        kept[...] = total[:, :half]
-        sent[...] = total[:, half:]
-
-    first_group = pl.program_id(0) < pl.num_programs(0) // 2
-    pl.when(first_group)(lambda: write(own))
-    pl.when(jnp.logical_not(first_group))(lambda: write(near))
-
-
-def query_product(place, video_rows, near, weights):
-    rows = video_rows.shape[0]
-    depth, columns = weights.shape[1:]
-    step = rows // 2
-    own_specs = [
-        pl.BlockSpec(
-            (step, depth),
-            functools.partial(lambda j, i, place: (jnp.minimum(i, 1), place[4 + j]), j),
-        )
-        for j in range(4)
-    ]
-    near_specs = [
-        pl.BlockSpec((step, depth), lambda i, place: (jnp.maximum(i - 2, 0), 0)) for _ in range(4)
-    ]
-    half = columns // 2
-    part = jax.ShapeDtypeStruct((2 * rows, half), jnp.float32)
-    return pl.pallas_call(
-        query_body,
-        grid_spec=pltpu.PrefetchScalarGridSpec(
-            num_scalar_prefetch=1,
-            grid=(4,),
-            in_specs=own_specs
-            + near_specs
-            + [pl.BlockSpec(weights.shape, lambda i, place: (0, 0, 0))],
-            out_specs=[pl.BlockSpec((step, half), lambda i, place: (i, 0))] * 2,
-        ),
-        out_shape=[part, part],
-        cost_estimate=pl.CostEstimate(
-            flops=16 * rows * depth * columns,
-            transcendentals=0,
-            bytes_accessed=8 * (2 * rows + columns) * depth + 8 * rows * columns,
-        ),
-        name="query_product",
-    )(place, *([video_rows] * 4), *near, weights)
-
-
-def out_body(place, *refs, k_sizes):
-    *lefts, weights, kept, sent = refs
-    total = product(place, lefts, weights, k_sizes)
-    pl.when(pl.program_id(0) < 2)(lambda: kept.__setitem__(..., total))
-    pl.when(pl.program_id(0) >= 2)(lambda: sent.__setitem__(..., total))
-
-
-def out_product(place, lefts, weights, k_sizes):
-    rows = lefts[0].shape[0]
+    pl.when(pl.program_id(0) < 2)(lambda: pack(total, sent))
+    pl.when(pl.program_id(0) >= 2)(lambda: kept.__setitem__(..., total))
+
+
+def out_product(place, groups, weights):
+    rows = groups[0][0].shape[0]
+    k_sizes = tuple(group[0].shape[1] for group in groups)
     columns = weights.shape[2]
     step = rows // 4
     left_specs = [
-        pl.BlockSpec((step, size), lambda i, place: (i, 0)) for size in k_sizes for _ in range(4)
+        pl.BlockSpec(
+            (step, size), functools.partial(lambda skip, i, place: ((i + 2) % 4 + skip, 0), skip)
+        )
+        for size in k_sizes
+        for skip in (0, 0, 0, 4)
     ]
-    part = jax.ShapeDtypeStruct((rows // 2, columns), jnp.float32)
+    lefts = [piece for own, core, over_y in groups for piece in (own, core, over_y, core)]
     return pl.pallas_call(
         functools.partial(out_body, k_sizes=k_sizes),
         grid_spec=pltpu.PrefetchScalarGridSpec(
@@ -172,11 +214,14 @@
             grid=(4,),
             in_specs=left_specs + [pl.BlockSpec(weights.shape, lambda i, place: (0, 0, 0))],
             out_specs=[
-                pl.BlockSpec((step, columns), lambda i, place: (jnp.minimum(i, 1), 0)),
                 pl.BlockSpec((step, columns), lambda i, place: (jnp.maximum(i - 2, 0), 0)),
+                pl.BlockSpec((step + 16, columns), lambda i, place: (jnp.minimum(i, 1), 0)),
             ],
         ),
-        out_shape=[part, part],
+        out_shape=[
+            jax.ShapeDtypeStruct((rows // 2, columns), jnp.float32),
+            jax.ShapeDtypeStruct((2 * (step + 16), columns), jnp.int16),
+        ],
         cost_estimate=pl.CostEstimate(
             flops=8 * rows * sum(k_sizes) * columns,
             transcendentals=0,
@@ -236,9 +281,40 @@
     )(kept, received, keys, values, speaker)
 
 
+def finish_body(kept, received, scales, *refs):
+    refs[-1][...] = (kept[...] + unpack(received, row_scale(scales))).astype(
+        jnp.bfloat16
+    )
+
+
+def finish(kept, received, first, whole, result):
+    rows, columns = kept.shape
+    step = rows // 2
+    width = 2 * HD
+    at = lambda i, j: (i, j)
+    given = [] if result is None else [result]
+    return pl.pallas_call(
+        finish_body,
+        grid=(2, columns // width),
+        in_specs=[
+            pl.BlockSpec((step, width), at),
+            pl.BlockSpec((step + 16, width), at),
+            pl.BlockSpec((step + 16, 128), lambda i, j: (i, 0)),
+        ]
+        + [pl.BlockSpec(memory_space=pl.ANY)] * len(given),
+        out_specs=pl.BlockSpec((step, width), lambda i, j: (i, first // width + j)),
+        out_shape=jax.ShapeDtypeStruct((rows, whole), jnp.bfloat16),
+        input_output_aliases={3: 0} if given else {},
+        cost_estimate=pl.CostEstimate(
+            flops=2 * rows * columns, transcendentals=0, bytes_accessed=8 * rows * columns
+        ),
+        name="finish",
+    )(kept, received, received, *given)
+
+
 def head_pieces(value):
     over_y = send(value, ACROSS_Y)
-    return [value, send(value, ACROSS_CORE), over_y, send(over_y, ACROSS_CORE)]
+    return value, send(jnp.concatenate([value, over_y], axis=0), ACROSS_CORE), over_y
 
 
 def plane_shards(video_rows, w_query, w_output, audio_tokens, w_key, w_value, row_lists, row_counts):
@@ -248,31 +324,44 @@
     ctx = lax.axis_index("ctx").astype(jnp.int32)
     h = lax.axis_index("head").astype(jnp.int32)
     x = ctx % 2
-    k_sizes = tuple(heads * HD for heads in QUERY_CHUNKS)
-
-    query_weights = []
-    first = 0
-    for size in k_sizes:
-        query_weights.append(
-            along_z(
-                jnp.concatenate(
-                    [
-                        lax.dynamic_slice(w_query, (0, x * block + first), (block, size)),
-                        lax.dynamic_slice(w_query, (0, (1 - x) * block + first), (block, size)),
-                    ],
-                    axis=1,
-                )
-            )
-        )
-        first += size
-
-    near = head_pieces(
-        send(
-            lax.dynamic_slice(video_rows, (0, (2 * h + 1 - x) * block), (rows, block)), ACROSS_X
-        )
-    )
-    order = jnp.arange(4, dtype=jnp.int32) ^ h
-    place = jnp.concatenate([order, 2 * order + x])
+    core = h % 2
+
+    z = ctx // 2
+    is_mid = (z == 1) | (z == 2)
+
+    def of_blocks(value, first, last):
+        first, last = first * HD, last * HD
+        return jnp.concatenate(
+            [value[:, first:last], value[:, block + first : block + last]], axis=1
+        )
+
+    heads_block = block // HD
+    gathered_weights = along_z(of_blocks(w_query, 0, GATHERED_HEADS))
+    piece = of_blocks(w_query, GATHERED_HEADS, heads_block)
+    swapped = send(piece, ONE_ALONG)
+    opposite = send(piece, MID_TO_MID)
+    last = send(swapped, MID_TO_MID)
+    to_end = send(opposite, MID_TO_END)
+    last_to_end = send(last, MID_TO_END)
+    hopped_weights = jnp.stack(
+        [
+            piece,
+            swapped,
+            jnp.where(is_mid, last, to_end),
+            jnp.where(is_mid, opposite, last_to_end),
+        ]
+    )
+
+    near_block = lambda plane: lax.dynamic_slice(
+        video_rows, (0, (2 * plane + 1 - x) * block), (rows, block)
+    )
+    near_half = send(
+        jnp.concatenate([near_block(2 * core), near_block(2 * core + 1)], axis=1), ACROSS_X
+    )
+    near = [near_half, send(near_half, ACROSS_CORE)]
+    planes = jnp.arange(4, dtype=jnp.int32)
+    by_core = planes ^ (2 * core)
+    place = jnp.concatenate([2 * by_core + x, jnp.stack([x, 1 - x])])
 
     position = jnp.arange(rows, dtype=jnp.int32)
     named = (row_lists[:, :, None] == position[None, None, :]) & (
@@ -292,34 +381,43 @@
         .reshape(-1, audio_width)
     )
     audio_length = whole_audio.shape[0] // SPK
-    speaker = gathered[:2, SPK * tokens * audio_width :].astype(jnp.int32).reshape(-1, 1)
-    key_rows = add_rows(
-        whole_audio, lax.dynamic_slice(w_key, (0, x * block), (audio_width, block))
-    ).astype(jnp.bfloat16)
-    value_rows = add_rows(
-        whole_audio, lax.dynamic_slice(w_value, (0, x * block), (audio_width, block))
-    ).astype(jnp.bfloat16)
-
+    speakers = gathered[:2, SPK * tokens * audio_width :].astype(jnp.int32)
+    own_block = lambda weights: lax.dynamic_slice(weights, (0, x * block), (audio_width, block))
+    key_rows = add_rows(whole_audio, own_block(w_key)).astype(jnp.bfloat16)
+    value_rows = add_rows(whole_audio, own_block(w_value)).astype(jnp.bfloat16)
+
+    speaker = speakers.reshape(-1, 1)
     attended = []
-    first = 0
-    for weights, size in zip(query_weights, k_sizes):
-        at = slice(first, first + size)
-        kept, sent = query_product(place, video_rows, near, weights)
-        received = send(sent, ACROSS_X)
-        attended += head_pieces(
-            attend(kept, received, key_rows[:, at], value_rows[:, at], speaker, audio_length)
-        )
-        first += size
-
-    results = []
+    for weights, order, first, last in (
+        (gathered_weights, by_core, 0, GATHERED_HEADS),
+        (hopped_weights, by_core ^ z, GATHERED_HEADS, heads_block),
+    ):
+        at = slice(first * HD, last * HD)
+        kept, sent = query_product(
+            jnp.concatenate([place, order]), video_rows, near, weights
+        )
+        attended.append(
+            head_pieces(
+                attend(
+                    kept,
+                    send(sent, ACROSS_X),
+                    key_rows[:, at],
+                    value_rows[:, at],
+                    speaker,
+                    audio_length,
+                )
+            )
+        )
+
+    result = None
     first = 0
     for heads in OUT_CHUNKS:
         size = heads * HD
-        weights = along_z(lax.slice_in_dim(w_output, first, first + size, axis=1))
-        kept, sent = out_product(place, attended, weights, k_sizes)
-        results.append((kept + send(sent, ACROSS_X)).astype(jnp.bfloat16))
+        weights = along_z(w_output[:, first : first + size])
+        kept, sent = out_product(planes ^ h, attended, weights)
+        result = finish(kept, send(sent, ACROSS_X), first, w_output.shape[1], result)
         first += size
-    return jnp.concatenate(results, axis=1)
+    return result
 
 
 def solution(mesh):

time: 322 us -> 276 us (0.86)
  waiting for transfers between devices: 210 us -> 131 us
  starting transfers between devices: 18.9 us -> 31 us
  Pallas kernels: 50.1 us -> 60 us
  other arithmetic: 9.07 us -> 15.3 us
  local copies, waits for them, and re-layouts: 16.5 us -> 20.6 us
    all_gather x4 -> x3, waiting for transfers between devices: 143 us -> 66.3 us  [along_z(): return lax.all_gather(value, 'ctx', axis=0, axis_index_groups=SAME_X)]
    ppermute x17 -> x18, starting transfers between devices: 18.8 us -> 31 us  [send(): return lax.ppermute(value, AXES, move)]
    pallas_call x0 -> x2, Pallas kernels: none -> 8.17 us  [finish(): pl.pallas_call(finish_body, grid=(2, columns // width), in_specs=[pl.Bloc...]
    another operation x0 -> x4, other arithmetic: none -> 6.5 us  [plane_shards(): jnp.stack([piece, swapped, jnp.where(is_mid, last, to_end), jnp.where(is_...]
    unnamed x32 -> x42, local copies, waits for them, and re-layouts: 2.28 us -> 6.15 us
    slice x2 -> x4, local copies, waits for them, and re-layouts: 4.22 us -> 6.79 us  [the longest x2 4.18 us: plane_shards(): weights = along_z(w_output[:, first:first + size])]
    ppermute x17 -> x18, waiting for transfers between devices: 66.7 us -> 65.1 us  [send(): return lax.ppermute(value, AXES, move)]
  transfers between devices with their start and end apart: 21 -> 21, of which waited for: 10 -> 10; matrix products, arithmetic and copies ran while one was open for 7% -> 11% of each run, Pallas kernels for 16% -> 21%
where the time goes in v5:
time: 276 us; the launch traced here: 275 us
  waiting for transfers between devices  131 us (47%)
  Pallas kernels  60 us (22%)
  starting transfers between devices  31 us (11%)
  local copies, waits for them, and re-layouts  20.6 us (7%)
  other arithmetic  15.3 us (6%)
  between operations  13.3 us (5%)
    all_gather x3, waiting for transfers between devices, along_z(): return lax.all_gather(value, 'ctx', axis=0, axis_index_groups=SAME_X)  66.3 us
    ppermute x18, waiting for transfers between devices, send(): return lax.ppermute(value, AXES, move)  65.1 us
    ppermute x18, starting transfers between devices, send(): return lax.ppermute(value, AXES, move)  31 us
    pallas_call x2, Pallas kernels, query_product(): pl.pallas_call(query_body, grid_spec=pltpu.PrefetchScalarGridSpec(num_sca...  20.6 us
    pallas_call x2, Pallas kernels, out_product(): pl.pallas_call(functools.partial(out_body, k_sizes=k_sizes), grid_spec=pl...  20.2 us
    pallas_call x2, Pallas kernels, attend(): pl.pallas_call(functools.partial(attend_body, audio_length=audio_length,...  11 us
    pallas_call x2, Pallas kernels, finish(): pl.pallas_call(finish_body, grid=(2, columns // width), in_specs=[pl.Bloc...  8.17 us
    another operation x4, other arithmetic, plane_shards(): jnp.stack([piece, swapped, jnp.where(is_mid, last, to_end), jnp.where(is_...  6.5 us
  transfers between devices with their start and end apart: 21, of which 10 were waited for; matrix products, arithmetic and copies ran while one was open for 11% of the time, Pallas kernels for 21%

profile of v5, /device:TPU:0, one launch (start us, length us, event | category | flops | bytes accessed | tf_op | source)
XLA Modules:
  0.0 274.5 jit_solution(17098967205872049188)
XLA Ops:
  6.5 1.4 fusion.9
  9.1 2.5 slice.47
  14.3 3.0 %collective-permute-start = (bf16[512,1280]{1,0:T(8,128)(2,1)}, bf16[512,1280]{1,0:T(8,128)(2,1)S(1)}, u32[]{:S(2)}, u32[]{:S(2)}) collective-permute-start(bf16[512,1280]{1,0:T(8,128)(2,1)} %pad_maximum_fusion.2), channel_id=1, source_target_pairs={{0,4},{1,5},{2,6},{3,7},{4,0},{5,1},{6,2},{7,3},{8,12},{9,13},{10,... | collective-permute-start | bytes 3932168 | tf_op jit(solution)/shard_map/ppermute | solution.py:85
  19.6 1.5 collective-permute-start.8
  21.1 6.5 %collective-permute-start.10 = (bf16[640,512]{1,0:T(8,128)(2,1)}, bf16[640,512]{1,0:T(8,128)(2,1)}, u32[]{:S(2)}, u32[]{:S(2)}) collective-permute-start(bf16[640,512]{1,0:T(8,128)(2,1)} %get-tuple-element.30), channel_id=1, source_target_pairs={{0,0},{1,1},{2,2},{3,3},{4,4},{5,5},{6,6},{7,7},{8,16},{9,17},{10,... | collective-permute-start | bytes 1966088 | tf_op jit(solution)/shard_map/ppermute | solution.py:85
  30.2 16.3 %collective-permute-done.refs_4_.refs_5_ = bf16[512,1280]{1,0:T(8,128)(2,1)S(1)} collective-permute-done((bf16[512,1280]{1,0:T(8,128)(2,1)}, bf16[512,1280]{1,0:T(8,128)(2,1)S(1)}, u32[]{:S(2)}, u32[]{:S(2)}) %collective-permute-start) | collective-permute-done | bytes 1310752 | tf_op jit(solution)/shard_map/ppermute | solution.py:85
  46.9 1.9 collective-permute-start.4
  49.8 14.5 %collective-permute-done.8 = bf16[640,512]{1,0:T(8,128)(2,1)} collective-permute-done((bf16[640,512]{1,0:T(8,128)(2,1)}, bf16[640,512]{1,0:T(8,128)(2,1)}, u32[]{:S(2)}, u32[]{:S(2)}) %collective-permute-start.8) | collective-permute-done | bytes 655392 | tf_op jit(solution)/shard_map/ppermute | solution.py:85
  64.4 6.5 %collective-permute-start.9 = (bf16[640,512]{1,0:T(8,128)(2,1)}, bf16[640,512]{1,0:T(8,128)(2,1)}, u32[]{:S(2)}, u32[]{:S(2)}) collective-permute-start(bf16[640,512]{1,0:T(8,128)(2,1)} %collective-permute-done.8), channel_id=1, source_target_pairs={{0,0},{1,1},{2,2},{3,3},{4,4},{5,5},{6,6},{7,7},{8,16},{9,17},{10,... | collective-permute-start | bytes 1966088 | tf_op jit(solution)/shard_map/ppermute | solution.py:85
  72.9 1.5 collective-permute-start.12
  74.4 44.0 %all-gather.7.cloned.1.call-done = bf16[2560,768]{1,0:T(8,128)(2,1)} async-done(((bf16[640,768]{1,0:T(8,128)(2,1)}), bf16[2560,768]{1,0:T(8,128)(2,1)}) %all-gather.7.cloned.1.call-update) | async-done | bytes 3932176 | tf_op jit(solution)/shard_map/all_gather | solution.py:89
  118.4 11.8 %query_product.2 = (f32[1024,384]{1,0:T(8,128)}, f32[1024,384]{1,0:T(8,128)}) custom-call(s32[10]{0:T(128)} %pad_add_fusion.place, bf16[512,5120]{1,0:T(8,128)(2,1)} %refs_3_.3, bf16[512,5120]{1,0:T(8,128)(2,1)} %refs_3_.3, bf16[512,5120]{1,0:T(8,128)(2,1)} %refs_3_.3, bf16[512,5120]{1,0:T(8,128)(2,1)} %refs_3_.3, bf16[512,1280]{1,0:T(8,128)(2,1)} %copy-done.1, ...), custom_call_target="tpu_custom_call" | custom-call | flops 4026531840 | bytes 12320768 | tf_op jit(solution)/shard_map/query_product/pallas_call | solution.py:160
  130.2 1.5 collective-permute-start.2
  133.4 1.6 reshape.44
  137.4 2.9 %pad_maximum_fusion.refs_8_.refs_9_ = bf16[4,640,512]{2,1,0:T(8,128)(2,1)} fusion(bf16[1,640,512]{2,1,0:T(8,128)(2,1)S(1)} %select_bitcast_fusion, bf16[1,640,512]{2,1,0:T(8,128)(2,1)S(1)} %select_bitcast_fusion.1, bf16[1,640,512]{2,1,0:T(8,128)(2,1)} %bitcast.7, bf16[1,640,512]{2,1,0:T(8,128)(2,1)S(1)} %copy-done.7), kind=kLoop, calls=%fused_computation | loop fusion | flops 3932160 | bytes 5242880 | tf_op jit(solution)/shard_map/stack | solution.py:346
  140.3 8.8 %query_product.3 = (f32[1024,256]{1,0:T(8,128)}, f32[1024,256]{1,0:T(8,128)}) custom-call(s32[10]{0:T(128)} %get-tuple-element.21.place, bf16[512,5120]{1,0:T(8,128)(2,1)} %refs_3_.3, bf16[512,5120]{1,0:T(8,128)(2,1)} %refs_3_.3, bf16[512,5120]{1,0:T(8,128)(2,1)} %refs_3_.3, bf16[512,5120]{1,0:T(8,128)(2,1)} %refs_3_.3, bf16[512,1280]{1,0:T(8,128)(2,1)} %copy-done.1, ...), custom_call_target="tpu_custom_call" | custom-call | flops 2684354560 | bytes 9961472 | tf_op jit(solution)/shard_map/query_product/pallas_call | solution.py:160
  151.6 1.6 convolution_convert_fusion
  153.8 13.9 %collective-permute-done.2.received = f32[1024,384]{1,0:T(8,128)S(1)} collective-permute-done((f32[1024,384]{1,0:T(8,128)}, f32[1024,384]{1,0:T(8,128)S(1)}, u32[]{:S(2)}, u32[]{:S(2)}) %collective-permute-start.2) | collective-permute-done | bytes 1572896 | tf_op jit(solution)/shard_map/ppermute | solution.py:85
  169.0 5.7 %attend.2.refs_0_ = bf16[1024,384]{1,0:T(8,128)(2,1)} custom-call(f32[1024,384]{1,0:T(8,128)} %get-tuple-element.13.kept, f32[1024,384]{1,0:T(8,128)} %copy-done.9, bf16[64,384]{1,0:T(8,128)(2,1)} %slice.48.keys, bf16[64,384]{1,0:T(8,128)(2,1)} %slice.49.values, s32[1024,1]{1,0:T(8,128)} %bitcast.26), custom_call_target="tpu_custom_call" | custom-call | flops 100663296 | bytes 3932160 | tf_op jit(solution)/shard_map/attend/pallas_call | solution.py:263
  178.8 10.2 %collective-permute-done.13.received = f32[1024,256]{1,0:T(8,128)} collective-permute-done((f32[1024,256]{1,0:T(8,128)}, f32[1024,256]{1,0:T(8,128)}, u32[]{:S(2)}, u32[]{:S(2)}) %collective-permute-start.13) | collective-permute-done | bytes 1048608 | tf_op jit(solution)/shard_map/ppermute | solution.py:85
  189.1 5.3 %attend.3.refs_4_ = bf16[1024,256]{1,0:T(8,128)(2,1)} custom-call(f32[1024,256]{1,0:T(8,128)} %get-tuple-element.15.kept, f32[1024,256]{1,0:T(8,128)} %collective-permute-done.13.received, bf16[64,256]{1,0:T(8,128)(2,1)} %slice.52.keys, bf16[64,256]{1,0:T(8,128)(2,1)} %slice.53.values, s32[1024,1]{1,0:T(8,128)} %bitcast.27), custom_call_target="tpu_custom_call" | custom-call | flops 67108864 | bytes 2621440 | tf_op jit(solution)/shard_map/attend/pallas_call | solution.py:263
  194.4 1.5 collective-permute-start.14
  198.1 9.1 %collective-permute-done.14.refs_6_ = bf16[1024,256]{1,0:T(8,128)(2,1)S(1)} collective-permute-done((bf16[1024,256]{1,0:T(8,128)(2,1)}, bf16[1024,256]{1,0:T(8,128)(2,1)S(1)}, u32[]{:S(2)}, u32[]{:S(2)}) %collective-permute-start.14) | collective-permute-done | bytes 524320 | tf_op jit(solution)/shard_map/ppermute | solution.py:85
  208.3 1.7 slice.46
  211.3 5.3 %all-gather.11.cloned.1.call-done = bf16[2560,1024]{1,0:T(8,128)(2,1)} async-done(((bf16[640,1024]{1,0:T(8,128)(2,1)}), bf16[2560,1024]{1,0:T(8,128)(2,1)}) %all-gather.11.cloned.1.call-update) | async-done | bytes 5242896 | tf_op jit(solution)/shard_map/all_gather | solution.py:89
  217.9 13.2 %out_product.3 = (f32[512,1024]{1,0:T(8,128)}, s16[544,1024]{1,0:T(8,128)(2,1)}) custom-call(s32[4]{0:T(128)} %iota_xor_fusion.1.place, bf16[1024,384]{1,0:T(8,128)(2,1)} %attend.2.refs_0_, bf16[2048,384]{1,0:T(8,128)(2,1)} %copy-done.3, bf16[1024,384]{1,0:T(8,128)(2,1)} %copy-done.6, bf16[2048,384]{1,0:T(8,128)(2,1)} %copy-done.3, ...), custom_call_target="tpu_custom_call" | custom-call | flops 5368709120 | bytes 14680064 | tf_op jit(solution)/shard_map/out_product/pallas_call | solution.py:210
  231.0 1.5 collective-permute-start.17
  232.5 17.0 %all-gather.9.cloned.1.call-done = bf16[2560,256]{1,0:T(8,128)(2,1)} async-done(((bf16[640,256]{1,0:T(8,128)(2,1)}), bf16[2560,256]{1,0:T(8,128)(2,1)}) %all-gather.9.cloned.1.call-update) | async-done | bytes 1310736 | tf_op jit(solution)/shard_map/all_gather | solution.py:89
  249.5 7.1 %out_product.2 = (f32[512,256]{1,0:T(8,128)}, s16[544,256]{1,0:T(8,128)(2,1)}) custom-call(s32[4]{0:T(128)} %iota_xor_fusion.1.place, bf16[1024,384]{1,0:T(8,128)(2,1)} %attend.2.refs_0_, bf16[2048,384]{1,0:T(8,128)(2,1)} %copy-done.3, bf16[1024,384]{1,0:T(8,128)(2,1)} %copy-done.6, bf16[2048,384]{1,0:T(8,128)(2,1)} %copy-done.3, ...), custom_call_target="tpu_custom_call" | custom-call | flops 1342177280 | bytes 7602176 | tf_op jit(solution)/shard_map/out_product/pallas_call | solution.py:210
  256.6 1.5 collective-permute-start.16
  259.1 6.2 %finish.2.refs_0_ = bf16[512,1280]{1,0:T(8,128)(2,1)} custom-call(f32[512,1024]{1,0:T(8,128)} %get-tuple-element.19.kept, s16[544,1024]{1,0:T(8,128)(2,1)} %copy-done.5, s16[544,1024]{1,0:T(8,128)(2,1)} %copy-done.5), custom_call_target="tpu_custom_call" | custom-call | flops 1048576 | bytes 4194304 | tf_op jit(solution)/shard_map/finish/pallas_call | solution.py:296
  266.0 2.0 finish.3
  (100 shorter events, 32.2 us)
Async XLA Ops:
  6.5 143.3 %copy-start = (bf16[768,1280]{1,0:T(8,128)(2,1)S(1)}, bf16[768,1280]{1,0:T(8,128)(2,1)}, u32[]{:S(2)}) copy-start(bf16[768,1280]{1,0:T(8,128)(2,1)} %param.13) | copy-start | bytes 5898244
  6.5 111.8 %all-gather.7.cloned.1.call-start = ((), (), s32[]{:S(2)}) async-start(), calls=%async_computation | async-start | bytes 4915200 | tf_op jit(solution)/shard_map/all_gather | solution.py:89
  9.1 207.6 %all-gather.11.cloned.1.call-start = ((), (), s32[]{:S(2)}) async-start(), calls=%async_computation.2 | async-start | bytes 6553600 | tf_op jit(solution)/shard_map/all_gather | solution.py:89
  11.6 237.9 %all-gather.9.cloned.1.call-start = ((), (), s32[]{:S(2)}) async-start(), calls=%async_computation.1 | async-start | bytes 1638400 | tf_op jit(solution)/shard_map/all_gather | solution.py:89
  14.3 13.4 %copy-start.18 = (s32[2,1]{0,1:T(1,128)S(1)}, s32[2,1]{0,1:T(1,128)}, u32[]{:S(2)}) copy-start(s32[2,1]{0,1:T(1,128)} %param.16) | copy-start | bytes 28
  14.3 13.5 %copy-start.17 = (s32[2,512]{1,0:T(2,128)S(1)}, s32[2,512]{1,0:T(2,128)}, u32[]{:S(2)}) copy-start(s32[2,512]{1,0:T(2,128)} %param.15) | copy-start | bytes 12292
  14.3 14.0 %copy-start.19 = (s32[2]{0:T(128)S(1)}, s32[2]{0:T(128)}, u32[]{:S(2)}) copy-start(s32[2]{0:T(128)} %constant.56) | copy-start | bytes 28
  14.3 32.3 %collective-permute-start = (bf16[512,1280]{1,0:T(8,128)(2,1)}, bf16[512,1280]{1,0:T(8,128)(2,1)S(1)}, u32[]{:S(2)}, u32[]{:S(2)}) collective-permute-start(bf16[512,1280]{1,0:T(8,128)(2,1)} %pad_maximum_fusion.2), channel_id=1, source_target_pairs={{0,4},{1,5},{2,6},{3,7},{4,0},{5,1},{6,2},{7,3},{8,12},{9,13},{10,... | collective-permute-start | bytes 3932168 | tf_op jit(solution)/shard_map/ppermute | solution.py:85
  19.6 44.7 %collective-permute-start.8 = (bf16[640,512]{1,0:T(8,128)(2,1)}, bf16[640,512]{1,0:T(8,128)(2,1)}, u32[]{:S(2)}, u32[]{:S(2)}) collective-permute-start(bf16[640,512]{1,0:T(8,128)(2,1)} %get-tuple-element.30), channel_id=1, source_target_pairs={{0,8},{1,9},{2,10},{3,11},{4,12},{5,13},{6,14},{7,15},{8,0},{9,1},... | collective-permute-start | bytes 1966088 | tf_op jit(solution)/shard_map/ppermute | solution.py:85
  21.1 50.5 %collective-permute-start.10 = (bf16[640,512]{1,0:T(8,128)(2,1)}, bf16[640,512]{1,0:T(8,128)(2,1)}, u32[]{:S(2)}, u32[]{:S(2)}) collective-permute-start(bf16[640,512]{1,0:T(8,128)(2,1)} %get-tuple-element.30), channel_id=1, source_target_pairs={{0,0},{1,1},{2,2},{3,3},{4,4},{5,5},{6,6},{7,7},{8,16},{9,17},{10,... | collective-permute-start | bytes 1966088 | tf_op jit(solution)/shard_map/ppermute | solution.py:85
  28.3 101.8 %copy-start.11 = (bf16[1,6656]{1,0:T(2,128)(2,1)}, bf16[1,6656]{1,0:T(2,128)(2,1)S(1)}, u32[]{:S(2)}) copy-start(bf16[1,6656]{1,0:T(2,128)(2,1)S(1)} %broadcast_in_dim.2) | copy-start | bytes 39940
  28.4 18.5 %collective-permute-start.3 = (bf16[1,6656]{1,0:T(2,128)(2,1)S(1)}, bf16[1,6656]{1,0:T(2,128)(2,1)S(1)}, u32[]{:S(2)}, u32[]{:S(2)}) collective-permute-start(bf16[1,6656]{1,0:T(2,128)(2,1)S(1)} %broadcast_in_dim.2), channel_id=1, source_target_pairs={{0,4},{1,5},{2,6},{3,7},{4,0},{5,1},{6,2},{7,3},{8,12},{9,13},{10,... | collective-permute-start | bytes 39944 | tf_op jit(solution)/shard_map/ppermute | solution.py:85
  46.5 71.8 %copy-start.1 = (bf16[512,1280]{1,0:T(8,128)(2,1)}, bf16[512,1280]{1,0:T(8,128)(2,1)S(1)}, u32[]{:S(2)}) copy-start(bf16[512,1280]{1,0:T(8,128)(2,1)S(1)} %collective-permute-done.refs_4_.refs_5_) | copy-start | bytes 3932164
  46.5 27.8 %collective-permute-start.1 = (bf16[512,1280]{1,0:T(8,128)(2,1)S(1)}, bf16[512,1280]{1,0:T(8,128)(2,1)}, u32[]{:S(2)}, u32[]{:S(2)}) collective-permute-start(bf16[512,1280]{1,0:T(8,128)(2,1)S(1)} %collective-permute-done.refs_4_.refs_5_), channel_id=1, source_target_pairs={{0,1},{1,0},{2,3},{3,2},{4,5},{5,4},{6,7},{7,6},{8,9},{9,8},{10,11... | collective-permute-start | bytes 3932168 | tf_op jit(solution)/shard_map/ppermute | solution.py:85
  46.8 83.4 %copy-start.12 = (bf16[1,6656]{1,0:T(2,128)(2,1)}, bf16[1,6656]{1,0:T(2,128)(2,1)S(1)}, u32[]{:S(2)}) copy-start(bf16[1,6656]{1,0:T(2,128)(2,1)S(1)} %collective-permute-done.3) | copy-start | bytes 39940
  46.9 24.0 %collective-permute-start.4 = (bf16[2,6656]{1,0:T(2,128)(2,1)S(1)}, bf16[2,6656]{1,0:T(2,128)(2,1)S(1)}, u32[]{:S(2)}, u32[]{:S(2)}) collective-permute-start(bf16[2,6656]{1,0:T(2,128)(2,1)S(1)} %pad_maximum_fusion.11), channel_id=1, source_target_pairs={{0,8},{1,9},{2,10},{3,11},{4,12},{5,13},{6,14},{7,15},{8,0},{9,1},... | collective-permute-start | bytes 79880 | tf_op jit(solution)/shard_map/ppermute | solution.py:85
  64.4 8.5 %collective-permute-start.9 = (bf16[640,512]{1,0:T(8,128)(2,1)}, bf16[640,512]{1,0:T(8,128)(2,1)}, u32[]{:S(2)}, u32[]{:S(2)}) collective-permute-start(bf16[640,512]{1,0:T(8,128)(2,1)} %collective-permute-done.8), channel_id=1, source_target_pairs={{0,0},{1,1},{2,2},{3,3},{4,4},{5,5},{6,6},{7,7},{8,16},{9,17},{10,... | collective-permute-start | bytes 1966088 | tf_op jit(solution)/shard_map/ppermute | solution.py:85
  70.9 59.3 %copy-start.15 = (bf16[2,6656]{1,0:T(2,128)(2,1)}, bf16[2,6656]{1,0:T(2,128)(2,1)S(1)}, u32[]{:S(2)}) copy-start(bf16[2,6656]{1,0:T(2,128)(2,1)S(1)} %collective-permute-done.4) | copy-start | bytes 79876
  71.6 60.2 %collective-permute-start.5 = (bf16[4,6656]{1,0:T(4,128)(2,1)}, bf16[4,6656]{1,0:T(4,128)(2,1)}, u32[]{:S(2)}, u32[]{:S(2)}) collective-permute-start(bf16[4,6656]{1,0:T(4,128)(2,1)} %pad_maximum_fusion.9), channel_id=1, source_target_pairs={{0,16},{1,17},{2,18},{3,19},{4,20},{5,21},{6,22},{7,23},{8,24},{9,... | collective-permute-start | bytes 159752 | tf_op jit(solution)/shard_map/ppermute | solution.py:85
  71.6 63.3 %collective-permute-start.11 = (bf16[640,512]{1,0:T(8,128)(2,1)}, bf16[640,512]{1,0:T(8,128)(2,1)}, u32[]{:S(2)}, u32[]{:S(2)}) collective-permute-start(bf16[640,512]{1,0:T(8,128)(2,1)} %collective-permute-done.10), channel_id=1, source_target_pairs={{8,0},{9,1},{10,2},{11,3},{12,4},{13,5},{14,6},{15,7},{16,24},{17,... | collective-permute-start | bytes 1966088 | tf_op jit(solution)/shard_map/ppermute | solution.py:85
  72.9 63.3 %collective-permute-start.12 = (bf16[640,512]{1,0:T(8,128)(2,1)}, bf16[640,512]{1,0:T(8,128)(2,1)}, u32[]{:S(2)}, u32[]{:S(2)}) collective-permute-start(bf16[640,512]{1,0:T(8,128)(2,1)} %collective-permute-done.9), channel_id=1, source_target_pairs={{8,0},{9,1},{10,2},{11,3},{12,4},{13,5},{14,6},{15,7},{16,24},{17,... | collective-permute-start | bytes 1966088 | tf_op jit(solution)/shard_map/ppermute | solution.py:85
  130.2 37.6 %collective-permute-start.2 = (f32[1024,384]{1,0:T(8,128)}, f32[1024,384]{1,0:T(8,128)S(1)}, u32[]{:S(2)}, u32[]{:S(2)}) collective-permute-start(f32[1024,384]{1,0:T(8,128)} %get-tuple-element.14), channel_id=1, source_target_pairs={{0,4},{1,5},{2,6},{3,7},{4,0},{5,1},{6,2},{7,3},{8,12},{9,13},{10,... | collective-permute-start | bytes 4718600 | tf_op jit(solution)/shard_map/ppermute | solution.py:85
  149.1 40.0 %collective-permute-start.13 = (f32[1024,256]{1,0:T(8,128)}, f32[1024,256]{1,0:T(8,128)}, u32[]{:S(2)}, u32[]{:S(2)}) collective-permute-start(f32[1024,256]{1,0:T(8,128)} %get-tuple-element.16), channel_id=1, source_target_pairs={{0,4},{1,5},{2,6},{3,7},{4,0},{5,1},{6,2},{7,3},{8,12},{9,13},{10,... | collective-permute-start | bytes 3145736 | tf_op jit(solution)/shard_map/ppermute | solution.py:85
  151.0 16.8 %copy-start.13 = (bf16[64,640]{1,0:T(8,128)(2,1)}, bf16[64,640]{1,0:T(8,128)(2,1)S(1)}, u32[]{:S(2)}) copy-start(bf16[64,640]{1,0:T(8,128)(2,1)S(1)} %convolution_convert_fusion.1) | copy-start | bytes 245764
  153.2 14.6 %copy-start.14 = (bf16[64,640]{1,0:T(8,128)(2,1)}, bf16[64,640]{1,0:T(8,128)(2,1)S(1)}, u32[]{:S(2)}) copy-start(bf16[64,640]{1,0:T(8,128)(2,1)S(1)} %convolution_convert_fusion) | copy-start | bytes 245764
  174.7 22.1 %copy-start.2 = (bf16[1024,384]{1,0:T(8,128)(2,1)S(1)}, bf16[1024,384]{1,0:T(8,128)(2,1)}, u32[]{:S(2)}) copy-start(bf16[1024,384]{1,0:T(8,128)(2,1)} %attend.2.refs_0_) | copy-start | bytes 2359300
  174.7 21.2 %collective-permute-start.6 = (bf16[1024,384]{1,0:T(8,128)(2,1)}, bf16[1024,384]{1,0:T(8,128)(2,1)S(1)}, u32[]{:S(2)}, u32[]{:S(2)}) collective-permute-start(bf16[1024,384]{1,0:T(8,128)(2,1)} %attend.2.refs_0_), channel_id=1, source_target_pairs={{0,2},{1,3},{2,0},{3,1},{4,6},{5,7},{6,4},{7,5},{8,10},{9,11},{10,... | collective-permute-start | bytes 2359304 | tf_op jit(solution)/shard_map/ppermute | solution.py:85
  194.4 12.8 %collective-permute-start.14 = (bf16[1024,256]{1,0:T(8,128)(2,1)}, bf16[1024,256]{1,0:T(8,128)(2,1)S(1)}, u32[]{:S(2)}, u32[]{:S(2)}) collective-permute-start(bf16[1024,256]{1,0:T(8,128)(2,1)} %attend.3.refs_4_), channel_id=1, source_target_pairs={{0,2},{1,3},{2,0},{3,1},{4,6},{5,7},{6,4},{7,5},{8,10},{9,11},{10,... | collective-permute-start | bytes 1572872 | tf_op jit(solution)/shard_map/ppermute | solution.py:85
  198.1 18.5 %collective-permute-start.7 = (bf16[2048,384]{1,0:T(8,128)(2,1)}, bf16[2048,384]{1,0:T(8,128)(2,1)S(1)}, u32[]{:S(2)}, u32[]{:S(2)}) collective-permute-start(bf16[2048,384]{1,0:T(8,128)(2,1)} %pad_maximum_fusion.1), channel_id=1, source_target_pairs={{0,1},{1,0},{2,3},{3,2},{4,5},{5,4},{6,7},{7,6},{8,9},{9,8},{10,11... | collective-permute-start | bytes 4718600 | tf_op jit(solution)/shard_map/ppermute | solution.py:85
  208.3 3.0 %collective-permute-start.15 = (bf16[2048,256]{1,0:T(8,128)(2,1)}, bf16[2048,256]{1,0:T(8,128)(2,1)}, u32[]{:S(2)}, u32[]{:S(2)}) collective-permute-start(bf16[2048,256]{1,0:T(8,128)(2,1)} %pad_maximum_fusion.3), channel_id=1, source_target_pairs={{0,1},{1,0},{2,3},{3,2},{4,5},{5,4},{6,7},{7,6},{8,9},{9,8},{10,11... | collective-permute-start | bytes 3145736 | tf_op jit(solution)/shard_map/ppermute | solution.py:85
  231.0 27.1 %collective-permute-start.17 = (s16[544,1024]{1,0:T(8,128)(2,1)}, s16[544,1024]{1,0:T(8,128)(2,1)S(1)}, u32[]{:S(2)}, u32[]{:S(2)}) collective-permute-start(s16[544,1024]{1,0:T(8,128)(2,1)} %get-tuple-element.20), channel_id=1, source_target_pairs={{0,4},{1,5},{2,6},{3,7},{4,0},{5,1},{6,2},{7,3},{8,12},{9,13},{10,... | collective-permute-start | bytes 3342344 | tf_op jit(solution)/shard_map/ppermute | solution.py:85
  256.6 8.7 %collective-permute-start.16 = (s16[544,256]{1,0:T(8,128)(2,1)}, s16[544,256]{1,0:T(8,128)(2,1)S(1)}, u32[]{:S(2)}, u32[]{:S(2)}) collective-permute-start(s16[544,256]{1,0:T(8,128)(2,1)} %get-tuple-element.18), channel_id=1, source_target_pairs={{0,4},{1,5},{2,6},{3,7},{4,0},{5,1},{6,2},{7,3},{8,12},{9,13},{10,... | collective-permute-start | bytes 835592 | tf_op jit(solution)/shard_map/ppermute | solution.py:85
  (9 other events, 34.9 us)
Sparse Core Ops, SparseCore 0:
  9.2 109.1 all-gather.6
  119.9 96.6 all-gather.10
  218.2 31.2 all-gather.8

commit v6 on v5

--- a/solution.py
+++ b/solution.py
@@ -190,37 +190,37 @@
             term = jnp.dot(lefts[i * 4 + j][...], right, preferred_element_type=jnp.float32)
             total = term if total is None else total + term
             first += size
-    pl.when(pl.program_id(0) < 2)(lambda: pack(total, sent))
-    pl.when(pl.program_id(0) >= 2)(lambda: kept.__setitem__(..., total))
+    pl.when(pl.program_id(0) == 0)(lambda: pack(total, sent))
+    pl.when(pl.program_id(0) == 1)(lambda: kept.__setitem__(..., total))
 
 
 def out_product(place, groups, weights):
     rows = groups[0][0].shape[0]
     k_sizes = tuple(group[0].shape[1] for group in groups)
     columns = weights.shape[2]
-    step = rows // 4
+    step = rows // 2
     left_specs = [
         pl.BlockSpec(
-            (step, size), functools.partial(lambda skip, i, place: ((i + 2) % 4 + skip, 0), skip)
+            (step, size), functools.partial(lambda skip, i, place: (1 - i + skip, 0), skip)
         )
         for size in k_sizes
-        for skip in (0, 0, 0, 4)
+        for skip in (0, 0, 0, 2)
     ]
     lefts = [piece for own, core, over_y in groups for piece in (own, core, over_y, core)]
     return pl.pallas_call(
         functools.partial(out_body, k_sizes=k_sizes),
         grid_spec=pltpu.PrefetchScalarGridSpec(
             num_scalar_prefetch=1,
-            grid=(4,),
+            grid=(2,),
             in_specs=left_specs + [pl.BlockSpec(weights.shape, lambda i, place: (0, 0, 0))],
             out_specs=[
-                pl.BlockSpec((step, columns), lambda i, place: (jnp.maximum(i - 2, 0), 0)),
-                pl.BlockSpec((step + 16, columns), lambda i, place: (jnp.minimum(i, 1), 0)),
+                pl.BlockSpec((step, columns), lambda i, place: (0, 0)),
+                pl.BlockSpec((step + 16, columns), lambda i, place: (0, 0)),
             ],
         ),
         out_shape=[
-            jax.ShapeDtypeStruct((rows // 2, columns), jnp.float32),
-            jax.ShapeDtypeStruct((2 * (step + 16), columns), jnp.int16),
+            jax.ShapeDtypeStruct((step, columns), jnp.float32),
+            jax.ShapeDtypeStruct((step + 16, columns), jnp.int16),
         ],
         cost_estimate=pl.CostEstimate(
             flops=8 * rows * sum(k_sizes) * columns,
@@ -289,20 +289,19 @@
 
 def finish(kept, received, first, whole, result):
     rows, columns = kept.shape
-    step = rows // 2
-    width = 2 * HD
-    at = lambda i, j: (i, j)
+    width = 4 * HD if columns % (4 * HD) == 0 and first % (4 * HD) == 0 else 2 * HD
+    at = lambda j: (0, j)
     given = [] if result is None else [result]
     return pl.pallas_call(
         finish_body,
-        grid=(2, columns // width),
+        grid=(columns // width,),
         in_specs=[
-            pl.BlockSpec((step, width), at),
-            pl.BlockSpec((step + 16, width), at),
-            pl.BlockSpec((step + 16, 128), lambda i, j: (i, 0)),
+            pl.BlockSpec((rows, width), at),
+            pl.BlockSpec((rows + 16, width), at),
+            pl.BlockSpec((rows + 16, 128), lambda j: (0, 0)),
         ]
         + [pl.BlockSpec(memory_space=pl.ANY)] * len(given),
-        out_specs=pl.BlockSpec((step, width), lambda i, j: (i, first // width + j)),
+        out_specs=pl.BlockSpec((rows, width), lambda j: (0, first // width + j)),
         out_shape=jax.ShapeDtypeStruct((rows, whole), jnp.bfloat16),
         input_output_aliases={3: 0} if given else {},
         cost_estimate=pl.CostEstimate(

time: 276 us -> 275 us (level)
  Pallas kernels: 60 us -> 56.4 us
  waiting for transfers between devices: 131 us -> 134 us
    pallas_call x2, Pallas kernels: 8.17 us -> 4.91 us  [finish(): pl.pallas_call(finish_body, grid=(columns // width,), in_specs=[pl.BlockS...]
  transfers between devices with their start and end apart: 21 -> 21, of which waited for: 10 -> 11; matrix products, arithmetic and copies ran while one was open for 11% -> 11% of each run, Pallas kernels for 21% -> 20%
where the time goes in v6:
time: 275 us; the launch traced here: 273 us
  waiting for transfers between devices  134 us (49%)
  Pallas kernels  56.4 us (21%)
  starting transfers between devices  31 us (11%)
  local copies, waits for them, and re-layouts  20.6 us (7%)
  other arithmetic  15.3 us (6%)
  between operations  13.3 us (5%)
    ppermute x18, waiting for transfers between devices, send(): return lax.ppermute(value, AXES, move)  67.5 us
    all_gather x3, waiting for transfers between devices, along_z(): return lax.all_gather(value, 'ctx', axis=0, axis_index_groups=SAME_X)  66 us
    ppermute x18, starting transfers between devices, send(): return lax.ppermute(value, AXES, move)  30.9 us
    pallas_call x2, Pallas kernels, query_product(): pl.pallas_call(query_body, grid_spec=pltpu.PrefetchScalarGridSpec(num_sca...  20.6 us
    pallas_call x2, Pallas kernels, out_product(): pl.pallas_call(functools.partial(out_body, k_sizes=k_sizes), grid_spec=pl...  19.8 us
    pallas_call x2, Pallas kernels, attend(): pl.pallas_call(functools.partial(attend_body, audio_length=audio_length,...  11 us
    another operation x4, other arithmetic, plane_shards(): jnp.stack([piece, swapped, jnp.where(is_mid, last, to_end), jnp.where(is_...  6.5 us
    unnamed x42, local copies, waits for them, and re-layouts  6.13 us
  transfers between devices with their start and end apart: 21, of which 11 were waited for; matrix products, arithmetic and copies ran while one was open for 11% of the time, Pallas kernels for 20%

profile of v6, /device:TPU:0, one launch (start us, length us, event | category | flops | bytes accessed | tf_op | source)
XLA Modules:
  0.0 272.9 jit_solution(7289988037021112444)
XLA Ops:
  9.1 2.5 slice.47
  14.3 3.0 %collective-permute-start = (bf16[512,1280]{1,0:T(8,128)(2,1)}, bf16[512,1280]{1,0:T(8,128)(2,1)S(1)}, u32[]{:S(2)}, u32[]{:S(2)}) collective-permute-start(bf16[512,1280]{1,0:T(8,128)(2,1)} %pad_maximum_fusion.2), channel_id=1, source_target_pairs={{0,4},{1,5},{2,6},{3,7},{4,0},{5,1},{6,2},{7,3},{8,12},{9,13},{10,... | collective-permute-start | bytes 3932168 | tf_op jit(solution)/shard_map/ppermute | solution.py:85
  19.6 1.5 collective-permute-start.8
  21.1 6.5 %collective-permute-start.10 = (bf16[640,512]{1,0:T(8,128)(2,1)}, bf16[640,512]{1,0:T(8,128)(2,1)}, u32[]{:S(2)}, u32[]{:S(2)}) collective-permute-start(bf16[640,512]{1,0:T(8,128)(2,1)} %get-tuple-element.30), channel_id=1, source_target_pairs={{0,0},{1,1},{2,2},{3,3},{4,4},{5,5},{6,6},{7,7},{8,16},{9,17},{10,... | collective-permute-start | bytes 1966088 | tf_op jit(solution)/shard_map/ppermute | solution.py:85
  30.2 16.3 %collective-permute-done.refs_4_.refs_5_ = bf16[512,1280]{1,0:T(8,128)(2,1)S(1)} collective-permute-done((bf16[512,1280]{1,0:T(8,128)(2,1)}, bf16[512,1280]{1,0:T(8,128)(2,1)S(1)}, u32[]{:S(2)}, u32[]{:S(2)}) %collective-permute-start) | collective-permute-done | bytes 1310752 | tf_op jit(solution)/shard_map/ppermute | solution.py:85
  46.9 1.9 collective-permute-start.4
  49.8 14.5 %collective-permute-done.8 = bf16[640,512]{1,0:T(8,128)(2,1)} collective-permute-done((bf16[640,512]{1,0:T(8,128)(2,1)}, bf16[640,512]{1,0:T(8,128)(2,1)}, u32[]{:S(2)}, u32[]{:S(2)}) %collective-permute-start.8) | collective-permute-done | bytes 655392 | tf_op jit(solution)/shard_map/ppermute | solution.py:85
  64.4 6.5 %collective-permute-start.9 = (bf16[640,512]{1,0:T(8,128)(2,1)}, bf16[640,512]{1,0:T(8,128)(2,1)}, u32[]{:S(2)}, u32[]{:S(2)}) collective-permute-start(bf16[640,512]{1,0:T(8,128)(2,1)} %collective-permute-done.8), channel_id=1, source_target_pairs={{0,0},{1,1},{2,2},{3,3},{4,4},{5,5},{6,6},{7,7},{8,16},{9,17},{10,... | collective-permute-start | bytes 1966088 | tf_op jit(solution)/shard_map/ppermute | solution.py:85
  72.9 1.5 collective-permute-start.12
  74.4 44.0 %all-gather.7.cloned.1.call-done = bf16[2560,768]{1,0:T(8,128)(2,1)} async-done(((bf16[640,768]{1,0:T(8,128)(2,1)}), bf16[2560,768]{1,0:T(8,128)(2,1)}) %all-gather.7.cloned.1.call-update) | async-done | bytes 3932176 | tf_op jit(solution)/shard_map/all_gather | solution.py:89
  118.4 11.8 %query_product.2 = (f32[1024,384]{1,0:T(8,128)}, f32[1024,384]{1,0:T(8,128)}) custom-call(s32[10]{0:T(128)} %pad_add_fusion.place, bf16[512,5120]{1,0:T(8,128)(2,1)} %refs_3_.3, bf16[512,5120]{1,0:T(8,128)(2,1)} %refs_3_.3, bf16[512,5120]{1,0:T(8,128)(2,1)} %refs_3_.3, bf16[512,5120]{1,0:T(8,128)(2,1)} %refs_3_.3, bf16[512,1280]{1,0:T(8,128)(2,1)} %copy-done.1, ...), custom_call_target="tpu_custom_call" | custom-call | flops 4026531840 | bytes 12320768 | tf_op jit(solution)/shard_map/query_product/pallas_call | solution.py:160
  130.2 1.5 collective-permute-start.2
  133.4 1.6 reshape.44
  137.4 2.9 %pad_maximum_fusion.refs_8_.refs_9_ = bf16[4,640,512]{2,1,0:T(8,128)(2,1)} fusion(bf16[1,640,512]{2,1,0:T(8,128)(2,1)S(1)} %select_bitcast_fusion, bf16[1,640,512]{2,1,0:T(8,128)(2,1)S(1)} %select_bitcast_fusion.1, bf16[1,640,512]{2,1,0:T(8,128)(2,1)} %bitcast.7, bf16[1,640,512]{2,1,0:T(8,128)(2,1)S(1)} %copy-done.7), kind=kLoop, calls=%fused_computation | loop fusion | flops 3932160 | bytes 5242880 | tf_op jit(solution)/shard_map/stack | solution.py:345
  140.3 8.8 %query_product.3 = (f32[1024,256]{1,0:T(8,128)}, f32[1024,256]{1,0:T(8,128)}) custom-call(s32[10]{0:T(128)} %get-tuple-element.21.place, bf16[512,5120]{1,0:T(8,128)(2,1)} %refs_3_.3, bf16[512,5120]{1,0:T(8,128)(2,1)} %refs_3_.3, bf16[512,5120]{1,0:T(8,128)(2,1)} %refs_3_.3, bf16[512,5120]{1,0:T(8,128)(2,1)} %refs_3_.3, bf16[512,1280]{1,0:T(8,128)(2,1)} %copy-done.1, ...), custom_call_target="tpu_custom_call" | custom-call | flops 2684354560 | bytes 9961472 | tf_op jit(solution)/shard_map/query_product/pallas_call | solution.py:160
  151.6 1.6 convolution_convert_fusion
  153.8 13.9 %collective-permute-done.2.received = f32[1024,384]{1,0:T(8,128)S(1)} collective-permute-done((f32[1024,384]{1,0:T(8,128)}, f32[1024,384]{1,0:T(8,128)S(1)}, u32[]{:S(2)}, u32[]{:S(2)}) %collective-permute-start.2) | collective-permute-done | bytes 1572896 | tf_op jit(solution)/shard_map/ppermute | solution.py:85
  169.0 5.7 %attend.2.refs_0_ = bf16[1024,384]{1,0:T(8,128)(2,1)} custom-call(f32[1024,384]{1,0:T(8,128)} %get-tuple-element.13.kept, f32[1024,384]{1,0:T(8,128)} %copy-done.9, bf16[64,384]{1,0:T(8,128)(2,1)} %slice.48.keys, bf16[64,384]{1,0:T(8,128)(2,1)} %slice.49.values, s32[1024,1]{1,0:T(8,128)} %bitcast.26), custom_call_target="tpu_custom_call" | custom-call | flops 100663296 | bytes 3932160 | tf_op jit(solution)/shard_map/attend/pallas_call | solution.py:263
  178.8 10.2 %collective-permute-done.13.received = f32[1024,256]{1,0:T(8,128)} collective-permute-done((f32[1024,256]{1,0:T(8,128)}, f32[1024,256]{1,0:T(8,128)}, u32[]{:S(2)}, u32[]{:S(2)}) %collective-permute-start.13) | collective-permute-done | bytes 1048608 | tf_op jit(solution)/shard_map/ppermute | solution.py:85
  189.1 5.3 %attend.3.refs_4_ = bf16[1024,256]{1,0:T(8,128)(2,1)} custom-call(f32[1024,256]{1,0:T(8,128)} %get-tuple-element.15.kept, f32[1024,256]{1,0:T(8,128)} %collective-permute-done.13.received, bf16[64,256]{1,0:T(8,128)(2,1)} %slice.52.keys, bf16[64,256]{1,0:T(8,128)(2,1)} %slice.53.values, s32[1024,1]{1,0:T(8,128)} %bitcast.27), custom_call_target="tpu_custom_call" | custom-call | flops 67108864 | bytes 2621440 | tf_op jit(solution)/shard_map/attend/pallas_call | solution.py:263
  194.4 1.5 collective-permute-start.14
  198.1 9.1 %collective-permute-done.14.refs_6_ = bf16[1024,256]{1,0:T(8,128)(2,1)S(1)} collective-permute-done((bf16[1024,256]{1,0:T(8,128)(2,1)}, bf16[1024,256]{1,0:T(8,128)(2,1)S(1)}, u32[]{:S(2)}, u32[]{:S(2)}) %collective-permute-start.14) | collective-permute-done | bytes 524320 | tf_op jit(solution)/shard_map/ppermute | solution.py:85
  208.3 1.7 slice.46
  211.3 5.3 %all-gather.11.cloned.1.call-done = bf16[2560,1024]{1,0:T(8,128)(2,1)} async-done(((bf16[640,1024]{1,0:T(8,128)(2,1)}), bf16[2560,1024]{1,0:T(8,128)(2,1)}) %all-gather.11.cloned.1.call-update) | async-done | bytes 5242896 | tf_op jit(solution)/shard_map/all_gather | solution.py:89
  217.9 13.4 %out_product.3 = (f32[512,1024]{1,0:T(8,128)}, s16[528,1024]{1,0:T(8,128)(2,1)}) custom-call(s32[4]{0:T(128)} %iota_xor_fusion.1.place, bf16[1024,384]{1,0:T(8,128)(2,1)} %attend.2.refs_0_, bf16[2048,384]{1,0:T(8,128)(2,1)} %copy-done.3, bf16[1024,384]{1,0:T(8,128)(2,1)} %copy-done.6, bf16[2048,384]{1,0:T(8,128)(2,1)} %copy-done.3, ...), custom_call_target="tpu_custom_call" | custom-call | flops 5368709120 | bytes 14680064 | tf_op jit(solution)/shard_map/out_product/pallas_call | solution.py:210
  231.3 1.5 collective-permute-start.17
  232.8 16.7 %all-gather.9.cloned.1.call-done = bf16[2560,256]{1,0:T(8,128)(2,1)} async-done(((bf16[640,256]{1,0:T(8,128)(2,1)}), bf16[2560,256]{1,0:T(8,128)(2,1)}) %all-gather.9.cloned.1.call-update) | async-done | bytes 1310736 | tf_op jit(solution)/shard_map/all_gather | solution.py:89
  249.5 6.4 %out_product.2 = (f32[512,256]{1,0:T(8,128)}, s16[528,256]{1,0:T(8,128)(2,1)}) custom-call(s32[4]{0:T(128)} %iota_xor_fusion.1.place, bf16[1024,384]{1,0:T(8,128)(2,1)} %attend.2.refs_0_, bf16[2048,384]{1,0:T(8,128)(2,1)} %copy-done.3, bf16[1024,384]{1,0:T(8,128)(2,1)} %copy-done.6, bf16[2048,384]{1,0:T(8,128)(2,1)} %copy-done.3, ...), custom_call_target="tpu_custom_call" | custom-call | flops 1342177280 | bytes 7602176 | tf_op jit(solution)/shard_map/out_product/pallas_call | solution.py:210
  255.9 1.5 collective-permute-start.16
  258.4 2.9 %finish.2.refs_0_ = bf16[512,1280]{1,0:T(8,128)(2,1)} custom-call(f32[512,1024]{1,0:T(8,128)} %get-tuple-element.19.kept, s16[528,1024]{1,0:T(8,128)(2,1)} %copy-done.5, s16[528,1024]{1,0:T(8,128)(2,1)} %copy-done.5), custom_call_target="tpu_custom_call" | custom-call | flops 1048576 | bytes 4194304 | tf_op jit(solution)/shard_map/finish/pallas_call | solution.py:295
  261.3 2.4 collective-permute-done.16.received.scales
  264.4 2.0 finish.3
  (100 shorter events, 33.6 us)
Async XLA Ops:
  6.5 143.3 %copy-start = (bf16[768,1280]{1,0:T(8,128)(2,1)S(1)}, bf16[768,1280]{1,0:T(8,128)(2,1)}, u32[]{:S(2)}) copy-start(bf16[768,1280]{1,0:T(8,128)(2,1)} %param.13) | copy-start | bytes 5898244
  6.5 111.8 %all-gather.7.cloned.1.call-start = ((), (), s32[]{:S(2)}) async-start(), calls=%async_computation | async-start | bytes 4915200 | tf_op jit(solution)/shard_map/all_gather | solution.py:89
  9.1 207.6 %all-gather.11.cloned.1.call-start = ((), (), s32[]{:S(2)}) async-start(), calls=%async_computation.2 | async-start | bytes 6553600 | tf_op jit(solution)/shard_map/all_gather | solution.py:89
  11.6 237.9 %all-gather.9.cloned.1.call-start = ((), (), s32[]{:S(2)}) async-start(), calls=%async_computation.1 | async-start | bytes 1638400 | tf_op jit(solution)/shard_map/all_gather | solution.py:89
  14.3 13.4 %copy-start.18 = (s32[2,1]{0,1:T(1,128)S(1)}, s32[2,1]{0,1:T(1,128)}, u32[]{:S(2)}) copy-start(s32[2,1]{0,1:T(1,128)} %param.16) | copy-start | bytes 28
  14.3 13.5 %copy-start.17 = (s32[2,512]{1,0:T(2,128)S(1)}, s32[2,512]{1,0:T(2,128)}, u32[]{:S(2)}) copy-start(s32[2,512]{1,0:T(2,128)} %param.15) | copy-start | bytes 12292
  14.3 14.0 %copy-start.19 = (s32[2]{0:T(128)S(1)}, s32[2]{0:T(128)}, u32[]{:S(2)}) copy-start(s32[2]{0:T(128)} %constant.56) | copy-start | bytes 28
  14.3 32.3 %collective-permute-start = (bf16[512,1280]{1,0:T(8,128)(2,1)}, bf16[512,1280]{1,0:T(8,128)(2,1)S(1)}, u32[]{:S(2)}, u32[]{:S(2)}) collective-permute-start(bf16[512,1280]{1,0:T(8,128)(2,1)} %pad_maximum_fusion.2), channel_id=1, source_target_pairs={{0,4},{1,5},{2,6},{3,7},{4,0},{5,1},{6,2},{7,3},{8,12},{9,13},{10,... | collective-permute-start | bytes 3932168 | tf_op jit(solution)/shard_map/ppermute | solution.py:85
  19.6 44.7 %collective-permute-start.8 = (bf16[640,512]{1,0:T(8,128)(2,1)}, bf16[640,512]{1,0:T(8,128)(2,1)}, u32[]{:S(2)}, u32[]{:S(2)}) collective-permute-start(bf16[640,512]{1,0:T(8,128)(2,1)} %get-tuple-element.30), channel_id=1, source_target_pairs={{0,8},{1,9},{2,10},{3,11},{4,12},{5,13},{6,14},{7,15},{8,0},{9,1},... | collective-permute-start | bytes 1966088 | tf_op jit(solution)/shard_map/ppermute | solution.py:85
  21.1 50.5 %collective-permute-start.10 = (bf16[640,512]{1,0:T(8,128)(2,1)}, bf16[640,512]{1,0:T(8,128)(2,1)}, u32[]{:S(2)}, u32[]{:S(2)}) collective-permute-start(bf16[640,512]{1,0:T(8,128)(2,1)} %get-tuple-element.30), channel_id=1, source_target_pairs={{0,0},{1,1},{2,2},{3,3},{4,4},{5,5},{6,6},{7,7},{8,16},{9,17},{10,... | collective-permute-start | bytes 1966088 | tf_op jit(solution)/shard_map/ppermute | solution.py:85
  28.3 101.8 %copy-start.11 = (bf16[1,6656]{1,0:T(2,128)(2,1)}, bf16[1,6656]{1,0:T(2,128)(2,1)S(1)}, u32[]{:S(2)}) copy-start(bf16[1,6656]{1,0:T(2,128)(2,1)S(1)} %broadcast_in_dim.2) | copy-start | bytes 39940
  28.4 18.5 %collective-permute-start.3 = (bf16[1,6656]{1,0:T(2,128)(2,1)S(1)}, bf16[1,6656]{1,0:T(2,128)(2,1)S(1)}, u32[]{:S(2)}, u32[]{:S(2)}) collective-permute-start(bf16[1,6656]{1,0:T(2,128)(2,1)S(1)} %broadcast_in_dim.2), channel_id=1, source_target_pairs={{0,4},{1,5},{2,6},{3,7},{4,0},{5,1},{6,2},{7,3},{8,12},{9,13},{10,... | collective-permute-start | bytes 39944 | tf_op jit(solution)/shard_map/ppermute | solution.py:85
  46.5 71.8 %copy-start.1 = (bf16[512,1280]{1,0:T(8,128)(2,1)}, bf16[512,1280]{1,0:T(8,128)(2,1)S(1)}, u32[]{:S(2)}) copy-start(bf16[512,1280]{1,0:T(8,128)(2,1)S(1)} %collective-permute-done.refs_4_.refs_5_) | copy-start | bytes 3932164
  46.5 27.8 %collective-permute-start.1 = (bf16[512,1280]{1,0:T(8,128)(2,1)S(1)}, bf16[512,1280]{1,0:T(8,128)(2,1)}, u32[]{:S(2)}, u32[]{:S(2)}) collective-permute-start(bf16[512,1280]{1,0:T(8,128)(2,1)S(1)} %collective-permute-done.refs_4_.refs_5_), channel_id=1, source_target_pairs={{0,1},{1,0},{2,3},{3,2},{4,5},{5,4},{6,7},{7,6},{8,9},{9,8},{10,11... | collective-permute-start | bytes 3932168 | tf_op jit(solution)/shard_map/ppermute | solution.py:85
  46.8 83.4 %copy-start.12 = (bf16[1,6656]{1,0:T(2,128)(2,1)}, bf16[1,6656]{1,0:T(2,128)(2,1)S(1)}, u32[]{:S(2)}) copy-start(bf16[1,6656]{1,0:T(2,128)(2,1)S(1)} %collective-permute-done.3) | copy-start | bytes 39940
  46.9 24.0 %collective-permute-start.4 = (bf16[2,6656]{1,0:T(2,128)(2,1)S(1)}, bf16[2,6656]{1,0:T(2,128)(2,1)S(1)}, u32[]{:S(2)}, u32[]{:S(2)}) collective-permute-start(bf16[2,6656]{1,0:T(2,128)(2,1)S(1)} %pad_maximum_fusion.11), channel_id=1, source_target_pairs={{0,8},{1,9},{2,10},{3,11},{4,12},{5,13},{6,14},{7,15},{8,0},{9,1},... | collective-permute-start | bytes 79880 | tf_op jit(solution)/shard_map/ppermute | solution.py:85
  64.4 8.5 %collective-permute-start.9 = (bf16[640,512]{1,0:T(8,128)(2,1)}, bf16[640,512]{1,0:T(8,128)(2,1)}, u32[]{:S(2)}, u32[]{:S(2)}) collective-permute-start(bf16[640,512]{1,0:T(8,128)(2,1)} %collective-permute-done.8), channel_id=1, source_target_pairs={{0,0},{1,1},{2,2},{3,3},{4,4},{5,5},{6,6},{7,7},{8,16},{9,17},{10,... | collective-permute-start | bytes 1966088 | tf_op jit(solution)/shard_map/ppermute | solution.py:85
  70.9 59.3 %copy-start.15 = (bf16[2,6656]{1,0:T(2,128)(2,1)}, bf16[2,6656]{1,0:T(2,128)(2,1)S(1)}, u32[]{:S(2)}) copy-start(bf16[2,6656]{1,0:T(2,128)(2,1)S(1)} %collective-permute-done.4) | copy-start | bytes 79876
  71.6 60.2 %collective-permute-start.5 = (bf16[4,6656]{1,0:T(4,128)(2,1)}, bf16[4,6656]{1,0:T(4,128)(2,1)}, u32[]{:S(2)}, u32[]{:S(2)}) collective-permute-start(bf16[4,6656]{1,0:T(4,128)(2,1)} %pad_maximum_fusion.9), channel_id=1, source_target_pairs={{0,16},{1,17},{2,18},{3,19},{4,20},{5,21},{6,22},{7,23},{8,24},{9,... | collective-permute-start | bytes 159752 | tf_op jit(solution)/shard_map/ppermute | solution.py:85
  71.6 63.3 %collective-permute-start.11 = (bf16[640,512]{1,0:T(8,128)(2,1)}, bf16[640,512]{1,0:T(8,128)(2,1)}, u32[]{:S(2)}, u32[]{:S(2)}) collective-permute-start(bf16[640,512]{1,0:T(8,128)(2,1)} %collective-permute-done.10), channel_id=1, source_target_pairs={{8,0},{9,1},{10,2},{11,3},{12,4},{13,5},{14,6},{15,7},{16,24},{17,... | collective-permute-start | bytes 1966088 | tf_op jit(solution)/shard_map/ppermute | solution.py:85
  72.9 63.3 %collective-permute-start.12 = (bf16[640,512]{1,0:T(8,128)(2,1)}, bf16[640,512]{1,0:T(8,128)(2,1)}, u32[]{:S(2)}, u32[]{:S(2)}) collective-permute-start(bf16[640,512]{1,0:T(8,128)(2,1)} %collective-permute-done.9), channel_id=1, source_target_pairs={{8,0},{9,1},{10,2},{11,3},{12,4},{13,5},{14,6},{15,7},{16,24},{17,... | collective-permute-start | bytes 1966088 | tf_op jit(solution)/shard_map/ppermute | solution.py:85
  130.2 37.6 %collective-permute-start.2 = (f32[1024,384]{1,0:T(8,128)}, f32[1024,384]{1,0:T(8,128)S(1)}, u32[]{:S(2)}, u32[]{:S(2)}) collective-permute-start(f32[1024,384]{1,0:T(8,128)} %get-tuple-element.14), channel_id=1, source_target_pairs={{0,4},{1,5},{2,6},{3,7},{4,0},{5,1},{6,2},{7,3},{8,12},{9,13},{10,... | collective-permute-start | bytes 4718600 | tf_op jit(solution)/shard_map/ppermute | solution.py:85
  149.1 40.0 %collective-permute-start.13 = (f32[1024,256]{1,0:T(8,128)}, f32[1024,256]{1,0:T(8,128)}, u32[]{:S(2)}, u32[]{:S(2)}) collective-permute-start(f32[1024,256]{1,0:T(8,128)} %get-tuple-element.16), channel_id=1, source_target_pairs={{0,4},{1,5},{2,6},{3,7},{4,0},{5,1},{6,2},{7,3},{8,12},{9,13},{10,... | collective-permute-start | bytes 3145736 | tf_op jit(solution)/shard_map/ppermute | solution.py:85
  151.0 16.8 %copy-start.13 = (bf16[64,640]{1,0:T(8,128)(2,1)}, bf16[64,640]{1,0:T(8,128)(2,1)S(1)}, u32[]{:S(2)}) copy-start(bf16[64,640]{1,0:T(8,128)(2,1)S(1)} %convolution_convert_fusion.1) | copy-start | bytes 245764
  153.2 14.6 %copy-start.14 = (bf16[64,640]{1,0:T(8,128)(2,1)}, bf16[64,640]{1,0:T(8,128)(2,1)S(1)}, u32[]{:S(2)}) copy-start(bf16[64,640]{1,0:T(8,128)(2,1)S(1)} %convolution_convert_fusion) | copy-start | bytes 245764
  174.7 22.1 %copy-start.2 = (bf16[1024,384]{1,0:T(8,128)(2,1)S(1)}, bf16[1024,384]{1,0:T(8,128)(2,1)}, u32[]{:S(2)}) copy-start(bf16[1024,384]{1,0:T(8,128)(2,1)} %attend.2.refs_0_) | copy-start | bytes 2359300
  174.7 21.2 %collective-permute-start.6 = (bf16[1024,384]{1,0:T(8,128)(2,1)}, bf16[1024,384]{1,0:T(8,128)(2,1)S(1)}, u32[]{:S(2)}, u32[]{:S(2)}) collective-permute-start(bf16[1024,384]{1,0:T(8,128)(2,1)} %attend.2.refs_0_), channel_id=1, source_target_pairs={{0,2},{1,3},{2,0},{3,1},{4,6},{5,7},{6,4},{7,5},{8,10},{9,11},{10,... | collective-permute-start | bytes 2359304 | tf_op jit(solution)/shard_map/ppermute | solution.py:85
  194.4 12.8 %collective-permute-start.14 = (bf16[1024,256]{1,0:T(8,128)(2,1)}, bf16[1024,256]{1,0:T(8,128)(2,1)S(1)}, u32[]{:S(2)}, u32[]{:S(2)}) collective-permute-start(bf16[1024,256]{1,0:T(8,128)(2,1)} %attend.3.refs_4_), channel_id=1, source_target_pairs={{0,2},{1,3},{2,0},{3,1},{4,6},{5,7},{6,4},{7,5},{8,10},{9,11},{10,... | collective-permute-start | bytes 1572872 | tf_op jit(solution)/shard_map/ppermute | solution.py:85
  198.1 18.5 %collective-permute-start.7 = (bf16[2048,384]{1,0:T(8,128)(2,1)}, bf16[2048,384]{1,0:T(8,128)(2,1)S(1)}, u32[]{:S(2)}, u32[]{:S(2)}) collective-permute-start(bf16[2048,384]{1,0:T(8,128)(2,1)} %pad_maximum_fusion.1), channel_id=1, source_target_pairs={{0,1},{1,0},{2,3},{3,2},{4,5},{5,4},{6,7},{7,6},{8,9},{9,8},{10,11... | collective-permute-start | bytes 4718600 | tf_op jit(solution)/shard_map/ppermute | solution.py:85
  208.3 3.0 %collective-permute-start.15 = (bf16[2048,256]{1,0:T(8,128)(2,1)}, bf16[2048,256]{1,0:T(8,128)(2,1)}, u32[]{:S(2)}, u32[]{:S(2)}) collective-permute-start(bf16[2048,256]{1,0:T(8,128)(2,1)} %pad_maximum_fusion.3), channel_id=1, source_target_pairs={{0,1},{1,0},{2,3},{3,2},{4,5},{5,4},{6,7},{7,6},{8,9},{9,8},{10,11... | collective-permute-start | bytes 3145736 | tf_op jit(solution)/shard_map/ppermute | solution.py:85
  231.3 26.0 %collective-permute-start.17 = (s16[528,1024]{1,0:T(8,128)(2,1)}, s16[528,1024]{1,0:T(8,128)(2,1)S(1)}, u32[]{:S(2)}, u32[]{:S(2)}) collective-permute-start(s16[528,1024]{1,0:T(8,128)(2,1)} %get-tuple-element.20), channel_id=1, source_target_pairs={{0,4},{1,5},{2,6},{3,7},{4,0},{5,1},{6,2},{7,3},{8,12},{9,13},{10,... | collective-permute-start | bytes 3244040 | tf_op jit(solution)/shard_map/ppermute | solution.py:85
  255.9 7.8 %collective-permute-start.16 = (s16[528,256]{1,0:T(8,128)(2,1)}, s16[528,256]{1,0:T(8,128)(2,1)S(1)}, u32[]{:S(2)}, u32[]{:S(2)}) collective-permute-start(s16[528,256]{1,0:T(8,128)(2,1)} %get-tuple-element.18), channel_id=1, source_target_pairs={{0,4},{1,5},{2,6},{3,7},{4,0},{5,1},{6,2},{7,3},{8,12},{9,13},{10,... | collective-permute-start | bytes 811016 | tf_op jit(solution)/shard_map/ppermute | solution.py:85
  (9 other events, 34.8 us)
Sparse Core Ops, SparseCore 0:
  9.2 109.1 all-gather.6
  119.9 96.6 all-gather.10
  218.2 31.2 all-gather.8

commit v7 on v6

--- a/solution.py
+++ b/solution.py
@@ -99,7 +99,7 @@
     rows, columns = value.shape
     groups = rows // 128
     peak = jnp.max(jnp.abs(value), axis=1, keepdims=True)
-    power = jnp.clip(jnp.floor(jnp.log2(jnp.maximum(peak, 1e-30))) + 1.0, -90.0, 120.0)
+    power = jnp.clip(jnp.floor(jnp.log2(jnp.maximum(peak, 1e-33))) + 1.0, -110.0, 120.0)
     scaled = jnp.clip(jnp.round(value * jnp.exp2(15.0 - power)), -32767.0, 32767.0)
     packed[:rows, :] = scaled.astype(jnp.int32).astype(jnp.int16)
     spread = jnp.where(diagonal(groups), power, 0.0).reshape(groups, 128, 128).sum(axis=1)
@@ -354,9 +354,9 @@
     near_block = lambda plane: lax.dynamic_slice(
         video_rows, (0, (2 * plane + 1 - x) * block), (rows, block)
     )
-    near_half = send(
-        jnp.concatenate([near_block(2 * core), near_block(2 * core + 1)], axis=1), ACROSS_X
-    )
+    near_half = jnp.concatenate([near_block(2 * core), near_block(2 * core + 1)], axis=1)
+    near_half, piece = lax.optimization_barrier((near_half, piece))
+    near_half = send(near_half, ACROSS_X)
     near = [near_half, send(near_half, ACROSS_CORE)]
     planes = jnp.arange(4, dtype=jnp.int32)
     by_core = planes ^ (2 * core)

time: 275 us -> 275 us (level)
  no operation moved by 1% of the time
where the time goes in v7:
time: 275 us; the launch traced here: 273 us
  waiting for transfers between devices  134 us (49%)
  Pallas kernels  56.4 us (21%)
  starting transfers between devices  31 us (11%)
  local copies, waits for them, and re-layouts  20.6 us (7%)
  other arithmetic  15.3 us (6%)
  between operations  13.3 us (5%)
    ppermute x18, waiting for transfers between devices, send(): return lax.ppermute(value, AXES, move)  67.4 us
    all_gather x3, waiting for transfers between devices, along_z(): return lax.all_gather(value, 'ctx', axis=0, axis_index_groups=SAME_X)  66.2 us
    ppermute x18, starting transfers between devices, send(): return lax.ppermute(value, AXES, move)  30.9 us
    pallas_call x2, Pallas kernels, query_product(): pl.pallas_call(query_body, grid_spec=pltpu.PrefetchScalarGridSpec(num_sca...  20.6 us
    pallas_call x2, Pallas kernels, out_product(): pl.pallas_call(functools.partial(out_body, k_sizes=k_sizes), grid_spec=pl...  19.8 us
    pallas_call x2, Pallas kernels, attend(): pl.pallas_call(functools.partial(attend_body, audio_length=audio_length,...  11 us
    another operation x4, other arithmetic, plane_shards(): jnp.stack([piece, swapped, jnp.where(is_mid, last, to_end), jnp.where(is_...  6.49 us
    unnamed x42, local copies, waits for them, and re-layouts  6.14 us
  transfers between devices with their start and end apart: 21, of which 11 were waited for; matrix products, arithmetic and copies ran while one was open for 11% of the time, Pallas kernels for 20%

profile of v7, /device:TPU:0, one launch (start us, length us, event | category | flops | bytes accessed | tf_op | source)
XLA Modules:
  0.0 272.9 jit_solution(13503609125301345346)
XLA Ops:
  9.1 2.5 slice.47
  16.6 2.9 %collective-permute-start = (bf16[512,1280]{1,0:T(8,128)(2,1)}, bf16[512,1280]{1,0:T(8,128)(2,1)S(1)}, u32[]{:S(2)}, u32[]{:S(2)}) collective-permute-start(bf16[512,1280]{1,0:T(8,128)(2,1)} %pad_maximum_fusion.2), channel_id=1, source_target_pairs={{0,4},{1,5},{2,6},{3,7},{4,0},{5,1},{6,2},{7,3},{8,12},{9,13},{10,... | collective-permute-start | bytes 3932168 | tf_op jit(solution)/shard_map/ppermute | solution.py:85
  19.5 1.6 collective-permute-start.8
  21.1 6.5 %collective-permute-start.10 = (bf16[640,512]{1,0:T(8,128)(2,1)}, bf16[640,512]{1,0:T(8,128)(2,1)}, u32[]{:S(2)}, u32[]{:S(2)}) collective-permute-start(bf16[640,512]{1,0:T(8,128)(2,1)} %get-tuple-element.32), channel_id=1, source_target_pairs={{0,0},{1,1},{2,2},{3,3},{4,4},{5,5},{6,6},{7,7},{8,16},{9,17},{10,... | collective-permute-start | bytes 1966088 | tf_op jit(solution)/shard_map/ppermute | solution.py:85
  30.1 18.6 %collective-permute-done.refs_4_.refs_5_ = bf16[512,1280]{1,0:T(8,128)(2,1)S(1)} collective-permute-done((bf16[512,1280]{1,0:T(8,128)(2,1)}, bf16[512,1280]{1,0:T(8,128)(2,1)S(1)}, u32[]{:S(2)}, u32[]{:S(2)}) %collective-permute-start) | collective-permute-done | bytes 1310752 | tf_op jit(solution)/shard_map/ppermute | solution.py:85
  49.1 1.9 collective-permute-start.4
  52.1 12.1 %collective-permute-done.8 = bf16[640,512]{1,0:T(8,128)(2,1)} collective-permute-done((bf16[640,512]{1,0:T(8,128)(2,1)}, bf16[640,512]{1,0:T(8,128)(2,1)}, u32[]{:S(2)}, u32[]{:S(2)}) %collective-permute-start.8) | collective-permute-done | bytes 655392 | tf_op jit(solution)/shard_map/ppermute | solution.py:85
  64.2 6.5 %collective-permute-start.9 = (bf16[640,512]{1,0:T(8,128)(2,1)}, bf16[640,512]{1,0:T(8,128)(2,1)}, u32[]{:S(2)}, u32[]{:S(2)}) collective-permute-start(bf16[640,512]{1,0:T(8,128)(2,1)} %collective-permute-done.8), channel_id=1, source_target_pairs={{0,0},{1,1},{2,2},{3,3},{4,4},{5,5},{6,6},{7,7},{8,16},{9,17},{10,... | collective-permute-start | bytes 1966088 | tf_op jit(solution)/shard_map/ppermute | solution.py:85
  72.7 1.5 collective-permute-start.12
  74.2 44.2 %all-gather.7.cloned.1.call-done = bf16[2560,768]{1,0:T(8,128)(2,1)} async-done(((bf16[640,768]{1,0:T(8,128)(2,1)}), bf16[2560,768]{1,0:T(8,128)(2,1)}) %all-gather.7.cloned.1.call-update) | async-done | bytes 3932176 | tf_op jit(solution)/shard_map/all_gather | solution.py:89
  118.4 11.8 %query_product.2 = (f32[1024,384]{1,0:T(8,128)}, f32[1024,384]{1,0:T(8,128)}) custom-call(s32[10]{0:T(128)} %pad_add_fusion.place, bf16[512,5120]{1,0:T(8,128)(2,1)} %refs_3_.3, bf16[512,5120]{1,0:T(8,128)(2,1)} %refs_3_.3, bf16[512,5120]{1,0:T(8,128)(2,1)} %refs_3_.3, bf16[512,5120]{1,0:T(8,128)(2,1)} %refs_3_.3, bf16[512,1280]{1,0:T(8,128)(2,1)} %copy-done.1, ...), custom_call_target="tpu_custom_call" | custom-call | flops 4026531840 | bytes 12320768 | tf_op jit(solution)/shard_map/query_product/pallas_call | solution.py:160
  130.2 1.5 collective-permute-start.2
  133.3 1.6 reshape.44
  137.3 2.9 %pad_maximum_fusion.refs_8_.refs_9_ = bf16[4,640,512]{2,1,0:T(8,128)(2,1)} fusion(bf16[1,640,512]{2,1,0:T(8,128)(2,1)S(1)} %select_bitcast_fusion, bf16[1,640,512]{2,1,0:T(8,128)(2,1)S(1)} %select_bitcast_fusion.1, bf16[1,640,512]{2,1,0:T(8,128)(2,1)} %bitcast.7, bf16[1,640,512]{2,1,0:T(8,128)(2,1)S(1)} %copy-done.7), kind=kLoop, calls=%fused_computation | loop fusion | flops 3932160 | bytes 5242880 | tf_op jit(solution)/shard_map/stack | solution.py:345
  140.2 8.8 %query_product.3 = (f32[1024,256]{1,0:T(8,128)}, f32[1024,256]{1,0:T(8,128)}) custom-call(s32[10]{0:T(128)} %get-tuple-element.23.place, bf16[512,5120]{1,0:T(8,128)(2,1)} %refs_3_.3, bf16[512,5120]{1,0:T(8,128)(2,1)} %refs_3_.3, bf16[512,5120]{1,0:T(8,128)(2,1)} %refs_3_.3, bf16[512,5120]{1,0:T(8,128)(2,1)} %refs_3_.3, bf16[512,1280]{1,0:T(8,128)(2,1)} %copy-done.1, ...), custom_call_target="tpu_custom_call" | custom-call | flops 2684354560 | bytes 9961472 | tf_op jit(solution)/shard_map/query_product/pallas_call | solution.py:160
  151.6 1.6 convolution_convert_fusion
  153.8 13.9 %collective-permute-done.2.received = f32[1024,384]{1,0:T(8,128)S(1)} collective-permute-done((f32[1024,384]{1,0:T(8,128)}, f32[1024,384]{1,0:T(8,128)S(1)}, u32[]{:S(2)}, u32[]{:S(2)}) %collective-permute-start.2) | collective-permute-done | bytes 1572896 | tf_op jit(solution)/shard_map/ppermute | solution.py:85
  169.0 5.7 %attend.2.refs_0_ = bf16[1024,384]{1,0:T(8,128)(2,1)} custom-call(f32[1024,384]{1,0:T(8,128)} %get-tuple-element.15.kept, f32[1024,384]{1,0:T(8,128)} %copy-done.9, bf16[64,384]{1,0:T(8,128)(2,1)} %slice.48.keys, bf16[64,384]{1,0:T(8,128)(2,1)} %slice.49.values, s32[1024,1]{1,0:T(8,128)} %bitcast.26), custom_call_target="tpu_custom_call" | custom-call | flops 100663296 | bytes 3932160 | tf_op jit(solution)/shard_map/attend/pallas_call | solution.py:263
  178.8 10.2 %collective-permute-done.13.received = f32[1024,256]{1,0:T(8,128)} collective-permute-done((f32[1024,256]{1,0:T(8,128)}, f32[1024,256]{1,0:T(8,128)}, u32[]{:S(2)}, u32[]{:S(2)}) %collective-permute-start.13) | collective-permute-done | bytes 1048608 | tf_op jit(solution)/shard_map/ppermute | solution.py:85
  189.1 5.3 %attend.3.refs_4_ = bf16[1024,256]{1,0:T(8,128)(2,1)} custom-call(f32[1024,256]{1,0:T(8,128)} %get-tuple-element.17.kept, f32[1024,256]{1,0:T(8,128)} %collective-permute-done.13.received, bf16[64,256]{1,0:T(8,128)(2,1)} %slice.52.keys, bf16[64,256]{1,0:T(8,128)(2,1)} %slice.53.values, s32[1024,1]{1,0:T(8,128)} %bitcast.27), custom_call_target="tpu_custom_call" | custom-call | flops 67108864 | bytes 2621440 | tf_op jit(solution)/shard_map/attend/pallas_call | solution.py:263
  194.4 1.5 collective-permute-start.14
  198.1 9.1 %collective-permute-done.14.refs_6_ = bf16[1024,256]{1,0:T(8,128)(2,1)S(1)} collective-permute-done((bf16[1024,256]{1,0:T(8,128)(2,1)}, bf16[1024,256]{1,0:T(8,128)(2,1)S(1)}, u32[]{:S(2)}, u32[]{:S(2)}) %collective-permute-start.14) | collective-permute-done | bytes 524320 | tf_op jit(solution)/shard_map/ppermute | solution.py:85
  208.3 1.7 slice.46
  211.3 5.3 %all-gather.11.cloned.1.call-done = bf16[2560,1024]{1,0:T(8,128)(2,1)} async-done(((bf16[640,1024]{1,0:T(8,128)(2,1)}), bf16[2560,1024]{1,0:T(8,128)(2,1)}) %all-gather.11.cloned.1.call-update) | async-done | bytes 5242896 | tf_op jit(solution)/shard_map/all_gather | solution.py:89
  217.9 13.4 %out_product.3 = (f32[512,1024]{1,0:T(8,128)}, s16[528,1024]{1,0:T(8,128)(2,1)}) custom-call(s32[4]{0:T(128)} %iota_xor_fusion.1.place, bf16[1024,384]{1,0:T(8,128)(2,1)} %attend.2.refs_0_, bf16[2048,384]{1,0:T(8,128)(2,1)} %copy-done.3, bf16[1024,384]{1,0:T(8,128)(2,1)} %copy-done.6, bf16[2048,384]{1,0:T(8,128)(2,1)} %copy-done.3, ...), custom_call_target="tpu_custom_call" | custom-call | flops 5368709120 | bytes 14680064 | tf_op jit(solution)/shard_map/out_product/pallas_call | solution.py:210
  231.3 1.5 collective-permute-start.17
  232.8 16.7 %all-gather.9.cloned.1.call-done = bf16[2560,256]{1,0:T(8,128)(2,1)} async-done(((bf16[640,256]{1,0:T(8,128)(2,1)}), bf16[2560,256]{1,0:T(8,128)(2,1)}) %all-gather.9.cloned.1.call-update) | async-done | bytes 1310736 | tf_op jit(solution)/shard_map/all_gather | solution.py:89
  249.5 6.4 %out_product.2 = (f32[512,256]{1,0:T(8,128)}, s16[528,256]{1,0:T(8,128)(2,1)}) custom-call(s32[4]{0:T(128)} %iota_xor_fusion.1.place, bf16[1024,384]{1,0:T(8,128)(2,1)} %attend.2.refs_0_, bf16[2048,384]{1,0:T(8,128)(2,1)} %copy-done.3, bf16[1024,384]{1,0:T(8,128)(2,1)} %copy-done.6, bf16[2048,384]{1,0:T(8,128)(2,1)} %copy-done.3, ...), custom_call_target="tpu_custom_call" | custom-call | flops 1342177280 | bytes 7602176 | tf_op jit(solution)/shard_map/out_product/pallas_call | solution.py:210
  255.9 1.5 collective-permute-start.16
  258.4 2.9 %finish.2.refs_0_ = bf16[512,1280]{1,0:T(8,128)(2,1)} custom-call(f32[512,1024]{1,0:T(8,128)} %get-tuple-element.21.kept, s16[528,1024]{1,0:T(8,128)(2,1)} %copy-done.5, s16[528,1024]{1,0:T(8,128)(2,1)} %copy-done.5), custom_call_target="tpu_custom_call" | custom-call | flops 1048576 | bytes 4194304 | tf_op jit(solution)/shard_map/finish/pallas_call | solution.py:295
  261.3 2.4 collective-permute-done.16.received.scales
  264.4 2.0 finish.3
  (100 shorter events, 33.6 us)
Async XLA Ops:
  6.5 143.3 %copy-start = (bf16[768,1280]{1,0:T(8,128)(2,1)S(1)}, bf16[768,1280]{1,0:T(8,128)(2,1)}, u32[]{:S(2)}) copy-start(bf16[768,1280]{1,0:T(8,128)(2,1)} %param.13) | copy-start | bytes 5898244
  6.5 111.8 %all-gather.7.cloned.1.call-start = ((), (), s32[]{:S(2)}) async-start(), calls=%async_computation | async-start | bytes 4915200 | tf_op jit(solution)/shard_map/all_gather | solution.py:89
  9.1 207.6 %all-gather.11.cloned.1.call-start = ((), (), s32[]{:S(2)}) async-start(), calls=%async_computation.2 | async-start | bytes 6553600 | tf_op jit(solution)/shard_map/all_gather | solution.py:89
  11.6 237.9 %all-gather.9.cloned.1.call-start = ((), (), s32[]{:S(2)}) async-start(), calls=%async_computation.1 | async-start | bytes 1638400 | tf_op jit(solution)/shard_map/all_gather | solution.py:89
  15.4 12.3 %copy-start.17 = (s32[2,512]{1,0:T(2,128)S(1)}, s32[2,512]{1,0:T(2,128)}, u32[]{:S(2)}) copy-start(s32[2,512]{1,0:T(2,128)} %param.15) | copy-start | bytes 12292
  15.4 12.8 %copy-start.19 = (s32[2]{0:T(128)S(1)}, s32[2]{0:T(128)}, u32[]{:S(2)}) copy-start(s32[2]{0:T(128)} %constant.56) | copy-start | bytes 28
  16.6 32.2 %collective-permute-start = (bf16[512,1280]{1,0:T(8,128)(2,1)}, bf16[512,1280]{1,0:T(8,128)(2,1)S(1)}, u32[]{:S(2)}, u32[]{:S(2)}) collective-permute-start(bf16[512,1280]{1,0:T(8,128)(2,1)} %pad_maximum_fusion.2), channel_id=1, source_target_pairs={{0,4},{1,5},{2,6},{3,7},{4,0},{5,1},{6,2},{7,3},{8,12},{9,13},{10,... | collective-permute-start | bytes 3932168 | tf_op jit(solution)/shard_map/ppermute | solution.py:85
  19.5 44.7 %collective-permute-start.8 = (bf16[640,512]{1,0:T(8,128)(2,1)}, bf16[640,512]{1,0:T(8,128)(2,1)}, u32[]{:S(2)}, u32[]{:S(2)}) collective-permute-start(bf16[640,512]{1,0:T(8,128)(2,1)} %get-tuple-element.32), channel_id=1, source_target_pairs={{0,8},{1,9},{2,10},{3,11},{4,12},{5,13},{6,14},{7,15},{8,0},{9,1},... | collective-permute-start | bytes 1966088 | tf_op jit(solution)/shard_map/ppermute | solution.py:85
  21.1 50.3 %collective-permute-start.10 = (bf16[640,512]{1,0:T(8,128)(2,1)}, bf16[640,512]{1,0:T(8,128)(2,1)}, u32[]{:S(2)}, u32[]{:S(2)}) collective-permute-start(bf16[640,512]{1,0:T(8,128)(2,1)} %get-tuple-element.32), channel_id=1, source_target_pairs={{0,0},{1,1},{2,2},{3,3},{4,4},{5,5},{6,6},{7,7},{8,16},{9,17},{10,... | collective-permute-start | bytes 1966088 | tf_op jit(solution)/shard_map/ppermute | solution.py:85
  28.3 101.9 %copy-start.11 = (bf16[1,6656]{1,0:T(2,128)(2,1)}, bf16[1,6656]{1,0:T(2,128)(2,1)S(1)}, u32[]{:S(2)}) copy-start(bf16[1,6656]{1,0:T(2,128)(2,1)S(1)} %broadcast_in_dim.2) | copy-start | bytes 39940
  28.3 20.8 %collective-permute-start.3 = (bf16[1,6656]{1,0:T(2,128)(2,1)S(1)}, bf16[1,6656]{1,0:T(2,128)(2,1)S(1)}, u32[]{:S(2)}, u32[]{:S(2)}) collective-permute-start(bf16[1,6656]{1,0:T(2,128)(2,1)S(1)} %broadcast_in_dim.2), channel_id=1, source_target_pairs={{0,4},{1,5},{2,6},{3,7},{4,0},{5,1},{6,2},{7,3},{8,12},{9,13},{10,... | collective-permute-start | bytes 39944 | tf_op jit(solution)/shard_map/ppermute | solution.py:85
  48.8 69.6 %copy-start.1 = (bf16[512,1280]{1,0:T(8,128)(2,1)}, bf16[512,1280]{1,0:T(8,128)(2,1)S(1)}, u32[]{:S(2)}) copy-start(bf16[512,1280]{1,0:T(8,128)(2,1)S(1)} %collective-permute-done.refs_4_.refs_5_) | copy-start | bytes 3932164
  48.8 25.4 %collective-permute-start.1 = (bf16[512,1280]{1,0:T(8,128)(2,1)S(1)}, bf16[512,1280]{1,0:T(8,128)(2,1)}, u32[]{:S(2)}, u32[]{:S(2)}) collective-permute-start(bf16[512,1280]{1,0:T(8,128)(2,1)S(1)} %collective-permute-done.refs_4_.refs_5_), channel_id=1, source_target_pairs={{0,1},{1,0},{2,3},{3,2},{4,5},{5,4},{6,7},{7,6},{8,9},{9,8},{10,11... | collective-permute-start | bytes 3932168 | tf_op jit(solution)/shard_map/ppermute | solution.py:85
  49.1 81.1 %copy-start.12 = (bf16[1,6656]{1,0:T(2,128)(2,1)}, bf16[1,6656]{1,0:T(2,128)(2,1)S(1)}, u32[]{:S(2)}) copy-start(bf16[1,6656]{1,0:T(2,128)(2,1)S(1)} %collective-permute-done.3) | copy-start | bytes 39940
  49.1 21.6 %collective-permute-start.4 = (bf16[2,6656]{1,0:T(2,128)(2,1)S(1)}, bf16[2,6656]{1,0:T(2,128)(2,1)S(1)}, u32[]{:S(2)}, u32[]{:S(2)}) collective-permute-start(bf16[2,6656]{1,0:T(2,128)(2,1)S(1)} %pad_maximum_fusion.11), channel_id=1, source_target_pairs={{0,8},{1,9},{2,10},{3,11},{4,12},{5,13},{6,14},{7,15},{8,0},{9,1},... | collective-permute-start | bytes 79880 | tf_op jit(solution)/shard_map/ppermute | solution.py:85
  64.2 8.5 %collective-permute-start.9 = (bf16[640,512]{1,0:T(8,128)(2,1)}, bf16[640,512]{1,0:T(8,128)(2,1)}, u32[]{:S(2)}, u32[]{:S(2)}) collective-permute-start(bf16[640,512]{1,0:T(8,128)(2,1)} %collective-permute-done.8), channel_id=1, source_target_pairs={{0,0},{1,1},{2,2},{3,3},{4,4},{5,5},{6,6},{7,7},{8,16},{9,17},{10,... | collective-permute-start | bytes 1966088 | tf_op jit(solution)/shard_map/ppermute | solution.py:85
  70.7 59.5 %copy-start.15 = (bf16[2,6656]{1,0:T(2,128)(2,1)}, bf16[2,6656]{1,0:T(2,128)(2,1)S(1)}, u32[]{:S(2)}) copy-start(bf16[2,6656]{1,0:T(2,128)(2,1)S(1)} %collective-permute-done.4) | copy-start | bytes 79876
  71.4 60.3 %collective-permute-start.5 = (bf16[4,6656]{1,0:T(4,128)(2,1)}, bf16[4,6656]{1,0:T(4,128)(2,1)}, u32[]{:S(2)}, u32[]{:S(2)}) collective-permute-start(bf16[4,6656]{1,0:T(4,128)(2,1)} %pad_maximum_fusion.9), channel_id=1, source_target_pairs={{0,16},{1,17},{2,18},{3,19},{4,20},{5,21},{6,22},{7,23},{8,24},{9,... | collective-permute-start | bytes 159752 | tf_op jit(solution)/shard_map/ppermute | solution.py:85
  71.4 63.5 %collective-permute-start.11 = (bf16[640,512]{1,0:T(8,128)(2,1)}, bf16[640,512]{1,0:T(8,128)(2,1)}, u32[]{:S(2)}, u32[]{:S(2)}) collective-permute-start(bf16[640,512]{1,0:T(8,128)(2,1)} %collective-permute-done.10), channel_id=1, source_target_pairs={{8,0},{9,1},{10,2},{11,3},{12,4},{13,5},{14,6},{15,7},{16,24},{17,... | collective-permute-start | bytes 1966088 | tf_op jit(solution)/shard_map/ppermute | solution.py:85
  72.7 63.4 %collective-permute-start.12 = (bf16[640,512]{1,0:T(8,128)(2,1)}, bf16[640,512]{1,0:T(8,128)(2,1)}, u32[]{:S(2)}, u32[]{:S(2)}) collective-permute-start(bf16[640,512]{1,0:T(8,128)(2,1)} %collective-permute-done.9), channel_id=1, source_target_pairs={{8,0},{9,1},{10,2},{11,3},{12,4},{13,5},{14,6},{15,7},{16,24},{17,... | collective-permute-start | bytes 1966088 | tf_op jit(solution)/shard_map/ppermute | solution.py:85
  130.2 37.6 %collective-permute-start.2 = (f32[1024,384]{1,0:T(8,128)}, f32[1024,384]{1,0:T(8,128)S(1)}, u32[]{:S(2)}, u32[]{:S(2)}) collective-permute-start(f32[1024,384]{1,0:T(8,128)} %get-tuple-element.16), channel_id=1, source_target_pairs={{0,4},{1,5},{2,6},{3,7},{4,0},{5,1},{6,2},{7,3},{8,12},{9,13},{10,... | collective-permute-start | bytes 4718600 | tf_op jit(solution)/shard_map/ppermute | solution.py:85
  149.1 40.0 %collective-permute-start.13 = (f32[1024,256]{1,0:T(8,128)}, f32[1024,256]{1,0:T(8,128)}, u32[]{:S(2)}, u32[]{:S(2)}) collective-permute-start(f32[1024,256]{1,0:T(8,128)} %get-tuple-element.18), channel_id=1, source_target_pairs={{0,4},{1,5},{2,6},{3,7},{4,0},{5,1},{6,2},{7,3},{8,12},{9,13},{10,... | collective-permute-start | bytes 3145736 | tf_op jit(solution)/shard_map/ppermute | solution.py:85
  151.0 16.8 %copy-start.13 = (bf16[64,640]{1,0:T(8,128)(2,1)}, bf16[64,640]{1,0:T(8,128)(2,1)S(1)}, u32[]{:S(2)}) copy-start(bf16[64,640]{1,0:T(8,128)(2,1)S(1)} %convolution_convert_fusion.1) | copy-start | bytes 245764
  153.2 14.6 %copy-start.14 = (bf16[64,640]{1,0:T(8,128)(2,1)}, bf16[64,640]{1,0:T(8,128)(2,1)S(1)}, u32[]{:S(2)}) copy-start(bf16[64,640]{1,0:T(8,128)(2,1)S(1)} %convolution_convert_fusion) | copy-start | bytes 245764
  174.7 22.1 %copy-start.2 = (bf16[1024,384]{1,0:T(8,128)(2,1)S(1)}, bf16[1024,384]{1,0:T(8,128)(2,1)}, u32[]{:S(2)}) copy-start(bf16[1024,384]{1,0:T(8,128)(2,1)} %attend.2.refs_0_) | copy-start | bytes 2359300
  174.7 21.2 %collective-permute-start.6 = (bf16[1024,384]{1,0:T(8,128)(2,1)}, bf16[1024,384]{1,0:T(8,128)(2,1)S(1)}, u32[]{:S(2)}, u32[]{:S(2)}) collective-permute-start(bf16[1024,384]{1,0:T(8,128)(2,1)} %attend.2.refs_0_), channel_id=1, source_target_pairs={{0,2},{1,3},{2,0},{3,1},{4,6},{5,7},{6,4},{7,5},{8,10},{9,11},{10,... | collective-permute-start | bytes 2359304 | tf_op jit(solution)/shard_map/ppermute | solution.py:85
  194.4 12.9 %copy-start.4 = (bf16[1024,256]{1,0:T(8,128)(2,1)S(1)}, bf16[1024,256]{1,0:T(8,128)(2,1)}, u32[]{:S(2)}) copy-start(bf16[1024,256]{1,0:T(8,128)(2,1)} %attend.3.refs_4_) | copy-start | bytes 1572868
  194.4 12.8 %collective-permute-start.14 = (bf16[1024,256]{1,0:T(8,128)(2,1)}, bf16[1024,256]{1,0:T(8,128)(2,1)S(1)}, u32[]{:S(2)}, u32[]{:S(2)}) collective-permute-start(bf16[1024,256]{1,0:T(8,128)(2,1)} %attend.3.refs_4_), channel_id=1, source_target_pairs={{0,2},{1,3},{2,0},{3,1},{4,6},{5,7},{6,4},{7,5},{8,10},{9,11},{10,... | collective-permute-start | bytes 1572872 | tf_op jit(solution)/shard_map/ppermute | solution.py:85
  198.1 18.5 %collective-permute-start.7 = (bf16[2048,384]{1,0:T(8,128)(2,1)}, bf16[2048,384]{1,0:T(8,128)(2,1)S(1)}, u32[]{:S(2)}, u32[]{:S(2)}) collective-permute-start(bf16[2048,384]{1,0:T(8,128)(2,1)} %pad_maximum_fusion.1), channel_id=1, source_target_pairs={{0,1},{1,0},{2,3},{3,2},{4,5},{5,4},{6,7},{7,6},{8,9},{9,8},{10,11... | collective-permute-start | bytes 4718600 | tf_op jit(solution)/shard_map/ppermute | solution.py:85
  208.3 3.0 %collective-permute-start.15 = (bf16[2048,256]{1,0:T(8,128)(2,1)}, bf16[2048,256]{1,0:T(8,128)(2,1)}, u32[]{:S(2)}, u32[]{:S(2)}) collective-permute-start(bf16[2048,256]{1,0:T(8,128)(2,1)} %pad_maximum_fusion.3), channel_id=1, source_target_pairs={{0,1},{1,0},{2,3},{3,2},{4,5},{5,4},{6,7},{7,6},{8,9},{9,8},{10,11... | collective-permute-start | bytes 3145736 | tf_op jit(solution)/shard_map/ppermute | solution.py:85
  231.3 26.0 %collective-permute-start.17 = (s16[528,1024]{1,0:T(8,128)(2,1)}, s16[528,1024]{1,0:T(8,128)(2,1)S(1)}, u32[]{:S(2)}, u32[]{:S(2)}) collective-permute-start(s16[528,1024]{1,0:T(8,128)(2,1)} %get-tuple-element.22), channel_id=1, source_target_pairs={{0,4},{1,5},{2,6},{3,7},{4,0},{5,1},{6,2},{7,3},{8,12},{9,13},{10,... | collective-permute-start | bytes 3244040 | tf_op jit(solution)/shard_map/ppermute | solution.py:85
  255.9 7.8 %collective-permute-start.16 = (s16[528,256]{1,0:T(8,128)(2,1)}, s16[528,256]{1,0:T(8,128)(2,1)S(1)}, u32[]{:S(2)}, u32[]{:S(2)}) collective-permute-start(s16[528,256]{1,0:T(8,128)(2,1)} %get-tuple-element.20), channel_id=1, source_target_pairs={{0,4},{1,5},{2,6},{3,7},{4,0},{5,1},{6,2},{7,3},{8,12},{9,13},{10,... | collective-permute-start | bytes 811016 | tf_op jit(solution)/shard_map/ppermute | solution.py:85
  (9 other events, 33.1 us)
Sparse Core Ops, SparseCore 0:
  9.2 109.1 all-gather.6
  119.9 96.6 all-gather.10
  218.2 31.2 all-gather.8

commit v8 on v7

--- a/solution.py
+++ b/solution.py
@@ -141,18 +141,18 @@
 def query_product(place, video_rows, near, weights):
     rows = video_rows.shape[0]
     depth, columns = weights.shape[1:]
-    step = rows // 2
+    step = rows
     half = columns // 2
     own_specs = [
         pl.BlockSpec(
             (step, depth),
-            functools.partial(lambda j, i, place: (jnp.minimum(i, 1), place[j]), j),
+            functools.partial(lambda j, i, place: (0, place[j]), j),
         )
         for j in range(4)
     ]
     near_specs = [
         pl.BlockSpec(
-            (step, depth), functools.partial(lambda j, i, place: (jnp.maximum(i - 2, 0), j % 2), j)
+            (step, depth), functools.partial(lambda j, i, place: (0, j % 2), j)
         )
         for j in range(4)
     ]
@@ -161,7 +161,7 @@
         query_body,
         grid_spec=pltpu.PrefetchScalarGridSpec(
             num_scalar_prefetch=1,
-            grid=(4,),
+            grid=(2,),
             in_specs=own_specs
             + near_specs
             + [
@@ -184,12 +184,9 @@
     *lefts, weights, kept, sent = refs
     total = None
     for j in range(4):
-        first = 0
-        for i, size in enumerate(k_sizes):
-            right = weights[place[j], first : first + size, :]
-            term = jnp.dot(lefts[i * 4 + j][...], right, preferred_element_type=jnp.float32)
-            total = term if total is None else total + term
-            first += size
+        left = jnp.concatenate([lefts[i * 4 + j][...] for i in range(len(k_sizes))], axis=1)
+        term = jnp.dot(left, weights[place[j]], preferred_element_type=jnp.float32)
+        total = term if total is None else total + term
     pl.when(pl.program_id(0) == 0)(lambda: pack(total, sent))
     pl.when(pl.program_id(0) == 1)(lambda: kept.__setitem__(..., total))
 

time: 275 us -> 275 us (level)
  transfers between devices with their start and end apart: 21 -> 21, of which waited for: 11 -> 12; matrix products, arithmetic and copies ran while one was open for 11% -> 11% of each run, Pallas kernels for 20% -> 20%
where the time goes in v8:
time: 275 us; the launch traced here: 273 us
  waiting for transfers between devices  133 us (48%)
  Pallas kernels  56.6 us (21%)
  starting transfers between devices  30.9 us (11%)
  local copies, waits for them, and re-layouts  20.6 us (7%)
  other arithmetic  15.3 us (6%)
  between operations  13.3 us (5%)
    ppermute x18, waiting for transfers between devices, send(): return lax.ppermute(value, AXES, move)  67.6 us
    all_gather x3, waiting for transfers between devices, along_z(): return lax.all_gather(value, 'ctx', axis=0, axis_index_groups=SAME_X)  65.8 us
    ppermute x18, starting transfers between devices, send(): return lax.ppermute(value, AXES, move)  30.8 us
    pallas_call x2, Pallas kernels, query_product(): pl.pallas_call(query_body, grid_spec=pltpu.PrefetchScalarGridSpec(num_sca...  20.7 us
    pallas_call x2, Pallas kernels, out_product(): pl.pallas_call(functools.partial(out_body, k_sizes=k_sizes), grid_spec=pl...  20 us
    pallas_call x2, Pallas kernels, attend(): pl.pallas_call(functools.partial(attend_body, audio_length=audio_length,...  11 us
    another operation x4, other arithmetic, plane_shards(): jnp.stack([piece, swapped, jnp.where(is_mid, last, to_end), jnp.where(is_...  6.49 us
    unnamed x42, local copies, waits for them, and re-layouts  6.14 us
  transfers between devices with their start and end apart: 21, of which 12 were waited for; matrix products, arithmetic and copies ran while one was open for 11% of the time, Pallas kernels for 20%

profile of v8, /device:TPU:0, one launch (start us, length us, event | category | flops | bytes accessed | tf_op | source)
XLA Modules:
  0.0 272.9 jit_solution(2842848806074544997)
XLA Ops:
  9.1 2.5 slice.47
  16.6 2.9 %collective-permute-start = (bf16[512,1280]{1,0:T(8,128)(2,1)}, bf16[512,1280]{1,0:T(8,128)(2,1)S(1)}, u32[]{:S(2)}, u32[]{:S(2)}) collective-permute-start(bf16[512,1280]{1,0:T(8,128)(2,1)} %pad_maximum_fusion.2), channel_id=1, source_target_pairs={{0,4},{1,5},{2,6},{3,7},{4,0},{5,1},{6,2},{7,3},{8,12},{9,13},{10,... | collective-permute-start | bytes 3932168 | tf_op jit(solution)/shard_map/ppermute | solution.py:85
  19.5 1.6 collective-permute-start.8
  21.1 6.5 %collective-permute-start.10 = (bf16[640,512]{1,0:T(8,128)(2,1)}, bf16[640,512]{1,0:T(8,128)(2,1)}, u32[]{:S(2)}, u32[]{:S(2)}) collective-permute-start(bf16[640,512]{1,0:T(8,128)(2,1)} %get-tuple-element.32), channel_id=1, source_target_pairs={{0,0},{1,1},{2,2},{3,3},{4,4},{5,5},{6,6},{7,7},{8,16},{9,17},{10,... | collective-permute-start | bytes 1966088 | tf_op jit(solution)/shard_map/ppermute | solution.py:85
  30.1 18.6 %collective-permute-done.refs_4_.refs_5_ = bf16[512,1280]{1,0:T(8,128)(2,1)S(1)} collective-permute-done((bf16[512,1280]{1,0:T(8,128)(2,1)}, bf16[512,1280]{1,0:T(8,128)(2,1)S(1)}, u32[]{:S(2)}, u32[]{:S(2)}) %collective-permute-start) | collective-permute-done | bytes 1310752 | tf_op jit(solution)/shard_map/ppermute | solution.py:85
  49.1 1.9 collective-permute-start.4
  52.1 12.1 %collective-permute-done.8 = bf16[640,512]{1,0:T(8,128)(2,1)} collective-permute-done((bf16[640,512]{1,0:T(8,128)(2,1)}, bf16[640,512]{1,0:T(8,128)(2,1)}, u32[]{:S(2)}, u32[]{:S(2)}) %collective-permute-start.8) | collective-permute-done | bytes 655392 | tf_op jit(solution)/shard_map/ppermute | solution.py:85
  64.2 6.5 %collective-permute-start.9 = (bf16[640,512]{1,0:T(8,128)(2,1)}, bf16[640,512]{1,0:T(8,128)(2,1)}, u32[]{:S(2)}, u32[]{:S(2)}) collective-permute-start(bf16[640,512]{1,0:T(8,128)(2,1)} %collective-permute-done.8), channel_id=1, source_target_pairs={{0,0},{1,1},{2,2},{3,3},{4,4},{5,5},{6,6},{7,7},{8,16},{9,17},{10,... | collective-permute-start | bytes 1966088 | tf_op jit(solution)/shard_map/ppermute | solution.py:85
  72.7 1.5 collective-permute-start.12
  74.2 44.2 %all-gather.7.cloned.1.call-done = bf16[2560,768]{1,0:T(8,128)(2,1)} async-done(((bf16[640,768]{1,0:T(8,128)(2,1)}), bf16[2560,768]{1,0:T(8,128)(2,1)}) %all-gather.7.cloned.1.call-update) | async-done | bytes 3932176 | tf_op jit(solution)/shard_map/all_gather | solution.py:89
  118.4 12.0 %query_product.2 = (f32[1024,384]{1,0:T(8,128)}, f32[1024,384]{1,0:T(8,128)}) custom-call(s32[10]{0:T(128)} %pad_add_fusion.place, bf16[512,5120]{1,0:T(8,128)(2,1)} %refs_3_.3, bf16[512,5120]{1,0:T(8,128)(2,1)} %refs_3_.3, bf16[512,5120]{1,0:T(8,128)(2,1)} %refs_3_.3, bf16[512,5120]{1,0:T(8,128)(2,1)} %refs_3_.3, bf16[512,1280]{1,0:T(8,128)(2,1)} %copy-done.1, ...), custom_call_target="tpu_custom_call" | custom-call | flops 4026531840 | bytes 12320768 | tf_op jit(solution)/shard_map/query_product/pallas_call | solution.py:160
  130.4 1.5 collective-permute-start.2
  133.5 1.6 reshape.44
  137.5 2.9 %pad_maximum_fusion.refs_8_.refs_9_ = bf16[4,640,512]{2,1,0:T(8,128)(2,1)} fusion(bf16[1,640,512]{2,1,0:T(8,128)(2,1)S(1)} %select_bitcast_fusion, bf16[1,640,512]{2,1,0:T(8,128)(2,1)S(1)} %select_bitcast_fusion.1, bf16[1,640,512]{2,1,0:T(8,128)(2,1)} %bitcast.7, bf16[1,640,512]{2,1,0:T(8,128)(2,1)S(1)} %copy-done.7), kind=kLoop, calls=%fused_computation | loop fusion | flops 3932160 | bytes 5242880 | tf_op jit(solution)/shard_map/stack | solution.py:342
  140.5 8.7 %query_product.3 = (f32[1024,256]{1,0:T(8,128)}, f32[1024,256]{1,0:T(8,128)}) custom-call(s32[10]{0:T(128)} %get-tuple-element.23.place, bf16[512,5120]{1,0:T(8,128)(2,1)} %refs_3_.3, bf16[512,5120]{1,0:T(8,128)(2,1)} %refs_3_.3, bf16[512,5120]{1,0:T(8,128)(2,1)} %refs_3_.3, bf16[512,5120]{1,0:T(8,128)(2,1)} %refs_3_.3, bf16[512,1280]{1,0:T(8,128)(2,1)} %copy-done.1, ...), custom_call_target="tpu_custom_call" | custom-call | flops 2684354560 | bytes 9961472 | tf_op jit(solution)/shard_map/query_product/pallas_call | solution.py:160
  151.7 1.6 convolution_convert_fusion
  153.9 14.1 %collective-permute-done.2.received = f32[1024,384]{1,0:T(8,128)S(1)} collective-permute-done((f32[1024,384]{1,0:T(8,128)}, f32[1024,384]{1,0:T(8,128)S(1)}, u32[]{:S(2)}, u32[]{:S(2)}) %collective-permute-start.2) | collective-permute-done | bytes 1572896 | tf_op jit(solution)/shard_map/ppermute | solution.py:85
  169.2 5.7 %attend.2.refs_0_ = bf16[1024,384]{1,0:T(8,128)(2,1)} custom-call(f32[1024,384]{1,0:T(8,128)} %get-tuple-element.15.kept, f32[1024,384]{1,0:T(8,128)} %copy-done.9, bf16[64,384]{1,0:T(8,128)(2,1)} %slice.48.keys, bf16[64,384]{1,0:T(8,128)(2,1)} %slice.49.values, s32[1024,1]{1,0:T(8,128)} %bitcast.26), custom_call_target="tpu_custom_call" | custom-call | flops 100663296 | bytes 3932160 | tf_op jit(solution)/shard_map/attend/pallas_call | solution.py:260
  179.0 10.2 %collective-permute-done.13.received = f32[1024,256]{1,0:T(8,128)} collective-permute-done((f32[1024,256]{1,0:T(8,128)}, f32[1024,256]{1,0:T(8,128)}, u32[]{:S(2)}, u32[]{:S(2)}) %collective-permute-start.13) | collective-permute-done | bytes 1048608 | tf_op jit(solution)/shard_map/ppermute | solution.py:85
  189.3 5.3 %attend.3.refs_4_ = bf16[1024,256]{1,0:T(8,128)(2,1)} custom-call(f32[1024,256]{1,0:T(8,128)} %get-tuple-element.17.kept, f32[1024,256]{1,0:T(8,128)} %collective-permute-done.13.received, bf16[64,256]{1,0:T(8,128)(2,1)} %slice.52.keys, bf16[64,256]{1,0:T(8,128)(2,1)} %slice.53.values, s32[1024,1]{1,0:T(8,128)} %bitcast.27), custom_call_target="tpu_custom_call" | custom-call | flops 67108864 | bytes 2621440 | tf_op jit(solution)/shard_map/attend/pallas_call | solution.py:260
  194.6 1.5 collective-permute-start.14
  198.4 9.1 %collective-permute-done.14.refs_6_ = bf16[1024,256]{1,0:T(8,128)(2,1)S(1)} collective-permute-done((bf16[1024,256]{1,0:T(8,128)(2,1)}, bf16[1024,256]{1,0:T(8,128)(2,1)S(1)}, u32[]{:S(2)}, u32[]{:S(2)}) %collective-permute-start.14) | collective-permute-done | bytes 524320 | tf_op jit(solution)/shard_map/ppermute | solution.py:85
  208.6 1.7 slice.46
  211.6 5.1 %all-gather.11.cloned.1.call-done = bf16[2560,1024]{1,0:T(8,128)(2,1)} async-done(((bf16[640,1024]{1,0:T(8,128)(2,1)}), bf16[2560,1024]{1,0:T(8,128)(2,1)}) %all-gather.11.cloned.1.call-update) | async-done | bytes 5242896 | tf_op jit(solution)/shard_map/all_gather | solution.py:89
  217.9 13.6 %out_product.3 = (f32[512,1024]{1,0:T(8,128)}, s16[528,1024]{1,0:T(8,128)(2,1)}) custom-call(s32[4]{0:T(128)} %iota_xor_fusion.1.place, bf16[1024,384]{1,0:T(8,128)(2,1)} %attend.2.refs_0_, bf16[2048,384]{1,0:T(8,128)(2,1)} %copy-done.3, bf16[1024,384]{1,0:T(8,128)(2,1)} %copy-done.6, bf16[2048,384]{1,0:T(8,128)(2,1)} %copy-done.3, ...), custom_call_target="tpu_custom_call" | custom-call | flops 5368709120 | bytes 14680064 | tf_op jit(solution)/shard_map/out_product/pallas_call | solution.py:207
  231.5 1.5 collective-permute-start.17
  233.0 16.5 %all-gather.9.cloned.1.call-done = bf16[2560,256]{1,0:T(8,128)(2,1)} async-done(((bf16[640,256]{1,0:T(8,128)(2,1)}), bf16[2560,256]{1,0:T(8,128)(2,1)}) %all-gather.9.cloned.1.call-update) | async-done | bytes 1310736 | tf_op jit(solution)/shard_map/all_gather | solution.py:89
  249.5 6.4 %out_product.2 = (f32[512,256]{1,0:T(8,128)}, s16[528,256]{1,0:T(8,128)(2,1)}) custom-call(s32[4]{0:T(128)} %iota_xor_fusion.1.place, bf16[1024,384]{1,0:T(8,128)(2,1)} %attend.2.refs_0_, bf16[2048,384]{1,0:T(8,128)(2,1)} %copy-done.3, bf16[1024,384]{1,0:T(8,128)(2,1)} %copy-done.6, bf16[2048,384]{1,0:T(8,128)(2,1)} %copy-done.3, ...), custom_call_target="tpu_custom_call" | custom-call | flops 1342177280 | bytes 7602176 | tf_op jit(solution)/shard_map/out_product/pallas_call | solution.py:207
  255.9 1.5 collective-permute-start.16
  258.5 2.9 %finish.2.refs_0_ = bf16[512,1280]{1,0:T(8,128)(2,1)} custom-call(f32[512,1024]{1,0:T(8,128)} %get-tuple-element.21.kept, s16[528,1024]{1,0:T(8,128)(2,1)} %copy-done.5, s16[528,1024]{1,0:T(8,128)(2,1)} %copy-done.5), custom_call_target="tpu_custom_call" | custom-call | flops 1048576 | bytes 4194304 | tf_op jit(solution)/shard_map/finish/pallas_call | solution.py:292
  261.4 2.3 collective-permute-done.16.received.scales
  264.4 2.0 finish.3
  (100 shorter events, 33.6 us)
Async XLA Ops:
  6.5 143.3 %copy-start = (bf16[768,1280]{1,0:T(8,128)(2,1)S(1)}, bf16[768,1280]{1,0:T(8,128)(2,1)}, u32[]{:S(2)}) copy-start(bf16[768,1280]{1,0:T(8,128)(2,1)} %param.13) | copy-start | bytes 5898244
  6.5 111.8 %all-gather.7.cloned.1.call-start = ((), (), s32[]{:S(2)}) async-start(), calls=%async_computation | async-start | bytes 4915200 | tf_op jit(solution)/shard_map/all_gather | solution.py:89
  9.1 207.6 %all-gather.11.cloned.1.call-start = ((), (), s32[]{:S(2)}) async-start(), calls=%async_computation.2 | async-start | bytes 6553600 | tf_op jit(solution)/shard_map/all_gather | solution.py:89
  11.6 237.9 %all-gather.9.cloned.1.call-start = ((), (), s32[]{:S(2)}) async-start(), calls=%async_computation.1 | async-start | bytes 1638400 | tf_op jit(solution)/shard_map/all_gather | solution.py:89
  15.4 12.3 %copy-start.17 = (s32[2,512]{1,0:T(2,128)S(1)}, s32[2,512]{1,0:T(2,128)}, u32[]{:S(2)}) copy-start(s32[2,512]{1,0:T(2,128)} %param.15) | copy-start | bytes 12292
  15.4 12.8 %copy-start.19 = (s32[2]{0:T(128)S(1)}, s32[2]{0:T(128)}, u32[]{:S(2)}) copy-start(s32[2]{0:T(128)} %constant.56) | copy-start | bytes 28
  16.6 32.2 %collective-permute-start = (bf16[512,1280]{1,0:T(8,128)(2,1)}, bf16[512,1280]{1,0:T(8,128)(2,1)S(1)}, u32[]{:S(2)}, u32[]{:S(2)}) collective-permute-start(bf16[512,1280]{1,0:T(8,128)(2,1)} %pad_maximum_fusion.2), channel_id=1, source_target_pairs={{0,4},{1,5},{2,6},{3,7},{4,0},{5,1},{6,2},{7,3},{8,12},{9,13},{10,... | collective-permute-start | bytes 3932168 | tf_op jit(solution)/shard_map/ppermute | solution.py:85
  19.5 44.7 %collective-permute-start.8 = (bf16[640,512]{1,0:T(8,128)(2,1)}, bf16[640,512]{1,0:T(8,128)(2,1)}, u32[]{:S(2)}, u32[]{:S(2)}) collective-permute-start(bf16[640,512]{1,0:T(8,128)(2,1)} %get-tuple-element.32), channel_id=1, source_target_pairs={{0,8},{1,9},{2,10},{3,11},{4,12},{5,13},{6,14},{7,15},{8,0},{9,1},... | collective-permute-start | bytes 1966088 | tf_op jit(solution)/shard_map/ppermute | solution.py:85
  21.1 50.3 %collective-permute-start.10 = (bf16[640,512]{1,0:T(8,128)(2,1)}, bf16[640,512]{1,0:T(8,128)(2,1)}, u32[]{:S(2)}, u32[]{:S(2)}) collective-permute-start(bf16[640,512]{1,0:T(8,128)(2,1)} %get-tuple-element.32), channel_id=1, source_target_pairs={{0,0},{1,1},{2,2},{3,3},{4,4},{5,5},{6,6},{7,7},{8,16},{9,17},{10,... | collective-permute-start | bytes 1966088 | tf_op jit(solution)/shard_map/ppermute | solution.py:85
  28.3 102.1 %copy-start.11 = (bf16[1,6656]{1,0:T(2,128)(2,1)}, bf16[1,6656]{1,0:T(2,128)(2,1)S(1)}, u32[]{:S(2)}) copy-start(bf16[1,6656]{1,0:T(2,128)(2,1)S(1)} %broadcast_in_dim.2) | copy-start | bytes 39940
  28.3 20.8 %collective-permute-start.3 = (bf16[1,6656]{1,0:T(2,128)(2,1)S(1)}, bf16[1,6656]{1,0:T(2,128)(2,1)S(1)}, u32[]{:S(2)}, u32[]{:S(2)}) collective-permute-start(bf16[1,6656]{1,0:T(2,128)(2,1)S(1)} %broadcast_in_dim.2), channel_id=1, source_target_pairs={{0,4},{1,5},{2,6},{3,7},{4,0},{5,1},{6,2},{7,3},{8,12},{9,13},{10,... | collective-permute-start | bytes 39944 | tf_op jit(solution)/shard_map/ppermute | solution.py:85
  48.8 69.6 %copy-start.1 = (bf16[512,1280]{1,0:T(8,128)(2,1)}, bf16[512,1280]{1,0:T(8,128)(2,1)S(1)}, u32[]{:S(2)}) copy-start(bf16[512,1280]{1,0:T(8,128)(2,1)S(1)} %collective-permute-done.refs_4_.refs_5_) | copy-start | bytes 3932164
  48.8 25.4 %collective-permute-start.1 = (bf16[512,1280]{1,0:T(8,128)(2,1)S(1)}, bf16[512,1280]{1,0:T(8,128)(2,1)}, u32[]{:S(2)}, u32[]{:S(2)}) collective-permute-start(bf16[512,1280]{1,0:T(8,128)(2,1)S(1)} %collective-permute-done.refs_4_.refs_5_), channel_id=1, source_target_pairs={{0,1},{1,0},{2,3},{3,2},{4,5},{5,4},{6,7},{7,6},{8,9},{9,8},{10,11... | collective-permute-start | bytes 3932168 | tf_op jit(solution)/shard_map/ppermute | solution.py:85
  49.1 81.4 %copy-start.12 = (bf16[1,6656]{1,0:T(2,128)(2,1)}, bf16[1,6656]{1,0:T(2,128)(2,1)S(1)}, u32[]{:S(2)}) copy-start(bf16[1,6656]{1,0:T(2,128)(2,1)S(1)} %collective-permute-done.3) | copy-start | bytes 39940
  49.1 21.6 %collective-permute-start.4 = (bf16[2,6656]{1,0:T(2,128)(2,1)S(1)}, bf16[2,6656]{1,0:T(2,128)(2,1)S(1)}, u32[]{:S(2)}, u32[]{:S(2)}) collective-permute-start(bf16[2,6656]{1,0:T(2,128)(2,1)S(1)} %pad_maximum_fusion.11), channel_id=1, source_target_pairs={{0,8},{1,9},{2,10},{3,11},{4,12},{5,13},{6,14},{7,15},{8,0},{9,1},... | collective-permute-start | bytes 79880 | tf_op jit(solution)/shard_map/ppermute | solution.py:85
  64.2 8.5 %collective-permute-start.9 = (bf16[640,512]{1,0:T(8,128)(2,1)}, bf16[640,512]{1,0:T(8,128)(2,1)}, u32[]{:S(2)}, u32[]{:S(2)}) collective-permute-start(bf16[640,512]{1,0:T(8,128)(2,1)} %collective-permute-done.8), channel_id=1, source_target_pairs={{0,0},{1,1},{2,2},{3,3},{4,4},{5,5},{6,6},{7,7},{8,16},{9,17},{10,... | collective-permute-start | bytes 1966088 | tf_op jit(solution)/shard_map/ppermute | solution.py:85
  70.7 59.7 %copy-start.15 = (bf16[2,6656]{1,0:T(2,128)(2,1)}, bf16[2,6656]{1,0:T(2,128)(2,1)S(1)}, u32[]{:S(2)}) copy-start(bf16[2,6656]{1,0:T(2,128)(2,1)S(1)} %collective-permute-done.4) | copy-start | bytes 79876
  71.4 60.5 %collective-permute-start.5 = (bf16[4,6656]{1,0:T(4,128)(2,1)}, bf16[4,6656]{1,0:T(4,128)(2,1)}, u32[]{:S(2)}, u32[]{:S(2)}) collective-permute-start(bf16[4,6656]{1,0:T(4,128)(2,1)} %pad_maximum_fusion.9), channel_id=1, source_target_pairs={{0,16},{1,17},{2,18},{3,19},{4,20},{5,21},{6,22},{7,23},{8,24},{9,... | collective-permute-start | bytes 159752 | tf_op jit(solution)/shard_map/ppermute | solution.py:85
  71.4 63.7 %collective-permute-start.11 = (bf16[640,512]{1,0:T(8,128)(2,1)}, bf16[640,512]{1,0:T(8,128)(2,1)}, u32[]{:S(2)}, u32[]{:S(2)}) collective-permute-start(bf16[640,512]{1,0:T(8,128)(2,1)} %collective-permute-done.10), channel_id=1, source_target_pairs={{8,0},{9,1},{10,2},{11,3},{12,4},{13,5},{14,6},{15,7},{16,24},{17,... | collective-permute-start | bytes 1966088 | tf_op jit(solution)/shard_map/ppermute | solution.py:85
  72.7 63.6 %collective-permute-start.12 = (bf16[640,512]{1,0:T(8,128)(2,1)}, bf16[640,512]{1,0:T(8,128)(2,1)}, u32[]{:S(2)}, u32[]{:S(2)}) collective-permute-start(bf16[640,512]{1,0:T(8,128)(2,1)} %collective-permute-done.9), channel_id=1, source_target_pairs={{8,0},{9,1},{10,2},{11,3},{12,4},{13,5},{14,6},{15,7},{16,24},{17,... | collective-permute-start | bytes 1966088 | tf_op jit(solution)/shard_map/ppermute | solution.py:85
  130.4 37.6 %collective-permute-start.2 = (f32[1024,384]{1,0:T(8,128)}, f32[1024,384]{1,0:T(8,128)S(1)}, u32[]{:S(2)}, u32[]{:S(2)}) collective-permute-start(f32[1024,384]{1,0:T(8,128)} %get-tuple-element.16), channel_id=1, source_target_pairs={{0,4},{1,5},{2,6},{3,7},{4,0},{5,1},{6,2},{7,3},{8,12},{9,13},{10,... | collective-permute-start | bytes 4718600 | tf_op jit(solution)/shard_map/ppermute | solution.py:85
  149.2 40.1 %collective-permute-start.13 = (f32[1024,256]{1,0:T(8,128)}, f32[1024,256]{1,0:T(8,128)}, u32[]{:S(2)}, u32[]{:S(2)}) collective-permute-start(f32[1024,256]{1,0:T(8,128)} %get-tuple-element.18), channel_id=1, source_target_pairs={{0,4},{1,5},{2,6},{3,7},{4,0},{5,1},{6,2},{7,3},{8,12},{9,13},{10,... | collective-permute-start | bytes 3145736 | tf_op jit(solution)/shard_map/ppermute | solution.py:85
  151.0 17.0 %copy-start.13 = (bf16[64,640]{1,0:T(8,128)(2,1)}, bf16[64,640]{1,0:T(8,128)(2,1)S(1)}, u32[]{:S(2)}) copy-start(bf16[64,640]{1,0:T(8,128)(2,1)S(1)} %convolution_convert_fusion.1) | copy-start | bytes 245764
  153.2 14.8 %copy-start.14 = (bf16[64,640]{1,0:T(8,128)(2,1)}, bf16[64,640]{1,0:T(8,128)(2,1)S(1)}, u32[]{:S(2)}) copy-start(bf16[64,640]{1,0:T(8,128)(2,1)S(1)} %convolution_convert_fusion) | copy-start | bytes 245764
  174.9 22.1 %copy-start.2 = (bf16[1024,384]{1,0:T(8,128)(2,1)S(1)}, bf16[1024,384]{1,0:T(8,128)(2,1)}, u32[]{:S(2)}) copy-start(bf16[1024,384]{1,0:T(8,128)(2,1)} %attend.2.refs_0_) | copy-start | bytes 2359300
  174.9 21.2 %collective-permute-start.6 = (bf16[1024,384]{1,0:T(8,128)(2,1)}, bf16[1024,384]{1,0:T(8,128)(2,1)S(1)}, u32[]{:S(2)}, u32[]{:S(2)}) collective-permute-start(bf16[1024,384]{1,0:T(8,128)(2,1)} %attend.2.refs_0_), channel_id=1, source_target_pairs={{0,2},{1,3},{2,0},{3,1},{4,6},{5,7},{6,4},{7,5},{8,10},{9,11},{10,... | collective-permute-start | bytes 2359304 | tf_op jit(solution)/shard_map/ppermute | solution.py:85
  194.6 12.9 %copy-start.4 = (bf16[1024,256]{1,0:T(8,128)(2,1)S(1)}, bf16[1024,256]{1,0:T(8,128)(2,1)}, u32[]{:S(2)}) copy-start(bf16[1024,256]{1,0:T(8,128)(2,1)} %attend.3.refs_4_) | copy-start | bytes 1572868
  194.6 12.8 %collective-permute-start.14 = (bf16[1024,256]{1,0:T(8,128)(2,1)}, bf16[1024,256]{1,0:T(8,128)(2,1)S(1)}, u32[]{:S(2)}, u32[]{:S(2)}) collective-permute-start(bf16[1024,256]{1,0:T(8,128)(2,1)} %attend.3.refs_4_), channel_id=1, source_target_pairs={{0,2},{1,3},{2,0},{3,1},{4,6},{5,7},{6,4},{7,5},{8,10},{9,11},{10,... | collective-permute-start | bytes 1572872 | tf_op jit(solution)/shard_map/ppermute | solution.py:85
  198.4 18.3 %collective-permute-start.7 = (bf16[2048,384]{1,0:T(8,128)(2,1)}, bf16[2048,384]{1,0:T(8,128)(2,1)S(1)}, u32[]{:S(2)}, u32[]{:S(2)}) collective-permute-start(bf16[2048,384]{1,0:T(8,128)(2,1)} %pad_maximum_fusion.1), channel_id=1, source_target_pairs={{0,1},{1,0},{2,3},{3,2},{4,5},{5,4},{6,7},{7,6},{8,9},{9,8},{10,11... | collective-permute-start | bytes 4718600 | tf_op jit(solution)/shard_map/ppermute | solution.py:85
  208.6 3.0 %collective-permute-start.15 = (bf16[2048,256]{1,0:T(8,128)(2,1)}, bf16[2048,256]{1,0:T(8,128)(2,1)}, u32[]{:S(2)}, u32[]{:S(2)}) collective-permute-start(bf16[2048,256]{1,0:T(8,128)(2,1)} %pad_maximum_fusion.3), channel_id=1, source_target_pairs={{0,1},{1,0},{2,3},{3,2},{4,5},{5,4},{6,7},{7,6},{8,9},{9,8},{10,11... | collective-permute-start | bytes 3145736 | tf_op jit(solution)/shard_map/ppermute | solution.py:85
  231.5 26.0 %collective-permute-start.17 = (s16[528,1024]{1,0:T(8,128)(2,1)}, s16[528,1024]{1,0:T(8,128)(2,1)S(1)}, u32[]{:S(2)}, u32[]{:S(2)}) collective-permute-start(s16[528,1024]{1,0:T(8,128)(2,1)} %get-tuple-element.22), channel_id=1, source_target_pairs={{0,4},{1,5},{2,6},{3,7},{4,0},{5,1},{6,2},{7,3},{8,12},{9,13},{10,... | collective-permute-start | bytes 3244040 | tf_op jit(solution)/shard_map/ppermute | solution.py:85
  255.9 7.8 %collective-permute-start.16 = (s16[528,256]{1,0:T(8,128)(2,1)}, s16[528,256]{1,0:T(8,128)(2,1)S(1)}, u32[]{:S(2)}, u32[]{:S(2)}) collective-permute-start(s16[528,256]{1,0:T(8,128)(2,1)} %get-tuple-element.20), channel_id=1, source_target_pairs={{0,4},{1,5},{2,6},{3,7},{4,0},{5,1},{6,2},{7,3},{8,12},{9,13},{10,... | collective-permute-start | bytes 811016 | tf_op jit(solution)/shard_map/ppermute | solution.py:85
  (9 other events, 33.1 us)
Sparse Core Ops, SparseCore 0:
  9.2 109.1 all-gather.6
  119.9 96.6 all-gather.10
  218.2 31.2 all-gather.8
